TPU v7x, 32 devices: a whole 2x2x4 slice. The times are simulated.
32 devices in a mesh: dp: 8 (over z, y), seq: 4 (over x, core).
Axes of the slice: x: 2, y: 2, z: 4, core: 2. Of those that a mesh axis runs over, the one named last changes fastest.
Arguments:
- content: float32 [8, 2048, 768], P('dp', 'seq'), may hold values from -6 to 6
- query_stream: float32 [8, 304, 768], P('dp', 'seq'), may hold values from -6 to 6
- segment_ids: int32 [8, 2048], P('dp', 'seq'), may hold values from 0 to 2047, as said below
- pad_mask: int32 [8, 2048], P('dp', 'seq'), may hold values from 0 to 1, as said below
- predicted: int32 [8, 304], P('dp', 'seq'), may hold values from 0 to 2046, as said below
- order: int32 [8, 2048], P('dp', 'seq'), may hold values from 0 to 2047, as said below
- rel_bucket: int32 [4095], replicated, may hold values from 0 to 31, as said below
- qkv_weight: bfloat16 [768, 2304], P(('dp', 'seq')), may hold values from -0.21875 to 0.21875
- qv_bias: bfloat16 [1536], P(('dp', 'seq')), may hold values from -3 to 3
- out_weight: bfloat16 [768, 768], P(('dp', 'seq')), may hold values from -0.875 to 0.875
- out_bias: bfloat16 [768], P(('dp', 'seq')), may hold values from -3 to 3
- attn_gain: bfloat16 [768], P(('dp', 'seq')), may hold values from 0.099609375 to 1.8984375
- attn_shift: bfloat16 [768], P(('dp', 'seq')), may hold values from -3 to 3
- up_weight: bfloat16 [768, 3072], P(('dp', 'seq')), may hold values from -0.21875 to 0.21875
- up_bias: bfloat16 [3072], P(('dp', 'seq')), may hold values from -3 to 3
- down_weight: bfloat16 [3072, 768], P(('dp', 'seq')), may hold values from -0.109375 to 0.109375
- down_bias: bfloat16 [768], P(('dp', 'seq')), may hold values from -3 to 3
- ffn_gain: bfloat16 [768], P(('dp', 'seq')), may hold values from 0.099609375 to 1.8984375
- ffn_shift: bfloat16 [768], P(('dp', 'seq')), may hold values from -3 to 3
- rel_table: bfloat16 [32, 12], replicated, may hold values from -4 to 4
- content_cot: float32 [8, 2048, 768], P('dp', 'seq'), may hold values from -6 to 6
- query_cot: float32 [8, 304, 768], P('dp', 'seq'), may hold values from -6 to 6
Outputs:
- content_out: float32 [8, 2048, 768], P('dp', 'seq')
- query_out: float32 [8, 304, 768], P('dp', 'seq')
- content_grad: float32 [8, 2048, 768], P('dp', 'seq')
- query_grad: float32 [8, 304, 768], P('dp', 'seq')
- qkv_weight_grad: float32 [768, 2304], P(('dp', 'seq'))
- qv_bias_grad: float32 [1536], P(('dp', 'seq'))
- out_weight_grad: float32 [768, 768], P(('dp', 'seq'))
- out_bias_grad: float32 [768], P(('dp', 'seq'))
- attn_gain_grad: float32 [768], P(('dp', 'seq'))
- attn_shift_grad: float32 [768], P(('dp', 'seq'))
- up_weight_grad: float32 [768, 3072], P(('dp', 'seq'))
- up_bias_grad: float32 [3072], P(('dp', 'seq'))
- down_weight_grad: float32 [3072, 768], P(('dp', 'seq'))
- down_bias_grad: float32 [768], P(('dp', 'seq'))
- ffn_gain_grad: float32 [768], P(('dp', 'seq'))
- ffn_shift_grad: float32 [768], P(('dp', 'seq'))
- rel_table_grad: float32 [32, 12], replicated
- stats: float32 [6], replicated
Inputs may be any that keep to these rules, and one draw needn't show every extreme that they name: `segment_ids`: each slot's id is the position of the last slot of its document, and for the document holding slot 2047 it is 2047; along each sequence the ids never fall; every document but that last one has 60 to 800 tokens, and in each sequence one has exactly 800. `pad_mask`: in each sequence the padding slots are exactly those of the last document. `predicted`: 304 distinct real token positions of the sequence, none the first of its document, listed in the permuted order. `order`: A permutation of 0 to 2047 in each sequence: unpredicted real tokens take the lowest ranks, then predicted[i] has rank (number of unpredicted real tokens) + i, padding the highest. `rel_bucket`: entry j - i + 2047 is the bucket of key position j seen from position i: 0 at distance 0, below 16 for keys before, at least 16 for keys after, never falling as the distance grows on either side.
All inputs are finite; a program needn't handle non-finite values.
Results may differ from a plain program's by a relative error of at most 0.014.
Values may be sent and summed in bfloat16 or wider, within the bound.
A program may use at most 320 MiB of HBM per device.

v0:
```python
import jax
import jax.numpy as jnp
from jax import lax
from jax.sharding import PartitionSpec as P

MODEL_WIDTH = 768
HEADS = 12
HEAD_DIM = 64
BUCKETS = 32
SEQ_LEN = 2048


EPS = 1e-05
NEG = -1000000000.0
SCALE = 0.125


def exact_gelu(values):
    return jax.nn.gelu(values, approximate=False)


def norm_fwd(residual, gain_vec, shift_vec):
    row_mean = jnp.mean(residual, axis=-1, keepdims=True)
    centered = residual - row_mean
    inv_std = lax.rsqrt(jnp.mean(centered * centered, axis=-1, keepdims=True) + EPS)
    normed = centered * inv_std
    return (normed * gain_vec + shift_vec, normed, inv_std)


def norm_back(upstream, normed, inv_std, gain_vec):
    grad_norm = upstream * gain_vec
    projected = jnp.mean(grad_norm, axis=-1, keepdims=True) + normed * jnp.mean(
        grad_norm * normed, axis=-1, keepdims=True
    )
    return (
        inv_std * (grad_norm - projected),
        jnp.sum(upstream * normed, axis=(0, 1)),
        jnp.sum(upstream, axis=(0, 1)),
    )


def bucket_edges(rel_bucket):
    entry_count = rel_bucket.shape[0]
    matches = rel_bucket[None, :] == jnp.arange(BUCKETS, dtype=jnp.int32)[:, None]
    places = jnp.arange(entry_count, dtype=jnp.int32)[None, :]
    starts = jnp.min(jnp.where(matches, places, entry_count), axis=1)
    counts = jnp.sum(matches.astype(jnp.int32), axis=1)
    return (starts, starts + counts)


def build_mask(
    query_pos, query_seg, query_limit, content_row, key_pos, key_seg, key_order, key_pad
):
    inside = (
        (query_seg[:, None] == key_seg[None, :])
        & (key_pad[None, :] == 1)
        & (key_order[None, :] <= query_limit[:, None])
    )
    itself = (key_pos[None, :] == query_pos[:, None]) & content_row[:, None]
    return (inside | itself, key_pos[None, :] - query_pos[:, None] + (SEQ_LEN - 1))


def masked_scores(query_heads, key_heads, table_low, edges, allowed, offsets):
    raw_scores = (
        jnp.einsum("rhd,lhd->hrl", query_heads, key_heads, preferred_element_type=jnp.float32)
        * SCALE
    )
    starts, ends = edges
    spread = offsets[..., None]
    onehot = ((spread >= starts) & (spread < ends)).astype(jnp.bfloat16)
    bias = jnp.einsum("rlb,bh->hrl", onehot, table_low, preferred_element_type=jnp.float32)
    return (jnp.where(allowed[None], raw_scores + bias, NEG), onehot)


def attend_forward(packed, table_low, edges, content_row):
    queries, key_values, key_seg, key_order, key_pad, query_pos, query_seg, query_limit = packed
    row_count = queries.shape[0]
    length = key_values.shape[0]
    key_pos = jnp.arange(length, dtype=jnp.int32)
    allowed, offsets = build_mask(
        query_pos, query_seg, query_limit, content_row, key_pos, key_seg, key_order, key_pad
    )
    query_heads = queries.reshape(row_count, HEADS, HEAD_DIM)
    key_heads = key_values[:, :MODEL_WIDTH].reshape(length, HEADS, HEAD_DIM)
    value_heads = key_values[:, MODEL_WIDTH:].reshape(length, HEADS, HEAD_DIM)
    scores, onehot = masked_scores(query_heads, key_heads, table_low, edges, allowed, offsets)
    row_max = jnp.max(scores, axis=-1, keepdims=True)
    expo_vals = jnp.exp(scores - row_max)
    row_total = jnp.sum(expo_vals, axis=-1, keepdims=True)
    probs_low = (expo_vals / row_total).astype(jnp.bfloat16)
    context = jnp.einsum("hrl,lhd->rhd", probs_low, value_heads, preferred_element_type=jnp.float32)
    return (
        context.reshape(row_count, MODEL_WIDTH),
        jnp.transpose((row_max + jnp.log(row_total))[..., 0]),
    )


def attend_backward(packed, table_low, edges, content_row):
    (
        queries,
        key_values,
        key_seg,
        key_order,
        key_pad,
        query_pos,
        query_seg,
        query_limit,
        row_lse,
        grad_context,
    ) = packed
    row_count = queries.shape[0]
    length = key_values.shape[0]
    key_pos = jnp.arange(length, dtype=jnp.int32)
    allowed, offsets = build_mask(
        query_pos, query_seg, query_limit, content_row, key_pos, key_seg, key_order, key_pad
    )
    query_heads = queries.reshape(row_count, HEADS, HEAD_DIM)
    key_heads = key_values[:, :MODEL_WIDTH].reshape(length, HEADS, HEAD_DIM)
    value_heads = key_values[:, MODEL_WIDTH:].reshape(length, HEADS, HEAD_DIM)
    scores, onehot = masked_scores(query_heads, key_heads, table_low, edges, allowed, offsets)
    probs = jnp.exp(scores - jnp.transpose(row_lse)[..., None])
    grad_heads = grad_context.reshape(row_count, HEADS, HEAD_DIM)
    grad_probs = jnp.einsum(
        "rhd,lhd->hrl", grad_heads, value_heads, preferred_element_type=jnp.float32
    )
    row_delta = jnp.sum(probs * grad_probs, axis=-1)
    grad_scores = (probs * (grad_probs - row_delta[..., None])).astype(jnp.bfloat16)
    grad_query = (
        jnp.einsum("hrl,lhd->rhd", grad_scores, key_heads, preferred_element_type=jnp.float32)
        * SCALE
    )
    grad_table = jnp.einsum("hrl,rlb->bh", grad_scores, onehot, preferred_element_type=jnp.float32)
    results = (grad_query.reshape(row_count, MODEL_WIDTH), grad_table, jnp.transpose(row_delta))
    probs_low = probs.astype(jnp.bfloat16)
    grad_key = (
        jnp.einsum("hrl,rhd->lhd", grad_scores, query_heads, preferred_element_type=jnp.float32)
        * SCALE
    )
    grad_value = jnp.einsum(
        "hrl,rhd->lhd", probs_low, grad_heads, preferred_element_type=jnp.float32
    )
    results = results + (
        jnp.concatenate(
            [grad_key.reshape(length, MODEL_WIDTH), grad_value.reshape(length, MODEL_WIDTH)],
            axis=-1,
        ),
    )
    return results


def local(
    content,
    query_stream,
    segment_ids,
    pad_mask,
    predicted,
    order,
    rel_bucket,
    qkv_weight,
    qv_bias,
    out_weight,
    out_bias,
    attn_gain,
    attn_shift,
    up_weight,
    up_bias,
    down_weight,
    down_bias,
    ffn_gain,
    ffn_shift,
    rel_table,
    content_cot,
    query_cot,
):
    seq_count = content.shape[0]
    shard_length = content.shape[1]
    pred_count = query_stream.shape[1]
    row_count = shard_length + pred_count
    group_size = lax.axis_size("seq")
    edges = bucket_edges(rel_bucket)
    shards = (
        lax.all_gather(qkv_weight, ("dp", "seq"), axis=0, tiled=True),
        lax.all_gather(out_weight, ("dp", "seq"), axis=0, tiled=True),
        lax.all_gather(up_weight, ("dp", "seq"), axis=0, tiled=True),
        lax.all_gather(down_weight, ("dp", "seq"), axis=0, tiled=True),
        lax.all_gather(qv_bias, ("dp", "seq"), axis=0, tiled=True),
        lax.all_gather(out_bias, ("dp", "seq"), axis=0, tiled=True),
        lax.all_gather(attn_gain, ("dp", "seq"), axis=0, tiled=True),
        lax.all_gather(attn_shift, ("dp", "seq"), axis=0, tiled=True),
        lax.all_gather(up_bias, ("dp", "seq"), axis=0, tiled=True),
        lax.all_gather(down_bias, ("dp", "seq"), axis=0, tiled=True),
        lax.all_gather(ffn_gain, ("dp", "seq"), axis=0, tiled=True),
        lax.all_gather(ffn_shift, ("dp", "seq"), axis=0, tiled=True),
    )
    query_key_value_weight, w_out, w_up, w_down = (shards[0], shards[1], shards[2], shards[3])
    bias_qv, bias_out, first_norm_gain, shift_one, bias_up, bias_down, gain_two, shift_two = [
        member.astype(jnp.float32) for member in shards[4:]
    ]
    all_rows = jnp.concatenate([content, query_stream], axis=1)
    reduced_precision_rows = all_rows.astype(jnp.bfloat16)
    queries = (
        jnp.einsum(
            "srd,de->sre",
            reduced_precision_rows,
            query_key_value_weight[:, :MODEL_WIDTH],
            preferred_element_type=jnp.float32,
        )
        + bias_qv[:MODEL_WIDTH]
    ).astype(jnp.bfloat16)
    value_shift = jnp.concatenate([jnp.zeros((MODEL_WIDTH,), jnp.float32), bias_qv[MODEL_WIDTH:]])
    key_values = (
        jnp.einsum(
            "zci,ip->zcp",
            reduced_precision_rows[:, :shard_length],
            query_key_value_weight[:, MODEL_WIDTH:],
            preferred_element_type=jnp.float32,
        )
        + value_shift
    ).astype(jnp.bfloat16)
    full_pairs, full_seg, full_order, full_pad = (
        lax.all_gather(key_values, "seq", axis=1, tiled=True),
        lax.all_gather(segment_ids, "seq", axis=1, tiled=True),
        lax.all_gather(order, "seq", axis=1, tiled=True),
        lax.all_gather(pad_mask, "seq", axis=1, tiled=True),
    )
    content_pos = lax.axis_index("seq") * shard_length + jnp.arange(shard_length, dtype=jnp.int32)
    query_pos = jnp.concatenate(
        [jnp.broadcast_to(content_pos[None, :], (seq_count, shard_length)), predicted], axis=1
    )
    query_seg = jnp.concatenate(
        [segment_ids, jnp.take_along_axis(full_seg, predicted, axis=1)], axis=1
    )
    query_limit = jnp.concatenate(
        [order, jnp.take_along_axis(full_order, predicted, axis=1) - 1], axis=1
    )
    content_row = jnp.arange(row_count, dtype=jnp.int32) < shard_length
    row_meta = (full_seg, full_order, full_pad, query_pos, query_seg, query_limit)

    def forward_one(packed):
        return attend_forward(packed, rel_table, edges, content_row)

    context, row_lse = lax.map(forward_one, (queries, full_pairs) + row_meta)
    context_low = context.astype(jnp.bfloat16)
    attn_out = (
        jnp.einsum("sre,ed->srd", context_low, w_out, preferred_element_type=jnp.float32) + bias_out
    )
    hidden_one, normed_one, inv_one = norm_fwd(all_rows + attn_out, first_norm_gain, shift_one)
    hidden_low = hidden_one.astype(jnp.bfloat16)
    pre_act = (
        jnp.einsum("srd,df->srf", hidden_low, w_up, preferred_element_type=jnp.float32) + bias_up
    )
    activ, gelu_pull = jax.vjp(exact_gelu, pre_act)
    activ_low = activ.astype(jnp.bfloat16)
    ffn_out = (
        jnp.einsum("srf,fd->srd", activ_low, w_down, preferred_element_type=jnp.float32) + bias_down
    )
    hidden_two, normed_two, inv_two = norm_fwd(hidden_one + ffn_out, gain_two, shift_two)
    pad_float = pad_mask.astype(jnp.float32)
    row_valid = jnp.concatenate(
        [pad_float, jnp.ones((seq_count, pred_count), jnp.float32)], axis=1
    )[..., None]
    outputs = hidden_two * row_valid
    pad_weight = pad_float[..., None]
    local_sums = jnp.stack(
        [
            jnp.sum(pad_weight * content * content),
            jnp.sum(query_stream * query_stream),
            jnp.sum(pad_weight * attn_out[:, :shard_length] * attn_out[:, :shard_length]),
            jnp.sum(attn_out[:, shard_length:] * attn_out[:, shard_length:]),
            jnp.sum(pad_weight * ffn_out[:, :shard_length] * ffn_out[:, :shard_length]),
            jnp.sum(ffn_out[:, shard_length:] * ffn_out[:, shard_length:]),
            jnp.sum(pad_float),
        ]
    )
    back_weights = (
        lax.all_gather(qkv_weight, ("dp", "seq"), axis=0, tiled=True),
        lax.all_gather(out_weight, ("dp", "seq"), axis=0, tiled=True),
        lax.all_gather(up_weight, ("dp", "seq"), axis=0, tiled=True),
        lax.all_gather(down_weight, ("dp", "seq"), axis=0, tiled=True),
        lax.all_gather(attn_gain, ("dp", "seq"), axis=0, tiled=True),
        lax.all_gather(ffn_gain, ("dp", "seq"), axis=0, tiled=True),
    )
    back_pairs = lax.all_gather(key_values, "seq", axis=1, tiled=True)
    backward_query_key_value, back_out, back_up, back_down = (
        back_weights[0],
        back_weights[1],
        back_weights[2],
        back_weights[3],
    )
    back_gain_one = back_weights[4].astype(jnp.float32)
    back_gain_two = back_weights[5].astype(jnp.float32)
    upstream = jnp.concatenate([content_cot, query_cot], axis=1) * row_valid
    grad_res_two, grad_gain_two, grad_shift_two = norm_back(
        upstream, normed_two, inv_two, back_gain_two
    )
    grad_ffn = grad_res_two.astype(jnp.bfloat16)
    grad_bias_down = jnp.sum(grad_ffn, axis=(0, 1), dtype=jnp.float32)
    grad_down = jnp.einsum("srf,srd->fd", activ_low, grad_ffn, preferred_element_type=jnp.float32)
    grad_activ = jnp.einsum("srd,fd->srf", grad_ffn, back_down, preferred_element_type=jnp.float32)
    grad_pre = gelu_pull(grad_activ)[0].astype(jnp.bfloat16)
    grad_bias_up = jnp.sum(grad_pre, axis=(0, 1), dtype=jnp.float32)
    grad_up = jnp.einsum("srd,srf->df", hidden_low, grad_pre, preferred_element_type=jnp.float32)
    grad_hidden = grad_res_two + jnp.einsum(
        "srf,df->srd", grad_pre, back_up, preferred_element_type=jnp.float32
    )
    grad_res_one, grad_gain_one, grad_shift_one = norm_back(
        grad_hidden, normed_one, inv_one, back_gain_one
    )
    grad_attn = grad_res_one.astype(jnp.bfloat16)
    grad_bias_out = jnp.sum(grad_attn, axis=(0, 1), dtype=jnp.float32)
    grad_out = jnp.einsum("sre,srd->ed", context_low, grad_attn, preferred_element_type=jnp.float32)
    grad_context = jnp.einsum(
        "srd,ed->sre", grad_attn, back_out, preferred_element_type=jnp.float32
    ).astype(jnp.bfloat16)

    def backward_all(packed):
        return attend_backward(packed, rel_table, edges, content_row)

    grad_queries, grad_tables, per_row_delta, grad_pairs = lax.map(
        backward_all, (queries, back_pairs) + row_meta + (row_lse, grad_context)
    )
    paired_gradients = lax.psum_scatter(
        grad_pairs.astype(jnp.bfloat16), "seq", scatter_dimension=1, tiled=True
    )
    query_grads = grad_queries.astype(jnp.bfloat16)
    grad_bias_qv = jnp.concatenate(
        [
            jnp.sum(query_grads, axis=(0, 1), dtype=jnp.float32),
            jnp.sum(paired_gradients[..., MODEL_WIDTH:], axis=(0, 1), dtype=jnp.float32),
        ]
    )
    grad_qkv = jnp.concatenate(
        [
            jnp.einsum(
                "srd,sre->de",
                reduced_precision_rows,
                query_grads,
                preferred_element_type=jnp.float32,
            ),
            jnp.einsum(
                "cvi,cvp->ip",
                reduced_precision_rows[:, :shard_length],
                paired_gradients,
                preferred_element_type=jnp.float32,
            ),
        ],
        axis=1,
    )
    grad_rows = grad_res_one + jnp.einsum(
        "sre,de->srd",
        query_grads,
        backward_query_key_value[:, :MODEL_WIDTH],
        preferred_element_type=jnp.float32,
    )
    grad_content = grad_rows[:, :shard_length] + jnp.einsum(
        "zwv,bv->zwb",
        paired_gradients,
        backward_query_key_value[:, MODEL_WIDTH:],
        preferred_element_type=jnp.float32,
    )
    grad_query = grad_rows[:, shard_length:]
    owned = (
        lax.psum_scatter(grad_qkv, ("dp", "seq"), scatter_dimension=0, tiled=True),
        lax.psum_scatter(grad_out, ("dp", "seq"), scatter_dimension=0, tiled=True),
        lax.psum_scatter(grad_up, ("dp", "seq"), scatter_dimension=0, tiled=True),
        lax.psum_scatter(grad_down, ("dp", "seq"), scatter_dimension=0, tiled=True),
        lax.psum_scatter(grad_bias_qv, ("dp", "seq"), scatter_dimension=0, tiled=True),
        lax.psum_scatter(grad_bias_out, ("dp", "seq"), scatter_dimension=0, tiled=True),
        lax.psum_scatter(grad_gain_one, ("dp", "seq"), scatter_dimension=0, tiled=True),
        lax.psum_scatter(grad_shift_one, ("dp", "seq"), scatter_dimension=0, tiled=True),
        lax.psum_scatter(grad_bias_up, ("dp", "seq"), scatter_dimension=0, tiled=True),
        lax.psum_scatter(grad_bias_down, ("dp", "seq"), scatter_dimension=0, tiled=True),
        lax.psum_scatter(grad_gain_two, ("dp", "seq"), scatter_dimension=0, tiled=True),
        lax.psum_scatter(grad_shift_two, ("dp", "seq"), scatter_dimension=0, tiled=True),
    )
    table_sum, totals = lax.psum((jnp.sum(grad_tables, axis=0), local_sums), ("dp", "seq"))
    content_count = totals[6] * MODEL_WIDTH
    query_count = float(seq_count * lax.axis_size("dp") * pred_count * group_size * MODEL_WIDTH)
    stats = jnp.sqrt(
        jnp.stack(
            [
                totals[0] / content_count,
                totals[1] / query_count,
                totals[2] / content_count,
                totals[3] / query_count,
                totals[4] / content_count,
                totals[5] / query_count,
            ]
        )
    )
    return (
        outputs[:, :shard_length],
        outputs[:, shard_length:],
        grad_content,
        grad_query,
        owned[0],
        owned[4],
        owned[1],
        owned[5],
        owned[6],
        owned[7],
        owned[2],
        owned[8],
        owned[3],
        owned[9],
        owned[10],
        owned[11],
        table_sum,
        stats,
    )


def solution(mesh):
    in_specs = (
        P("dp", "seq", None),
        P("dp", "seq", None),
        P("dp", "seq"),
        P("dp", "seq"),
        P("dp", "seq"),
        P("dp", "seq"),
        P(),
        P(("dp", "seq"), None),
        P(("dp", "seq")),
        P(("dp", "seq"), None),
        P(("dp", "seq")),
        P(("dp", "seq")),
        P(("dp", "seq")),
        P(("dp", "seq"), None),
        P(("dp", "seq")),
        P(("dp", "seq"), None),
        P(("dp", "seq")),
        P(("dp", "seq")),
        P(("dp", "seq")),
        P(),
        P("dp", "seq", None),
        P("dp", "seq", None),
    )
    out_specs = (
        P("dp", "seq", None),
        P("dp", "seq", None),
        P("dp", "seq", None),
        P("dp", "seq", None),
        P(("dp", "seq"), None),
        P(("dp", "seq")),
        P(("dp", "seq"), None),
        P(("dp", "seq")),
        P(("dp", "seq")),
        P(("dp", "seq")),
        P(("dp", "seq"), None),
        P(("dp", "seq")),
        P(("dp", "seq"), None),
        P(("dp", "seq")),
        P(("dp", "seq")),
        P(("dp", "seq")),
        P(),
        P(),
    )
    return jax.shard_map(local, mesh=mesh, in_specs=in_specs, out_specs=out_specs, check_vma=False)
```

profile of v0, /device:TPU:0, one launch (start us, length us, event | category | flops | bytes accessed | tf_op | source)
XLA Modules:
  0.0 1047.3 jit_solution(13042704287993670860)
XLA Ops:
  14.7 42.6 %all-reduce.19 = (bf16[1536]{0:T(1024)(128)(2,1)S(1)}, bf16[768]{0:T(1024)(128)(2,1)S(1)}, bf16[768]{0:T(1024)(128)(2,1)S(1)}, bf16[768]{0:T(1024)(128)(2,1)S(1)...) all-reduce(bf16[1536]{0:T(1024)(128)(2,1)S(1)} %dynamic-update-slic, ...), channel_id=1, replica_groups=mesh['dp'=8,'seq'=4] {'dp','seq'}, use_global_device_ids=true, to_apply=%add.2 | all-reduce | flops 9216 | bytes 36864
  57.5 16.3 %all-gather.7.cloned.1.call-done = bf16[768,2304]{1,0:T(8,128)(2,1)} async-done(((bf16[24,2304]{1,0:T(8,128)(2,1)}), bf16[768,2304]{1,0:T(8,128)(2,1)}) %all-gather.7.cloned.1.call-update) | async-done | bytes 3538960 | tf_op jit(solution)/shard_map/all_gather | solution.py:182
  73.8 4.7 fusion.27
  80.5 5.2 all_gather.64
  89.0 5.2 all_gather.62
  94.1 5.7 all_gather.65
  99.9 1.1 gather_fusion
  101.0 1.1 gather_fusion.1
  102.9 1.0 fusion.43
  105.0 38.3 %fusion.1 = f32[588,2048,12]{1,2,0:T(8,128)} fusion(s32[588,2048]{1,0:T(8,128)S(1)} %subtract_add_fusion, s32[32]{0:T(128)S(1)} %add.217, s32[32]{0:T(128)S(1)} %get-tuple-element.199, bf16[32,12]{0,1:T(8,128)(2,1)S(1)} %copy-done), kind=kOutput, calls=%fused_computation.4 | convolution fusion | flops 1040449536 | bytes 62620672 | tf_op jit(solution)/shard_map/while/body/eval_jaxpr/rlb,bh->hrl/dot_general | solution.py:71
  143.3 2.4 fusion.23
  145.8 3.1 add_convert_fusion.1
  148.8 2.2 copy.75
  151.1 5.8 fusion.79
  156.9 4.7 copy.76
  161.6 4.7 copy.74
  166.3 65.1 %fusion.83 = (f32[12,588]{1,0:T(8,128)S(1)}, f32[12,588,2048]{2,1,0:T(8,128)}) fusion(f32[588,2048,12]{1,2,0:T(8,128)} %fusion.1, bf16[588,12,64]{0,2,1:T(8,128)(2,1)} %bitcast.119, bf16[2048,12,64]{0,2,1:T(8,128)(2,1)} %bitcast.106, pred[588,2048]{1,0:T(8,128)(4,1)S(1)} %fusion.23), kind=kOutput, calls=%fused_computation.160 | convolution fusion | flops 1907483776 | bytes 120886848 | tf_op jit(solution)/shard_map/while/body/eval_jaxpr/rhd,lhd->hrl/dot_general | solution.py:65
  231.4 19.5 %fusion.9 = f32[12,588]{1,0:T(8,128)S(1)} fusion(f32[12,588,2048]{2,1,0:T(8,128)} %get-tuple-element.250, f32[12,588]{1,0:T(8,128)S(1)} %get-tuple-element.249), kind=kLoop, calls=%fused_computation.18 | loop fusion | flops 28894320 | bytes 57859200 | tf_op jit(solution)/shard_map/while/body/eval_jaxpr/reduce_sum | solution.py:89
  250.9 22.3 %fusion.38 = bf16[12,64,588]{2,1,0:T(8,128)(2,1)} fusion(bf16[2048,12,64]{0,2,1:T(8,128)(2,1)} %bitcast.111, f32[12,588,2048]{2,1,0:T(8,128)} %get-tuple-element.250, f32[12,588]{1,0:T(8,128)S(1)} %fusion.9, f32[12,588]{1,0:T(8,128)S(1)} %get-tuple-element.249), kind=kOutput, calls=%fused_computation.95 | convolution fusion | flops 1893491712 | bytes 61908096 | tf_op jit(solution)/shard_map/while/body/eval_jaxpr/hrl,lhd->rhd/dot_general | solution.py:91
  273.3 3.8 fusion.78
  277.6 22.5 %multiply_convert_fusion.1 = (bf16[588,3072]{1,0:T(8,128)(2,1)}, f32[588,3072]{1,0:T(8,128)}, f32[588,3072]{1,0:T(8,128)}) fusion(f32[3072]{0:T(1024)S(1)} %copy-done.50, bf16[768,3072]{1,0:T(8,128)(2,1)} %all-gather.11.cloned.1.call-done, f32[588,768]{1,0:T(8,128)S(1)} %get-tuple-element.230, f32[768]{0:T(1024)S(1)} %copy-done.32, f32[768]{0:T(1024)S(1)} %copy-done.30, ...), kind=kOutput, calls=%fused_computation.28 | convolution fusion | flops 2896008192 | bytes 24611424 | tf_op jit(solution)/shard_map/srd,df->srf/dot_general | solution.py:250
  300.1 11.2 %all-gather.13.cloned.1.call-done = bf16[3072,768]{1,0:T(8,128)(2,1)} async-done(((bf16[96,768]{1,0:T(8,128)(2,1)}), bf16[3072,768]{1,0:T(8,128)(2,1)}) %all-gather.13.cloned.1.call-update) | async-done | bytes 4718608 | tf_op jit(solution)/shard_map/all_gather | solution.py:185
  311.4 8.0 fusion.76
  319.7 1.3 multiply_reduce_fusion.1
  321.0 2.8 convert_reduce_fusion.2
  323.8 10.2 convert_reduce_fusion
  334.1 4.0 multiply_reduce_fusion.2
  338.1 1.2 convert_reduce_fusion.3
  339.3 1.3 copy-done.6
  340.6 1.9 convolution_convert_fusion
  342.5 1.5 copy.79
  344.0 22.8 %fusion.24 = bf16[12,64,2048]{2,1,0:T(8,128)(2,1)} fusion(bf16[588,12,64]{0,2,1:T(8,128)(2,1)S(1)} %bitcast.117, f32[12,588,2048]{2,1,0:T(8,128)} %get-tuple-element.250, f32[12,588]{1,0:T(8,128)S(1)} %log_add_fusion), kind=kOutput, calls=%fused_computation.50 | convolution fusion | flops 1880162304 | bytes 61879872 | tf_op jit(solution)/shard_map/while/body/eval_jaxpr/hrl,rhd->lhd/dot_general | solution.py:139
  366.9 40.5 %multiply_reduce_fusion = (f32[12,588]{1,0:T(8,128)S(1)}, f32[12,588,2048]{2,1,0:T(8,128)}) fusion(f32[12,588,2048]{2,1,0:T(8,128)} %get-tuple-element.250, f32[12,588]{1,0:T(8,128)S(1)} %log_add_fusion, bf16[588,12,64]{0,2,1:T(8,128)(2,1)S(1)} %bitcast.118, bf16[2048,12,64]{0,2,1:T(8,128)(2,1)} %bitcast.112), kind=kOutput, calls=%fused_computation.14 | convolution fusion | flops 1893033088 | bytes 119710848 | tf_op jit(solution)/shard_map/while/body/eval_jaxpr/rhd,lhd->hrl/dot_general | solution.py:123
  407.4 45.9 %multiply_convert_fusion = bf16[12,588,2048]{2,1,0:T(8,128)(2,1)} fusion(f32[12,588,2048]{2,1,0:T(8,128)} %get-tuple-element.254, f32[12,588,2048]{2,1,0:T(8,128)} %get-tuple-element.250, f32[12,588]{1,0:T(8,128)S(1)} %get-tuple-element.253, f32[12,588]{1,0:T(8,128)S(1)} %log_add_fusion), kind=kLoop, calls=%fused_computation.13 | loop fusion | flops 57802752 | bytes 144563328 | tf_op jit(solution)/shard_map/while/body/eval_jaxpr/convert_element_type | solution.py:127
  453.3 12.6 %multiply_convert_fusion.2 = bf16[12,64,2048]{2,1,0:T(8,128)(2,1)S(1)} fusion(bf16[588,12,64]{0,2,1:T(8,128)(2,1)S(1)} %bitcast.120, bf16[12,588,2048]{2,1,0:T(8,128)(2,1)} %multiply_convert_fusion), kind=kOutput, calls=%fused_computation.44 | convolution fusion | flops 1852833792 | bytes 32950272 | tf_op jit(solution)/shard_map/while/body/eval_jaxpr/hrl,rhd->lhd/dot_general | solution.py:136
  465.8 3.7 pad_maximum_fusion.1
  469.6 1.1 copy-done.19
  470.8 4.0 fusion.60
  474.9 8.8 fusion.72
  483.8 1.4 copy-done.27
  485.2 8.6 fusion.63
  493.9 1.8 copy-done.2
  495.7 13.5 %convert_reduce_fusion.1 = (f32[12,64]{1,0:T(8,128)S(1)}, bf16[12,64,588]{2,1,0:T(8,128)(2,1)S(1)}) fusion(bf16[2048,12,64]{0,2,1:T(8,128)(2,1)S(1)} %bitcast.107, bf16[12,588,2048]{2,1,0:T(8,128)(2,1)} %multiply_convert_fusion), kind=kOutput, calls=%fused_computation.59 | convolution fusion | flops 1851493632 | bytes 32953344 | tf_op jit(solution)/shard_map/while/body/eval_jaxpr/hrl,lhd->rhd/dot_general | solution.py:129
  509.3 0.9 copy-done.13
  510.2 2.6 fusion.55
  512.8 14.2 %reduce-scatter.8.cloned.1.call-done = bf16[1,512,1536]{1,2,0:T(8,128)(2,1)} async-done(((bf16[1,2048,1536]{1,2,0:T(8,128)(2,1)}), bf16[1,512,1536]{1,2,0:T(8,128)(2,1)}) %reduce-scatter.8.cloned.1.call-update) | async-done | bytes 1572880 | tf_op jit(solution)/shard_map/reduce_scatter | solution.py:322
  526.9 2.9 convolution_bitcast_fusion
  529.9 3.3 pad_maximum_fusion
  533.2 8.0 copy.84
  542.5 2.0 multiply_reduce_fusion.9
  544.6 1.0 slice.116
  545.5 2.7 slice.115
  548.2 0.9 copy.81
  549.2 2.8 add_bitcast_fusion
  552.0 1.2 copy-done.21
  553.3 0.9 copy.82
  555.5 1.4 fusion.34
  557.0 4.6 stack.40
  561.7 41.3 %fusion.44 = f32[32,12]{0,1:T(8,128)S(1)} fusion(bf16[12,588,2048]{2,1,0:T(8,128)(2,1)} %multiply_convert_fusion, s32[588,2048]{1,0:T(8,128)} %copy-done.16, s32[32]{0:T(128)S(1)} %copy-done.62, s32[32]{0:T(128)S(1)} %copy-done.59), kind=kOutput, calls=%fused_computation.99 | convolution fusion | flops 1040449536 | bytes 33720064 | tf_op jit(solution)/shard_map/while/body/eval_jaxpr/hrl,rlb->bh/dot_general | solution.py:132
  603.2 41.0 %all-reduce.18 = (f32[1536]{0:T(1024)S(1)}, f32[768]{0:T(1024)S(1)}, f32[768]{0:T(1024)S(1)}, f32[768]{0:T(1024)S(1)}, f32[3072]{0:T(1024)S(1)}, /*index=5*/f32[...) all-reduce(f32[1536]{0:T(1024)S(1)} %pad_maximum_fusion.3, ...), channel_id=5, replica_groups=mesh['dp'=8,'seq'=4] {'dp','seq'}, use_global_device_ids=true, to_apply=%region_17.19.clone | all-reduce | flops 9607 | bytes 76856
  654.6 4.4 slice_add_fusion
  659.0 114.7 %reduce-scatter.12.cloned.1.call-done = f32[24,3072]{1,0:T(8,128)} async-done(((f32[768,3072]{1,0:T(8,128)}), f32[24,3072]{1,0:T(8,128)}) %reduce-scatter.12.cloned.1.call-update) | async-done | bytes 294928 | tf_op jit(solution)/shard_map/reduce_scatter | solution.py:365
  773.7 141.9 %reduce-scatter.14.cloned.1.call-done = f32[96,768]{1,0:T(8,128)} async-done(((f32[3072,768]{1,0:T(8,128)}), f32[96,768]{1,0:T(8,128)}) %reduce-scatter.14.cloned.1.call-update) | async-done | bytes 294928 | tf_op jit(solution)/shard_map/reduce_scatter | solution.py:366
  915.6 124.6 %reduce-scatter.16.cloned.1.call-done = f32[24,2304]{1,0:T(8,128)} async-done(((f32[768,2304]{1,0:T(8,128)}), f32[24,2304]{1,0:T(8,128)}) %reduce-scatter.16.cloned.1.call-update) | async-done | bytes 221200
  (218 shorter events, 24.4 us)
Async XLA Ops:
  7.2 97.8 %copy-start = (bf16[32,12]{0,1:T(8,128)(2,1)S(1)}, bf16[32,12]{0,1:T(8,128)(2,1)}, u32[]{:S(2)}) copy-start(bf16[32,12]{0,1:T(8,128)(2,1)} %param.43) | copy-start | bytes 2308
  7.2 66.6 %all-gather.7.cloned.1.call-start = ((), (), s32[]{:S(2)}) async-start(), calls=%async_computation.5 | async-start | bytes 3649536 | tf_op jit(solution)/shard_map/all_gather | solution.py:182
  7.9 143.1 %all-gather.15.cloned.1.call-start = ((), (), s32[]{:S(2)}) async-start(), calls=%async_computation.13 | async-start | bytes 7864320 | tf_op jit(solution)/shard_map/all_gather | solution.py:221
  57.4 23.0 %copy-start.40 = (s32[1,512]{1,0:T(1,128)S(1)}, s32[1,512]{1,0:T(1,128)}, u32[]{:S(2)}) copy-start(s32[1,512]{1,0:T(1,128)} %param.27) | copy-start | bytes 6148
  57.4 28.2 %copy-start.57 = (s32[1,76]{1,0:T(1,128)S(1)}, s32[1,76]{1,0:T(1,128)}, u32[]{:S(2)}) copy-start(s32[1,76]{1,0:T(1,128)} %param.28) | copy-start | bytes 916
  57.4 28.2 %copy-start.48 = (s32[4095]{0:T(1024)S(1)}, s32[4095]{0:T(1024)}, u32[]{:S(2)}) copy-start(s32[4095]{0:T(1024)} %param.30) | copy-start | bytes 49144
  57.4 31.5 %copy-start.53 = (s32[1,512]{1,0:T(1,128)S(1)}, s32[1,512]{1,0:T(1,128)}, u32[]{:S(2)}) copy-start(s32[1,512]{1,0:T(1,128)} %param.26) | copy-start | bytes 6148
  57.4 36.7 %copy-start.52 = (s32[1,512]{1,0:T(1,128)S(1)}, s32[1,512]{1,0:T(1,128)}, u32[]{:S(2)}) copy-start(s32[1,512]{1,0:T(1,128)} %param.29) | copy-start | bytes 6148
  57.5 45.4 %copy-start.31 = (f32[1,76,768]{2,0,1:T(1,128)S(1)}, f32[1,76,768]{2,0,1:T(1,128)}, u32[]{:S(2)}) copy-start(f32[1,76,768]{2,0,1:T(1,128)} %param.45) | copy-start | bytes 700420
  78.4 24.4 %copy-start.9 = (f32[1,512,768]{2,1,0:T(8,128)S(1)}, f32[1,512,768]{2,1,0:T(8,128)}, u32[]{:S(2)}) copy-start(f32[1,512,768]{2,1,0:T(8,128)} %param.44) | copy-start | bytes 4718596
  78.4 26.0 %copy-start.29 = (f32[1,76,768]{2,0,1:T(1,128)S(1)}, f32[1,76,768]{2,0,1:T(1,128)}, u32[]{:S(2)}) copy-start(f32[1,76,768]{2,0,1:T(1,128)} %param.25) | copy-start | bytes 700420
  78.5 194.8 %all-gather.9.cloned.1.call-start = ((), (), s32[]{:S(2)}) async-start(), calls=%async_computation.6 | async-start | bytes 1216512 | tf_op jit(solution)/shard_map/all_gather | solution.py:183
  79.2 198.3 %all-gather.11.cloned.1.call-start = ((), (), s32[]{:S(2)}) async-start(), calls=%async_computation.7 | async-start | bytes 4866048 | tf_op jit(solution)/shard_map/all_gather | solution.py:184
  79.8 231.6 %all-gather.13.cloned.1.call-start = ((), (), s32[]{:S(2)}) async-start(), calls=%async_computation.8 | async-start | bytes 4866048 | tf_op jit(solution)/shard_map/all_gather | solution.py:185
  80.4 446.6 %reduce-scatter.8.cloned.1.call-start = ((), (), s32[]{:S(2)}) async-start(), calls=%async_computation.9 | async-start | bytes 7864320 | tf_op jit(solution)/shard_map/reduce_scatter | solution.py:322
  80.4 6.7 copy-start.38
  85.9 19.1 %copy-start.58 = (s32[32]{0:T(128)}, s32[32]{0:T(128)S(1)}, u32[]{:S(2)}) copy-start(s32[32]{0:T(128)S(1)} %get-tuple-element.199) | copy-start | bytes 388
  86.0 18.9 %copy-start.34 = (f32[588]{0:T(1024)}, f32[588]{0:T(1024)S(1)}, u32[]{:S(2)}) copy-start(f32[588]{0:T(1024)S(1)} %pad_reduce_fusion) | copy-start | bytes 7060
  87.2 17.7 %copy-start.36 = (f32[768]{0:T(1024)}, f32[768]{0:T(1024)S(1)}, u32[]{:S(2)}) copy-start(f32[768]{0:T(1024)S(1)} %convert_element_type.174) | copy-start | bytes 9220
  104.5 41.3 %copy-start.23 = (f32[1,76,768]{2,1,0:T(8,128)}, f32[1,76,768]{2,1,0:T(8,128)S(1)}, u32[]{:S(2)}) copy-start(f32[1,76,768]{2,1,0:T(8,128)S(1)} %copy.96) | copy-start | bytes 700420
  104.9 38.4 %copy-start.16 = (s32[588,2048]{1,0:T(8,128)}, s32[588,2048]{1,0:T(8,128)S(1)}, u32[]{:S(2)}) copy-start(s32[588,2048]{1,0:T(8,128)S(1)} %subtract_add_fusion) | copy-start | bytes 14450692
  104.9 38.4 %copy-start.61 = (s32[32]{0:T(128)}, s32[32]{0:T(128)S(1)}, u32[]{:S(2)}) copy-start(s32[32]{0:T(128)S(1)} %add.217) | copy-start | bytes 388
  105.0 40.8 %copy-start.3 = (f32[1,512,768]{2,1,0:T(8,128)S(1)}, f32[1,512,768]{2,1,0:T(8,128)}, u32[]{:S(2)}) copy-start(f32[1,512,768]{2,1,0:T(8,128)} %param.24) | copy-start | bytes 4718596
  250.9 22.3 %copy-start.45 = (f32[768]{0:T(1024)S(1)}, f32[768]{0:T(1024)}, u32[]{:S(2)}) copy-start(f32[768]{0:T(1024)} %convert_element_type.167) | copy-start | bytes 9220
  273.3 4.3 copy-start.30
  273.3 4.3 copy-start.32
  273.3 4.3 copy-start.50
  277.5 33.9 %copy-start.54 = (f32[768]{0:T(1024)S(1)}, f32[768]{0:T(1024)}, u32[]{:S(2)}) copy-start(f32[768]{0:T(1024)} %convert_element_type.173) | copy-start | bytes 9220
  311.3 8.3 copy-start.10
  311.3 8.3 copy-start.18
  311.4 8.3 copy-start.35
  311.4 8.4 copy-start.37
  319.7 4.1 copy-start.60
  321.0 13.1 %slice-start = ((s8[4718592]{0:T(1024)(128)(4,1)}), s8[4194304]{0:T(1024)(128)(4,1)S(1)}, s32[]{:S(2)}) async-start(s8[4718592]{0:T(1024)(128)(4,1)} %bitcast.131), calls=%async_computation.15 | async-start | bytes 8388608
  323.8 10.3 copy-start.26
  323.8 10.3 slice-start.1
  334.1 4.0 copy-start.20
  407.4 45.9 %copy-start.11 = (bf16[588,768]{0,1:T(8,128)(2,1)S(1)}, bf16[588,768]{0,1:T(8,128)(2,1)}, u32[]{:S(2)}) copy-start(bf16[588,768]{0,1:T(8,128)(2,1)} %copy.75) | copy-start | bytes 2709508
  453.3 12.6 %copy-start.8 = (bf16[12,64,2048]{2,1,0:T(8,128)(2,1)S(1)}, bf16[12,64,2048]{2,1,0:T(8,128)(2,1)}, u32[]{:S(2)}) copy-start(bf16[12,64,2048]{2,1,0:T(8,128)(2,1)} %fusion.24) | copy-start | bytes 9437188
  469.6 5.3 copy-start.33
  469.6 189.4 %reduce-scatter.10.cloned.1.call-start = ((), (), s32[]{:S(2)}) async-start(), calls=%async_computation.10 | async-start | bytes 2433024 | tf_op jit(solution)/shard_map/reduce_scatter | solution.py:364
  474.8 298.9 %reduce-scatter.12.cloned.1.call-start = ((), (), s32[]{:S(2)}) async-start(), calls=%async_computation.11 | async-start | bytes 9732096 | tf_op jit(solution)/shard_map/reduce_scatter | solution.py:365
  483.7 431.9 %reduce-scatter.14.cloned.1.call-start = ((), (), s32[]{:S(2)}) async-start(), calls=%async_computation.12 | async-start | bytes 9732096 | tf_op jit(solution)/shard_map/reduce_scatter | solution.py:366
  493.8 16.3 %copy-start.24 = (f32[1,76,768]{2,1,0:T(8,128)S(1)}, f32[1,76,768]{2,1,0:T(8,128)}, u32[]{:S(2)}) copy-start(f32[1,76,768]{2,1,0:T(8,128)} %copy-done.23) | copy-start | bytes 700420
  493.8 546.4 %reduce-scatter.16.cloned.1.call-start = ((), (), s32[]{:S(2)}) async-start(), calls=%async_computation.14 | async-start | bytes 7299072
  495.7 14.5 %copy-start.4 = (f32[1,512,768]{2,1,0:T(8,128)S(1)}, f32[1,512,768]{2,1,0:T(8,128)}, u32[]{:S(2)}) copy-start(f32[1,512,768]{2,1,0:T(8,128)} %param.24) | copy-start | bytes 4718596
  509.2 17.7 %copy-start.5 = (f32[1,512,768]{2,1,0:T(8,128)S(1)}, f32[1,512,768]{2,1,0:T(8,128)}, u32[]{:S(2)}) copy-start(f32[1,512,768]{2,1,0:T(8,128)} %param.24) | copy-start | bytes 4718596
  526.9 3.0 copy-start.12
  541.3 7.9 copy-start.7
  549.2 5.0 copy-start.14
  549.2 5.7 copy-start.25
  549.2 6.3 copy-start.39
  553.2 8.3 copy-start.59
  553.2 8.3 copy-start.62
  561.6 41.4 %copy-start.15 = (bf16[1,512,1536]{1,2,0:T(8,128)(2,1)S(1)}, bf16[1,512,1536]{1,2,0:T(8,128)(2,1)}, u32[]{:S(2)}) copy-start(bf16[1,512,1536]{1,2,0:T(8,128)(2,1)} %reduce-scatter.8.cloned.1.call-done) | copy-start | bytes 4718596
  561.6 41.6 %copy-start.44 = (f32[768]{0:T(1024)S(1)}, f32[768]{0:T(1024)}, u32[]{:S(2)}) copy-start(f32[768]{0:T(1024)} %get-tuple-element.221) | copy-start | bytes 9220
  561.6 41.6 %copy-start.46 = (f32[768]{0:T(1024)S(1)}, f32[768]{0:T(1024)}, u32[]{:S(2)}) copy-start(f32[768]{0:T(1024)} %get-tuple-element.195) | copy-start | bytes 9220
  561.6 41.6 %copy-start.47 = (f32[768]{0:T(1024)S(1)}, f32[768]{0:T(1024)}, u32[]{:S(2)}) copy-start(f32[768]{0:T(1024)} %get-tuple-element.190) | copy-start | bytes 9220
  561.6 41.6 %copy-start.49 = (f32[768]{0:T(1024)S(1)}, f32[768]{0:T(1024)}, u32[]{:S(2)}) copy-start(f32[768]{0:T(1024)} %get-tuple-element.223) | copy-start | bytes 9220
  561.6 41.6 %copy-start.51 = (f32[3072]{0:T(1024)S(1)}, f32[3072]{0:T(1024)}, u32[]{:S(2)}) copy-start(f32[3072]{0:T(1024)} %get-tuple-element.257) | copy-start | bytes 36868
  561.6 41.6 %copy-start.55 = (f32[768]{0:T(1024)S(1)}, f32[768]{0:T(1024)}, u32[]{:S(2)}) copy-start(f32[768]{0:T(1024)} %get-tuple-element.192) | copy-start | bytes 9220
  561.6 41.6 %copy-start.56 = (f32[768]{0:T(1024)S(1)}, f32[768]{0:T(1024)}, u32[]{:S(2)}) copy-start(f32[768]{0:T(1024)} %get-tuple-element.197) | copy-start | bytes 9220
  561.7 93.0 %copy-start.22 = (f32[1,588,768]{2,1,0:T(8,128)S(1)}, f32[1,588,768]{2,1,0:T(8,128)}, u32[]{:S(2)}) copy-start(f32[1,588,768]{2,1,0:T(8,128)} %copy-done.21) | copy-start | bytes 5419012
  654.0 386.2 %copy-start.1 = (bf16[32,12]{0,1:T(8,128)(2,1)S(1)}, bf16[32,12]{0,1:T(8,128)(2,1)}, u32[]{:S(2)}) copy-start(bf16[32,12]{0,1:T(8,128)(2,1)} %param.43) | copy-start | bytes 2308
  (11 other events, 16.1 us)
Sparse Core Ops, SparseCore 0:
  10.9 62.7 all-gather.6
  78.6 45.2 all-gather.14
  126.8 54.0 all-gather.8
  183.6 62.5 all-gather.10
  249.0 62.3 all-gather.12
  469.7 57.1 reduce-scatter.7
  533.6 99.2 reduce-scatter.9
  639.4 134.2 reduce-scatter.11
  781.2 134.3 reduce-scatter.13
  921.7 118.4 reduce-scatter.15
where the time goes:
time: 1050 us
  waiting for transfers between devices  425 us (40%)
  matrix products  349 us (33%)
  blocking collectives  99.7 us (9%)
  other arithmetic  92.3 us (9%)
  local copies, waits for them, and re-layouts  60.9 us (6%)
  between operations  19.7 us (2%)
    reduce_scatter x1, waiting for transfers between devices, local(): lax.psum_scatter(grad_down, ('dp', 'seq'), scatter_dimension=0, tiled=True)  142 us
    unnamed x11, waiting for transfers between devices  127 us
    reduce_scatter x1, waiting for transfers between devices, local(): lax.psum_scatter(grad_up, ('dp', 'seq'), scatter_dimension=0, tiled=True)  115 us
    unnamed x2, blocking collectives  83.7 us
    dot_general x1, matrix products, masked_scores(): jnp.einsum('rhd,lhd->hrl', query_heads, key_heads, preferred_element_type...  65.1 us
    convert_element_type x1, other arithmetic, attend_backward(): (probs * (grad_probs - row_delta[..., None])).astype(jnp.bfloat16)  45.9 us
    dot_general x1, matrix products, attend_backward(): jnp.einsum('hrl,rlb->bh', grad_scores, onehot, preferred_element_type=jnp...  41.3 us
    dot_general x1, matrix products, attend_backward(): jnp.einsum('rhd,lhd->hrl', grad_heads, value_heads, preferred_element_typ...  40.5 us
  transfers between devices with their start and end apart: 10, of which 6 were waited for; matrix products, arithmetic and copies ran while one was open for 32% of the time, Pallas kernels for 0%

commit v1 on v0

--- a/solution.py
+++ b/solution.py
@@ -1,6 +1,11 @@
+import functools
+import math
+
 import jax
 import jax.numpy as jnp
 from jax import lax
+from jax.experimental import pallas as pl
+from jax.experimental.pallas import tpu as pltpu
 from jax.sharding import PartitionSpec as P
 
 MODEL_WIDTH = 768
@@ -148,7 +153,7 @@
     return results
 
 
-def local(
+def local_general(
     content,
     query_stream,
     segment_ids,
@@ -410,6 +415,1206 @@
     )
 
 
+LOG2E = math.log2(math.e)
+TILE = 256
+HALF = 128
+REACH = 9
+DIAGS = 2 * REACH + 1
+WIDE = SEQ_LEN + HALF
+MASKED = -1e30
+F32 = jnp.float32
+BF16 = jnp.bfloat16
+
+
+def bias_kernel(rows_q, own, rev_ref, fold_ref, hot_ref, shift_ref, tile_ref, qbias_ref):
+    lane = lax.broadcasted_iota(jnp.int32, (HALF, HALF), 1)
+    for h in range(own):
+        for e in range(-REACH, REACH + 1):
+            start = HALF * (15 - e)
+            row = rev_ref[h : h + 1, start : start + 2 * HALF]
+            skew = pltpu.roll(
+                jnp.broadcast_to(row, (HALF, 2 * HALF)), 0, 1, stride=1, stride_axis=0
+            )
+            tile_ref[h, e + REACH] = skew[:, HALF:]
+    for t in range(rows_q // HALF):
+        shift = shift_ref[t * HALF : (t + 1) * HALF, :]
+        place = lane + shift
+        wrap = place >= HALF
+        idx = jnp.where(wrap, place - HALF, place)
+        for h in range(own):
+            spread = jnp.dot(
+                hot_ref[t * HALF : (t + 1) * HALF, :], fold_ref[h], preferred_element_type=F32
+            )
+            prev = jnp.take_along_axis(spread[:, :HALF], idx, axis=1)
+            for j in range(SEQ_LEN // HALF):
+                cur = jnp.take_along_axis(
+                    spread[:, (j + 1) * HALF : (j + 2) * HALF], idx, axis=1
+                )
+                out = jnp.where(wrap, cur, prev) * LOG2E
+                qbias_ref[h, j * HALF : (j + 1) * HALF, t * HALF : (t + 1) * HALF] = out.T
+                prev = cur
+
+
+def bias_call(rev, fold, hot, shift):
+    own = rev.shape[0]
+    rows_q = hot.shape[0]
+    return pl.pallas_call(
+        functools.partial(bias_kernel, rows_q, own),
+        out_shape=(
+            jax.ShapeDtypeStruct((own, DIAGS, HALF, HALF), F32),
+            jax.ShapeDtypeStruct((own, SEQ_LEN, rows_q), F32),
+        ),
+        compiler_params=pltpu.CompilerParams(vmem_limit_bytes=50 << 20),
+        name="bias_tiles",
+    )(rev, fold, hot, shift)
+
+
+def bias_block(tile_ref, h, e):
+    mid = tile_ref[h, e]
+    return jnp.concatenate(
+        [
+            jnp.concatenate([mid, tile_ref[h, e - 1]], axis=1),
+            jnp.concatenate([tile_ref[h, e + 1], mid], axis=1),
+        ],
+        axis=0,
+    )
+
+
+def mask_block(kmeta_ref, rseg_ref, rlim_ref, krow, rcol, width):
+    kseg = kmeta_ref[0, pl.ds(krow, TILE), :]
+    kord = kmeta_ref[1, pl.ds(krow, TILE), :]
+    parts = []
+    for w in range(width // HALF):
+        rseg = rseg_ref[:, pl.ds(rcol + w * HALF, HALF)]
+        rlim = rlim_ref[:, pl.ds(rcol + w * HALF, HALF)]
+        ok = (kseg == rseg) & (kord <= rlim)
+        parts.append(jnp.where(ok, 0.0, MASKED))
+    return parts[0] if len(parts) == 1 else jnp.concatenate(parts, axis=1)
+
+
+def fwd_kernel(
+    own,
+    rows_q,
+    span_ref,
+    qt_ref,
+    k_ref,
+    vt_ref,
+    kmeta_ref,
+    rseg_ref,
+    rlim_ref,
+    tile_ref,
+    qbias_ref,
+    ctx_ref,
+    rows_ref,
+    lse_ref,
+    s_scr,
+):
+    def run(rcol, width, lo, hi, bias_of):
+        heads = range(own)
+
+        def fold(op, x):
+            rows = [x[i * 8 : (i + 1) * 8] for i in range(x.shape[0] // 8)]
+            while len(rows) > 1:
+                rows = [op(rows[i], rows[i + 1]) for i in range(0, len(rows), 2)]
+            return rows[0]
+
+        def score(kt, tops):
+            krow = pl.multiple_of(kt * TILE, TILE)
+            mask = mask_block(kmeta_ref, rseg_ref, rlim_ref, krow, rcol, width)
+            new = []
+            for h in heads:
+                s = jnp.dot(
+                    k_ref[h, pl.ds(krow, TILE), :],
+                    qt_ref[h * HEAD_DIM : (h + 1) * HEAD_DIM, pl.ds(rcol, width)],
+                    preferred_element_type=F32,
+                )
+                s = s * (SCALE * LOG2E) + (bias_of(h, kt) + mask)
+                s_scr[h, pl.ds(krow, TILE), :width] = s
+                new.append(jnp.maximum(tops[h], fold(jnp.maximum, s)))
+            return tuple(new)
+
+        tops = lax.fori_loop(
+            lo, hi + 1, score, tuple(jnp.full((8, width), MASKED, F32) for _ in heads)
+        )
+        tops = [jnp.max(t, axis=0, keepdims=True) for t in tops]
+
+        def weigh(kt, carry):
+            krow = pl.multiple_of(kt * TILE, TILE)
+            sums, accs = carry
+            new_sums, new_accs = [], []
+            for h in heads:
+                p = jnp.exp2(s_scr[h, pl.ds(krow, TILE), :width] - tops[h])
+                new_sums.append(sums[h] + fold(jnp.add, p))
+                new_accs.append(
+                    accs[h]
+                    + jnp.dot(
+                        vt_ref[h * HEAD_DIM : (h + 1) * HEAD_DIM, pl.ds(krow, TILE)],
+                        p.astype(BF16),
+                        preferred_element_type=F32,
+                    )
+                )
+            return tuple(new_sums), tuple(new_accs)
+
+        sums, accs = lax.fori_loop(
+            lo,
+            hi + 1,
+            weigh,
+            (
+                tuple(jnp.zeros((8, width), F32) for _ in heads),
+                tuple(jnp.zeros((HEAD_DIM, width), F32) for _ in heads),
+            ),
+        )
+        outs = []
+        for h in heads:
+            total = jnp.sum(sums[h], axis=0, keepdims=True)
+            outs.append(accs[h] / total)
+            lse_ref[h : h + 1, pl.ds(rcol, width)] = tops[h] + jnp.log2(total)
+        out = jnp.concatenate(outs, axis=0)
+        ctx_ref[:, pl.ds(rcol, width)] = out.astype(BF16)
+        rows_ref[pl.ds(rcol, width), :] = out.T.astype(BF16)
+
+    def content_tile(qt, carry):
+        def bias_of(h, kt):
+            return bias_block(tile_ref, h, 2 * (kt - qt) + REACH)
+
+        run(pl.multiple_of(qt * TILE, TILE), TILE, span_ref[0, qt], span_ref[1, qt], bias_of)
+        return carry
+
+    lax.fori_loop(0, SEQ_LEN // TILE, content_tile, 0)
+
+    def query_tile(t, carry):
+        col = pl.multiple_of(t * HALF, HALF)
+
+        def bias_of(h, kt):
+            return qbias_ref[h, pl.ds(pl.multiple_of(kt * TILE, TILE), TILE), pl.ds(col, HALF)]
+
+        run(
+            pl.multiple_of(SEQ_LEN + t * HALF, HALF),
+            HALF,
+            span_ref[0, SEQ_LEN // TILE],
+            span_ref[1, SEQ_LEN // TILE],
+            bias_of,
+        )
+        return carry
+
+    lax.fori_loop(0, rows_q // HALF, query_tile, 0)
+
+
+def fwd_call(span, qt, k3, vt, kmeta, rseg, rlim, tiles, qbias):
+    own = k3.shape[0]
+    rows = qt.shape[1]
+    rows_q = rows - SEQ_LEN
+    vm = pl.BlockSpec(memory_space=pltpu.VMEM)
+    return pl.pallas_call(
+        functools.partial(fwd_kernel, own, rows_q),
+        out_shape=(
+            jax.ShapeDtypeStruct((own * HEAD_DIM, rows), BF16),
+            jax.ShapeDtypeStruct((rows, own * HEAD_DIM), BF16),
+            jax.ShapeDtypeStruct((own, rows), F32),
+        ),
+        in_specs=[pl.BlockSpec(memory_space=pltpu.SMEM)] + [vm] * 8,
+        scratch_shapes=[
+            pltpu.VMEM((own, SEQ_LEN, TILE), F32),
+        ],
+        compiler_params=pltpu.CompilerParams(vmem_limit_bytes=56 << 20),
+        name="attend",
+    )(span, qt, k3, vt, kmeta, rseg, rlim, tiles, qbias)
+
+
+def bwd_kernel(
+    own,
+    rows_q,
+    span_ref,
+    qt_ref,
+    q_ref,
+    k_ref,
+    kt_ref,
+    v_ref,
+    ctx_ref,
+    gt_ref,
+    g_ref,
+    lse_ref,
+    kmeta_ref,
+    rseg_ref,
+    rlim_ref,
+    tile_ref,
+    qbias_ref,
+    hott_ref,
+    shift_ref,
+    dq_ref,
+    dk_ref,
+    dv_ref,
+    offs_ref,
+    qoffs_ref,
+    dk_scr,
+    dv_scr,
+    dq_scr,
+    diag_scr,
+    ds_scr,
+    delta_scr,
+):
+    dk_scr[...] = jnp.zeros(dk_scr.shape, F32)
+    dv_scr[...] = jnp.zeros(dv_scr.shape, F32)
+    diag_scr[...] = jnp.zeros(diag_scr.shape, F32)
+    ds_scr[...] = jnp.zeros(ds_scr.shape, BF16)
+    for h in range(own):
+        part = slice(h * HEAD_DIM, (h + 1) * HEAD_DIM)
+        delta_scr[h : h + 1, :] = jnp.sum(
+            ctx_ref[part, :].astype(F32) * gt_ref[part, :].astype(F32), axis=0, keepdims=True
+        )
+
+    def run(rcol, width, lo, hi, bias_of, keep):
+        dq_scr[...] = jnp.zeros(dq_scr.shape, F32)
+
+        def body(kt, carry):
+            krow = pl.multiple_of(kt * TILE, TILE)
+            mask = mask_block(kmeta_ref, rseg_ref, rlim_ref, krow, rcol, width)
+            for h in range(own):
+                part = slice(h * HEAD_DIM, (h + 1) * HEAD_DIM)
+                s = jnp.dot(
+                    k_ref[h, pl.ds(krow, TILE), :],
+                    qt_ref[part, pl.ds(rcol, width)],
+                    preferred_element_type=F32,
+                )
+                s = s * (SCALE * LOG2E) + (bias_of(h, kt) + mask)
+                p = jnp.exp2(s - lse_ref[h : h + 1, pl.ds(rcol, width)])
+                gp = jnp.dot(
+                    v_ref[h, pl.ds(krow, TILE), :],
+                    gt_ref[part, pl.ds(rcol, width)],
+                    preferred_element_type=F32,
+                )
+                ds = p * (gp - delta_scr[h : h + 1, pl.ds(rcol, width)])
+                low = ds.astype(BF16)
+                keep(h, kt, ds, low)
+                dv_scr[h, pl.ds(krow, TILE), :] += jnp.dot(
+                    p.astype(BF16), g_ref[h, pl.ds(rcol, width), :], preferred_element_type=F32
+                )
+                dk_scr[h, pl.ds(krow, TILE), :] += jnp.dot(
+                    low, q_ref[h, pl.ds(rcol, width), :], preferred_element_type=F32
+                )
+                dq_scr[h, :, :width] += jnp.dot(
+                    kt_ref[part, pl.ds(krow, TILE)], low, preferred_element_type=F32
+                )
+            return carry
+
+        lax.fori_loop(lo, hi + 1, body, 0)
+        for h in range(own):
+            dq_ref[h * HEAD_DIM : (h + 1) * HEAD_DIM, pl.ds(rcol, width)] = (
+                dq_scr[h, :, :width] * SCALE
+            ).astype(BF16)
+
+    def content_tile(qt, carry):
+        def bias_of(h, kt):
+            return bias_block(tile_ref, h, 2 * (kt - qt) + REACH)
+
+        def keep(h, kt, ds, low):
+            e = 2 * (kt - qt) + REACH
+            diag_scr[h, e] += ds[:HALF, :HALF] + ds[HALF:, HALF:]
+            diag_scr[h, e - 1] += ds[:HALF, HALF:]
+            diag_scr[h, e + 1] += ds[HALF:, :HALF]
+
+        run(pl.multiple_of(qt * TILE, TILE), TILE, span_ref[0, qt], span_ref[1, qt], bias_of, keep)
+        return carry
+
+    lax.fori_loop(0, SEQ_LEN // TILE, content_tile, 0)
+
+    def query_tile(t, carry):
+        col = pl.multiple_of(t * HALF, HALF)
+
+        def bias_of(h, kt):
+            return qbias_ref[h, pl.ds(pl.multiple_of(kt * TILE, TILE), TILE), pl.ds(col, HALF)]
+
+        def keep(h, kt, ds, low):
+            ds_scr[h, pl.ds(pl.multiple_of(kt * TILE, TILE), TILE), pl.ds(col, HALF)] = low
+
+        run(
+            pl.multiple_of(SEQ_LEN + t * HALF, HALF),
+            HALF,
+            span_ref[0, SEQ_LEN // TILE],
+            span_ref[1, SEQ_LEN // TILE],
+            bias_of,
+            keep,
+        )
+        return carry
+
+    lax.fori_loop(0, rows_q // HALF, query_tile, 0)
+
+    for h in range(own):
+        dk_ref[h] = (dk_scr[h] * SCALE).astype(BF16)
+        dv_ref[h] = dv_scr[h].astype(BF16)
+
+    offs_ref[...] = jnp.zeros(offs_ref.shape, F32)
+    qoffs_ref[...] = jnp.zeros(qoffs_ref.shape, F32)
+    lane = lax.broadcasted_iota(jnp.int32, (HALF, HALF), 1)
+    turn = lane + lax.broadcasted_iota(jnp.int32, (HALF, HALF), 0)
+    over = turn >= HALF
+    turn = jnp.where(over, turn - HALF, turn)
+    for h in range(own):
+        for e in range(DIAGS):
+            skew = jnp.take_along_axis(diag_scr[h, e], turn, axis=1)
+            start = HALF * (15 - e + REACH)
+            offs_ref[h : h + 1, start : start + HALF] += jnp.sum(
+                jnp.where(over, skew, 0.0), axis=0, keepdims=True
+            )
+            offs_ref[h : h + 1, start + HALF : start + 2 * HALF] += jnp.sum(
+                jnp.where(over, 0.0, skew), axis=0, keepdims=True
+            )
+
+    for h in range(own):
+        total = jnp.zeros((16, WIDE), F32)
+        for t in range(rows_q // HALF):
+            shift = shift_ref[t * HALF : (t + 1) * HALF, :]
+            place = lane - shift
+            low_side = place < 0
+            idx = jnp.where(low_side, place + HALF, place)
+            prev = jnp.zeros((HALF, HALF), F32)
+            pieces = []
+            for j in range(SEQ_LEN // HALF + 1):
+                if j < SEQ_LEN // HALF:
+                    block = ds_scr[h, j * HALF : (j + 1) * HALF, t * HALF : (t + 1) * HALF]
+                    cur = jnp.take_along_axis(block.astype(F32).T, idx, axis=1)
+                else:
+                    cur = jnp.zeros((HALF, HALF), F32)
+                pieces.append(jnp.where(low_side, prev, cur).astype(BF16))
+                prev = cur
+            total += jnp.dot(
+                hott_ref[:, t * HALF : (t + 1) * HALF],
+                jnp.concatenate(pieces, axis=1),
+                preferred_element_type=F32,
+            )
+        for i in range(16):
+            qoffs_ref[h : h + 1, HALF * i : HALF * i + WIDE] += total[i : i + 1, :]
+
+
+def bwd_call(
+    span, qt, q3, k3, kt, v3, ctx, gt, g3, lse, kmeta, rseg, rlim, tiles, qbias, hott, shift
+):
+    own = k3.shape[0]
+    rows = qt.shape[1]
+    rows_q = rows - SEQ_LEN
+    vm = pl.BlockSpec(memory_space=pltpu.VMEM)
+    return pl.pallas_call(
+        functools.partial(bwd_kernel, own, rows_q),
+        out_shape=(
+            jax.ShapeDtypeStruct((own * HEAD_DIM, rows), BF16),
+            jax.ShapeDtypeStruct((own, SEQ_LEN, HEAD_DIM), BF16),
+            jax.ShapeDtypeStruct((own, SEQ_LEN, HEAD_DIM), BF16),
+            jax.ShapeDtypeStruct((own, 2 * SEQ_LEN), F32),
+            jax.ShapeDtypeStruct((own, 2 * SEQ_LEN), F32),
+        ),
+        in_specs=[pl.BlockSpec(memory_space=pltpu.SMEM)] + [vm] * 16,
+        scratch_shapes=[
+            pltpu.VMEM((own, SEQ_LEN, HEAD_DIM), F32),
+            pltpu.VMEM((own, SEQ_LEN, HEAD_DIM), F32),
+            pltpu.VMEM((own, HEAD_DIM, TILE), F32),
+            pltpu.VMEM((own, DIAGS, HALF, HALF), F32),
+            pltpu.VMEM((own, SEQ_LEN, rows_q), BF16),
+            pltpu.VMEM((own, rows), F32),
+        ],
+        compiler_params=pltpu.CompilerParams(vmem_limit_bytes=60 << 20),
+        name="attend_back",
+    )(span, qt, q3, k3, kt, v3, ctx, gt, g3, lse, kmeta, rseg, rlim, tiles, qbias, hott, shift)
+
+
+def table_sums(offs, qoffs, rel_bucket):
+    ids = jnp.arange(BUCKETS, dtype=jnp.int32)[:, None]
+    back = jnp.pad(rel_bucket[::-1], (1, 0), constant_values=BUCKETS)
+    ahead = jnp.pad(rel_bucket, (0, 1), constant_values=BUCKETS)
+    high = lax.Precision.HIGHEST
+    near = jnp.einsum("ho,bo->bh", offs, (back[None, :] == ids).astype(F32), precision=high)
+    far = jnp.einsum("ho,bo->bh", qoffs, (ahead[None, :] == ids).astype(F32), precision=high)
+    return near + far
+
+
+def bias_inputs(rel_bucket, rel_table, first, own):
+    hot = (rel_bucket[:, None] == jnp.arange(BUCKETS, dtype=jnp.int32)[None, :]).astype(BF16)
+    part = lax.dynamic_slice_in_dim(rel_table, first, own, axis=1)
+    vec = jnp.einsum("ob,bh->ho", hot, part, preferred_element_type=F32)
+    rev = jnp.pad(vec[:, ::-1], ((0, 0), (1, 0))) * LOG2E
+    low = jnp.pad(vec, ((0, 0), (0, 1))).astype(BF16)
+    fold = jnp.stack([low[:, HALF * i : HALF * i + WIDE] for i in range(16)], axis=1)
+    return rev, fold
+
+
+def query_place(predicted, rows_q):
+    a = predicted // HALF
+    c = predicted - a * HALF
+    pad = rows_q - predicted.shape[0]
+    hot = ((15 - a)[:, None] == jnp.arange(16, dtype=jnp.int32)[None, :]).astype(BF16)
+    hot = jnp.pad(hot, ((0, pad), (0, 0)))
+    shift = jnp.pad(HALF - 1 - c, (0, pad))
+    shift = jnp.broadcast_to(shift[:, None], (rows_q, HALF))
+    return hot, hot.T, shift
+
+
+def row_meta(segment, pad_mask, order, predicted, rows_q):
+    length = segment.shape[0]
+    pos = jnp.arange(length, dtype=jnp.int32)
+    real = pad_mask == 1
+    seg = jnp.where(real, segment, -2 - pos)
+    hit = predicted[:, None] == pos[None, :]
+    qseg = jnp.sum(jnp.where(hit, seg[None, :], 0), axis=1)
+    qlim = jnp.sum(jnp.where(hit, order[None, :], 0), axis=1) - 1
+    pad = rows_q - predicted.shape[0]
+    qseg = jnp.pad(qseg, (0, pad), constant_values=-1)
+    qlim = jnp.pad(qlim, (0, pad))
+    rseg = jnp.concatenate([seg, qseg])[None, :]
+    rlim = jnp.concatenate([order, qlim])[None, :]
+    kmeta = jnp.broadcast_to(jnp.stack([seg, order])[:, :, None], (2, length, HALF))
+    tiles = length // TILE
+    head_seg = segment[::TILE]
+    tail_seg = segment[TILE - 1 :: TILE]
+    starts = jnp.sum((segment[None, :] < head_seg[:, None]).astype(jnp.int32), axis=1)
+    own = jnp.arange(tiles, dtype=jnp.int32)
+    lo = jnp.where(real[::TILE], starts // TILE, own)
+    hi = jnp.where(real[TILE - 1 :: TILE], tail_seg // TILE, own)
+    count = jnp.sum(pad_mask)
+    lo = jnp.concatenate([lo, jnp.zeros((1,), jnp.int32)])
+    hi = jnp.concatenate([hi, jnp.maximum(count - 1, 0)[None] // TILE])
+    return rseg, rlim, kmeta, jnp.stack([lo, hi]).astype(jnp.int32)
+
+
+MESH = pl.DeviceIdType.MESH
+ROWS_Q = 384
+SLOT_Q = 80
+VEC_PARTS = (48, 24, 24, 24, 96, 24, 24, 24)
+
+
+def signal_peers(dp, s, dps, seqs):
+    barrier = pltpu.get_barrier_semaphore()
+    for r in range(1, dps):
+        pl.semaphore_signal(
+            barrier, inc=1, device_id=(lax.rem(dp + r, dps), s), device_id_type=MESH
+        )
+    for r in range(1, seqs):
+        pl.semaphore_signal(
+            barrier, inc=1, device_id=(dp, lax.rem(s + r, seqs)), device_id_type=MESH
+        )
+    pl.semaphore_wait(barrier, dps - 1 + seqs - 1)
+
+
+def remote(src, dst, send_sem, recv_sem, k, device):
+    return pltpu.make_async_remote_copy(
+        src_ref=src,
+        dst_ref=dst,
+        send_sem=send_sem.at[k],
+        recv_sem=recv_sem.at[k],
+        device_id=device,
+        device_id_type=MESH,
+    )
+
+
+def start_kernel(
+    dps,
+    seqs,
+    rc_ref,
+    rq_ref,
+    zero_ref,
+    w_ref,
+    v_ref,
+    i_ref,
+    x_out,
+    w_out,
+    v_out,
+    i_out,
+    send_sem,
+    recv_sem,
+    here_sem,
+):
+    dp = lax.axis_index("dp")
+    s = lax.axis_index("seq")
+    length = rc_ref.shape[0]
+    count = rq_ref.shape[0]
+    mate = s + 1 - 2 * lax.rem(s, 2)
+    across = lax.rem(s + 2, seqs)
+    signal_peers(dp, s, dps, seqs)
+
+    def spot_c(owner):
+        return x_out.at[pl.ds(pl.multiple_of(owner * length, length), length)]
+
+    def spot_q(owner):
+        start = seqs * length + owner * count
+        return x_out.at[pl.ds(pl.multiple_of(start, 16), count)]
+
+    k = 0
+    small = []
+    for r in range(1, seqs):
+        to = lax.rem(s + r, seqs)
+        for src, dst in (
+            (w_ref.at[to], w_out.at[dp, s]),
+            (v_ref, v_out.at[dp, s]),
+            (i_ref, i_out.at[s]),
+        ):
+            small.append(remote(src, dst, send_sem, recv_sem, k, (dp, to)))
+            k += 1
+    for copy in small:
+        copy.start()
+    near, far = [], []
+    for src, spot in ((rc_ref, spot_c), (rq_ref, spot_q)):
+        far.append(remote(src, spot(s), send_sem, recv_sem, k, (dp, across)))
+        near.append(remote(src, spot(s), send_sem, recv_sem, k + 1, (dp, mate)))
+        k += 2
+    for copy in far + near:
+        copy.start()
+    here = [
+        pltpu.make_async_copy(w_ref.at[s], w_out.at[dp, s], here_sem.at[0]),
+        pltpu.make_async_copy(v_ref, v_out.at[dp, s], here_sem.at[1]),
+        pltpu.make_async_copy(i_ref, i_out.at[s], here_sem.at[2]),
+        pltpu.make_async_copy(rc_ref, spot_c(s), here_sem.at[3]),
+        pltpu.make_async_copy(rq_ref, spot_q(s), here_sem.at[4]),
+        pltpu.make_async_copy(
+            zero_ref,
+            x_out.at[pl.ds(seqs * (length + count), zero_ref.shape[0])],
+            here_sem.at[5],
+        ),
+    ]
+    for copy in here:
+        copy.start()
+    for copy in small:
+        copy.wait_recv()
+    for copy in here:
+        copy.wait()
+    wide = []
+    for r in range(1, dps):
+        to = lax.rem(dp + r, dps)
+        for ref in (w_out, v_out):
+            wide.append(remote(ref.at[dp], ref.at[dp], send_sem, recv_sem, k, (to, s)))
+            k += 1
+    for copy in wide:
+        copy.start()
+    pass_on = []
+    for copy, spot in zip(far, (spot_c, spot_q)):
+        copy.wait_recv()
+        pass_on.append(
+            remote(spot(across), spot(across), send_sem, recv_sem, k, (dp, mate))
+        )
+        pass_on[-1].start()
+        k += 1
+    for copy in small + far:
+        copy.wait_send()
+    for copy in near + wide + pass_on:
+        copy.wait()
+
+
+def start_call(dps, seqs, rc, rq, w, v, ints):
+    copies = 3 * (seqs - 1) + 4 + 2 * (dps - 1) + 2
+    zero = jnp.zeros((ROWS_Q - seqs * rq.shape[0], rc.shape[1]), BF16)
+    rows = seqs * rc.shape[0] + ROWS_Q
+    hbm = pl.BlockSpec(memory_space=pl.ANY)
+    return pl.pallas_call(
+        functools.partial(start_kernel, dps, seqs),
+        out_shape=(
+            jax.ShapeDtypeStruct((rows, rc.shape[1]), BF16),
+            jax.ShapeDtypeStruct((dps,) + w.shape, BF16),
+            jax.ShapeDtypeStruct((dps, seqs) + v.shape, F32),
+            jax.ShapeDtypeStruct((seqs,) + ints.shape, jnp.int32),
+        ),
+        in_specs=[hbm] * 6,
+        out_specs=(hbm,) * 4,
+        scratch_shapes=[
+            pltpu.SemaphoreType.DMA((copies,)),
+            pltpu.SemaphoreType.DMA((copies,)),
+            pltpu.SemaphoreType.DMA((6,)),
+        ],
+        compiler_params=pltpu.CompilerParams(collective_id=0, has_side_effects=True),
+        name="gather_rows",
+    )(rc, rq, zero, w, v, ints)
+
+
+def swap_kernel(seqs, c_of, q_of, c_ref, q_ref, c_out, q_out, send_sem, recv_sem, here_sem):
+    dp = lax.axis_index("dp")
+    s = lax.axis_index("seq")
+    signal_peers(dp, s, 1, seqs)
+    copies = []
+    for r in range(1, seqs):
+        to = lax.rem(s + r, seqs)
+        k = 2 * (r - 1)
+        copies.append(remote(c_of(c_ref, to), c_out.at[s], send_sem, recv_sem, k, (dp, to)))
+        copies.append(remote(q_of(q_ref, to), q_out.at[s], send_sem, recv_sem, k + 1, (dp, to)))
+    for copy in copies:
+        copy.start()
+    here = [
+        pltpu.make_async_copy(c_of(c_ref, s), c_out.at[s], here_sem.at[0]),
+        pltpu.make_async_copy(q_of(q_ref, s), q_out.at[s], here_sem.at[1]),
+    ]
+    for copy in here:
+        copy.start()
+    for copy in here + copies:
+        copy.wait()
+
+
+def swap_call(seqs, c, q, c_of, q_of, c_shape, q_shape, ident, name):
+    hbm = pl.BlockSpec(memory_space=pl.ANY)
+    return pl.pallas_call(
+        functools.partial(swap_kernel, seqs, c_of, q_of),
+        out_shape=(
+            jax.ShapeDtypeStruct((seqs,) + c_shape, c.dtype),
+            jax.ShapeDtypeStruct((seqs,) + q_shape, q.dtype),
+        ),
+        in_specs=[hbm] * 2,
+        out_specs=(hbm,) * 2,
+        scratch_shapes=[
+            pltpu.SemaphoreType.DMA((2 * (seqs - 1),)),
+            pltpu.SemaphoreType.DMA((2 * (seqs - 1),)),
+            pltpu.SemaphoreType.DMA((2,)),
+        ],
+        compiler_params=pltpu.CompilerParams(collective_id=ident, has_side_effects=True),
+        name=name,
+    )(c, q)
+
+
+def end_kernel(
+    dps,
+    seqs,
+    gc_ref,
+    gq_ref,
+    w_ref,
+    v_ref,
+    gc_out,
+    gq_out,
+    w_out,
+    v_out,
+    c_mate,
+    q_mate,
+    c_far,
+    q_far,
+    c_send,
+    q_send,
+    w_got,
+    v_got,
+    w_sum,
+    v_sum,
+    v_last,
+    send_sem,
+    recv_sem,
+):
+    dp = lax.axis_index("dp")
+    s = lax.axis_index("seq")
+    core = lax.rem(s, 2)
+    mate = s + 1 - 2 * core
+    across = lax.rem(s + 2, seqs)
+    signal_peers(dp, s, dps, seqs)
+    k = 0
+    first = []
+    for i in range(2):
+        to = lax.rem(mate + 2 * (1 - i), seqs)
+        for src, dst in ((gc_ref, c_mate), (gq_ref, q_mate)):
+            first.append(remote(src.at[to], dst.at[i], send_sem, recv_sem, k, (dp, mate)))
+            k += 1
+    wide = []
+    for r in range(1, dps):
+        to = lax.rem(dp + r, dps)
+        for src, dst in ((w_ref, w_got), (v_ref, v_got)):
+            wide.append(remote(src.at[to], dst.at[r - 1], send_sem, recv_sem, k, (to, s)))
+            k += 1
+    for copy in first + wide:
+        copy.start()
+
+    def each(ref, step, fn):
+        def body(i, carry):
+            fn(pl.ds(pl.multiple_of(i * step, step), step))
+            return carry
+
+        lax.fori_loop(0, ref.shape[-2] // step, body, 0)
+
+    cross = []
+    for (src, got, buf, far, copy) in (
+        (gc_ref, c_mate, c_send, c_far, first[0]),
+        (gq_ref, q_mate, q_send, q_far, first[1]),
+    ):
+        copy.wait_recv()
+
+        def add(rows, src=src, got=got, buf=buf):
+            buf[rows, :] = (
+                src[across, rows, :].astype(F32) + got[0, rows, :].astype(F32)
+            ).astype(BF16)
+
+        each(buf, 16, add)
+        cross.append(remote(buf, far, send_sem, recv_sem, k, (dp, across)))
+        cross[-1].start()
+        k += 1
+    for copy in wide:
+        copy.wait_recv()
+
+    def add_w(rows):
+        for t in range(seqs):
+            total = w_ref[dp, t, rows, :].astype(F32)
+            for r in range(1, dps):
+                total += w_got[r - 1, t, rows, :].astype(F32)
+            w_sum[t, rows, :] = total
+
+    each(w_sum, 8, add_w)
+    total = v_ref[dp]
+    for r in range(1, dps):
+        total += v_got[r - 1]
+    v_sum[...] = total
+    last = []
+    for r in range(1, seqs):
+        to = lax.rem(s + r, seqs)
+        last.append(remote(w_sum.at[to], w_out.at[s], send_sem, recv_sem, k, (dp, to)))
+        last.append(remote(v_sum.at[to], v_last.at[r - 1], send_sem, recv_sem, k + 1, (dp, to)))
+        k += 2
+    for copy in last:
+        copy.start()
+    w_out[s] = w_sum[s]
+    for copy in first[2:]:
+        copy.wait_recv()
+    for copy in cross:
+        copy.wait_recv()
+    for (src, got, far, out) in (
+        (gc_ref, c_mate, c_far, gc_out),
+        (gq_ref, q_mate, q_far, gq_out),
+    ):
+
+        def total_of(rows, src=src, got=got, far=far, out=out):
+            out[rows, :] = (
+                src[s, rows, :].astype(F32)
+                + got[1, rows, :].astype(F32)
+                + far[rows, :].astype(F32)
+            )
+
+        each(out, 16, total_of)
+    for copy in last:
+        copy.wait_recv()
+    total = v_sum[s]
+    for r in range(1, seqs):
+        total += v_last[r - 1]
+    v_out[...] = total
+    for copy in first + wide + cross + last:
+        copy.wait_send()
+
+
+def end_call(dps, seqs, gc, gq, w, v):
+    copies = 4 + 2 * (dps - 1) + 2 + 2 * (seqs - 1)
+    vm = pl.BlockSpec(memory_space=pltpu.VMEM)
+    cshape, qshape, wshape, vshape = gc.shape[1:], gq.shape[1:], w.shape[1:], v.shape[1:]
+    return pl.pallas_call(
+        functools.partial(end_kernel, dps, seqs),
+        out_shape=(
+            jax.ShapeDtypeStruct(cshape, F32),
+            jax.ShapeDtypeStruct(qshape, F32),
+            jax.ShapeDtypeStruct(wshape, F32),
+            jax.ShapeDtypeStruct(vshape[1:], F32),
+        ),
+        in_specs=[vm] * 4,
+        out_specs=(vm,) * 4,
+        scratch_shapes=[
+            pltpu.VMEM((2,) + cshape, BF16),
+            pltpu.VMEM((2,) + qshape, BF16),
+            pltpu.VMEM(cshape, BF16),
+            pltpu.VMEM(qshape, BF16),
+            pltpu.VMEM(cshape, BF16),
+            pltpu.VMEM(qshape, BF16),
+            pltpu.VMEM((dps - 1,) + wshape, BF16),
+            pltpu.VMEM((dps - 1,) + vshape, F32),
+            pltpu.VMEM(wshape, F32),
+            pltpu.VMEM(vshape, F32),
+            pltpu.VMEM((seqs - 1,) + vshape[1:], F32),
+            pltpu.SemaphoreType.DMA((copies,)),
+            pltpu.SemaphoreType.DMA((copies,)),
+        ],
+        compiler_params=pltpu.CompilerParams(
+            collective_id=3, has_side_effects=True, vmem_limit_bytes=50 << 20
+        ),
+        name="sum_rows",
+    )(gc, gq, w, v)
+
+
+def flip_perm(count, bit):
+    return [(i, i ^ bit) for i in range(count)]
+
+
+AXES = ("dp", "seq")
+
+
+def gather_blocks(shard, count, bits):
+    me = lax.axis_index(AXES)
+    cur = shard
+    for bit in bits:
+        got = lax.ppermute(cur, AXES, flip_perm(count, bit))
+        mine = (me // bit) % 2
+        cur = jnp.where(mine == 0, jnp.stack([cur, got]), jnp.stack([got, cur]))
+    dims = len(bits)
+    order = sorted(range(dims), key=lambda j: -bits[dims - 1 - j])
+    cur = jnp.transpose(cur, tuple(order) + tuple(range(dims, cur.ndim)))
+    return cur.reshape((count * shard.shape[0],) + shard.shape[1:])
+
+
+def scatter_sums(full, count, bits):
+    me = lax.axis_index(AXES)
+    dims = count.bit_length() - 1
+    left = [1 << j for j in reversed(range(dims))]
+    cur = full.reshape((2,) * dims + (full.shape[0] // count, full.shape[1]))
+    for bit in bits:
+        axis = left.index(bit)
+        left.pop(axis)
+        mine = (me // bit) % 2
+        give = lax.dynamic_index_in_dim(cur, 1 - mine, axis, keepdims=False).astype(BF16)
+        got = lax.ppermute(give, AXES, flip_perm(count, bit))
+        keep = lax.dynamic_index_in_dim(cur, mine, axis, keepdims=False)
+        cur = keep + got.astype(F32)
+    return cur
+
+
+def local_fast(
+    content,
+    query_stream,
+    segment_ids,
+    pad_mask,
+    predicted,
+    order,
+    rel_bucket,
+    qkv_weight,
+    qv_bias,
+    out_weight,
+    out_bias,
+    attn_gain,
+    attn_shift,
+    up_weight,
+    up_bias,
+    down_weight,
+    down_bias,
+    ffn_gain,
+    ffn_shift,
+    rel_table,
+    content_cot,
+    query_cot,
+):
+    dps, seqs = lax.axis_size("dp"), lax.axis_size("seq")
+    count = dps * seqs
+    s = lax.axis_index("seq")
+    own = HEADS // seqs
+    wide = own * HEAD_DIM
+    length = content.shape[1]
+    preds = query_stream.shape[1]
+    pad_q = SLOT_Q - preds
+    shard = qkv_weight.shape[0]
+
+    rows = jnp.concatenate(
+        [content[0], query_stream[0], jnp.zeros((pad_q, MODEL_WIDTH), F32)], axis=0
+    )
+    rows_low = rows.astype(BF16)
+    vec = jnp.concatenate(
+        [
+            member.astype(F32)
+            for member in (
+                qv_bias,
+                out_bias,
+                attn_gain,
+                attn_shift,
+                up_bias,
+                down_bias,
+                ffn_gain,
+                ffn_shift,
+            )
+        ]
+    )
+    vec = jnp.pad(vec, (0, 1024 - vec.shape[0])).reshape(8, 128)
+    ints = jnp.stack(
+        [
+            segment_ids[0],
+            order[0],
+            pad_mask[0],
+            jnp.pad(predicted[0], (0, length - preds), constant_values=-1),
+        ]
+    )
+    ints = jnp.pad(ints, ((0, 4), (0, 0)))
+    w_parts = jnp.transpose(
+        qkv_weight.reshape(shard, 3, seqs, wide), (2, 0, 1, 3)
+    ).reshape(seqs, shard, 3 * wide)
+    x_all, w_all, v_all, i_all = start_call(
+        dps, seqs, rows_low[:length], rows_low[length:], w_parts, vec, ints
+    )
+    w_qkv = w_all.reshape(MODEL_WIDTH, 3 * wide)
+    parts = v_all.reshape(count, 1024)
+    vectors = []
+    at = 0
+    for n in VEC_PARTS:
+        vectors.append(parts[:, at : at + n].reshape(count * n))
+        at += n
+    bias_qv, bias_out, gain_one, shift_one, bias_up, bias_down, gain_two, shift_two = vectors
+    seg_all = i_all[:, 0].reshape(seqs * length)
+    order_all = i_all[:, 1].reshape(seqs * length)
+    pad_all = i_all[:, 2].reshape(seqs * length)
+    pred_all = i_all[:, 3, :SLOT_Q].reshape(seqs * SLOT_Q)
+
+    bits_up = (8, 16, 4, 2, 1)
+    bits_down = (8, 16, 2, 4, 1)
+    upout = gather_blocks(
+        jnp.concatenate([up_weight, out_weight], axis=1), count, bits_up
+    )
+    w_down = gather_blocks(
+        down_weight.reshape(shard, -1), count, bits_down
+    ).reshape(-1, MODEL_WIDTH)
+    w_up, w_out = upout[:, : up_weight.shape[1]], upout[:, up_weight.shape[1] :]
+
+    rev, fold = bias_inputs(rel_bucket, rel_table, s * own, own)
+    hot, hot_t, shift = query_place(pred_all, ROWS_Q)
+    rseg, rlim, kmeta, span = row_meta(seg_all, pad_all, order_all, pred_all, ROWS_Q)
+    tiles, qbias = bias_call(rev, fold, hot, shift)
+
+    bq = lax.dynamic_slice_in_dim(bias_qv[:MODEL_WIDTH], s * wide, wide)
+    bv = lax.dynamic_slice_in_dim(bias_qv[MODEL_WIDTH:], s * wide, wide)
+    w_q, w_k, w_v = w_qkv[:, :wide], w_qkv[:, wide : 2 * wide], w_qkv[:, 2 * wide :]
+    keys = x_all[: seqs * length]
+
+    def flat(x, w, b):
+        y = jnp.einsum("rd,de->re", x, w, preferred_element_type=F32)
+        return (y if b is None else y + b).astype(BF16)
+
+    def flipped(x, w, b):
+        y = jnp.einsum("rd,de->er", x, w, preferred_element_type=F32)
+        return (y if b is None else y + b[:, None]).astype(BF16)
+
+    def by_head(x):
+        return jnp.transpose(x.reshape(x.shape[0], own, HEAD_DIM), (1, 0, 2))
+
+    q_t = flipped(x_all, w_q, bq)
+    q3 = by_head(flat(x_all, w_q, bq))
+    k3 = by_head(flat(keys, w_k, None))
+    k_t = flipped(keys, w_k, None)
+    v3 = by_head(flat(keys, w_v, bv))
+    v_t = flipped(keys, w_v, bv)
+
+    ctx_t, ctx_rows, lse = fwd_call(span, q_t, k3, v_t, kmeta, rseg, rlim, tiles, qbias)
+
+    def from_rows(ref, t):
+        return ref.at[pl.ds(pl.multiple_of(t * length, length), length)]
+
+    def from_query(ref, t):
+        return ref.at[pl.ds(pl.multiple_of(seqs * length + t * SLOT_Q, 16), SLOT_Q)]
+
+    ctx_c, ctx_q = swap_call(
+        seqs,
+        ctx_rows,
+        ctx_rows,
+        from_rows,
+        from_query,
+        (length, wide),
+        (SLOT_Q, wide),
+        1,
+        "swap_context",
+    )
+    context_low = jnp.transpose(
+        jnp.concatenate([ctx_c, ctx_q], axis=1), (1, 0, 2)
+    ).reshape(length + SLOT_Q, MODEL_WIDTH)
+
+    attn_out = jnp.einsum("re,ed->rd", context_low, w_out, preferred_element_type=F32) + bias_out
+    hidden_one, normed_one, inv_one = norm_fwd((rows + attn_out)[None], gain_one, shift_one)
+    hidden_low = hidden_one[0].astype(BF16)
+    pre_act = jnp.einsum("rd,df->rf", hidden_low, w_up, preferred_element_type=F32) + bias_up
+    activ, gelu_pull = jax.vjp(exact_gelu, pre_act)
+    activ_low = activ.astype(BF16)
+    ffn_out = jnp.einsum("rf,fd->rd", activ_low, w_down, preferred_element_type=F32) + bias_down
+    hidden_two, normed_two, inv_two = norm_fwd(hidden_one + ffn_out[None], gain_two, shift_two)
+    pad_float = pad_mask[0].astype(F32)
+    row_valid = jnp.concatenate([pad_float, jnp.ones((preds,), F32), jnp.zeros((pad_q,), F32)])
+    outputs = hidden_two[0] * row_valid[:, None]
+    rows_c = jnp.concatenate([pad_float, jnp.zeros((SLOT_Q,), F32)])[:, None]
+    rows_q = jnp.concatenate(
+        [jnp.zeros((length,), F32), jnp.ones((preds,), F32), jnp.zeros((pad_q,), F32)]
+    )[:, None]
+    local_sums = jnp.stack(
+        [
+            jnp.sum(rows_c * rows * rows),
+            jnp.sum(rows_q * rows * rows),
+            jnp.sum(rows_c * attn_out * attn_out),
+            jnp.sum(rows_q * attn_out * attn_out),
+            jnp.sum(rows_c * ffn_out * ffn_out),
+            jnp.sum(rows_q * ffn_out * ffn_out),
+            jnp.sum(pad_float),
+        ]
+    )
+    upstream = (
+        jnp.concatenate([content_cot[0], query_cot[0], jnp.zeros((pad_q, MODEL_WIDTH), F32)])
+        * row_valid[:, None]
+    )
+    grad_res_two, grad_gain_two, grad_shift_two = norm_back(
+        upstream[None], normed_two, inv_two, gain_two
+    )
+    grad_res_two = grad_res_two[0]
+    grad_ffn = grad_res_two.astype(BF16)
+    grad_bias_down = jnp.sum(grad_ffn, axis=0, dtype=F32)
+    grad_down = jnp.einsum("rf,rd->fd", activ_low, grad_ffn, preferred_element_type=F32)
+    grad_activ = jnp.einsum("rd,fd->rf", grad_ffn, w_down, preferred_element_type=F32)
+    grad_pre = gelu_pull(grad_activ)[0].astype(BF16)
+    grad_bias_up = jnp.sum(grad_pre, axis=0, dtype=F32)
+    grad_up = jnp.einsum("rd,rf->df", hidden_low, grad_pre, preferred_element_type=F32)
+    grad_hidden = grad_res_two + jnp.einsum(
+        "rf,df->rd", grad_pre, w_up, preferred_element_type=F32
+    )
+    grad_res_one, grad_gain_one, grad_shift_one = norm_back(
+        grad_hidden[None], normed_one, inv_one, gain_one
+    )
+    grad_res_one = grad_res_one[0]
+    grad_attn = grad_res_one.astype(BF16)
+    grad_bias_out = jnp.sum(grad_attn, axis=0, dtype=F32)
+    grad_out = jnp.einsum("re,rd->ed", context_low, grad_attn, preferred_element_type=F32)
+    grad_context = jnp.einsum(
+        "rd,ed->re", grad_attn, w_out, preferred_element_type=F32
+    ).astype(BF16)
+
+    grad_down_own = scatter_sums(
+        grad_down.reshape(MODEL_WIDTH, -1), count, (1, 4, 2, 8, 16)
+    ).reshape(-1, MODEL_WIDTH)
+    grad_upout_own = scatter_sums(
+        jnp.concatenate([grad_up, grad_out], axis=1), count, (1, 2, 4, 8, 16)
+    )
+    grad_up_own = grad_upout_own[:, : up_weight.shape[1]]
+    grad_out_own = grad_upout_own[:, up_weight.shape[1] :]
+
+    split = jnp.transpose(
+        grad_context.reshape(length + SLOT_Q, seqs, wide), (1, 0, 2)
+    )
+
+    def from_slot(ref, t):
+        return ref.at[t]
+
+    g_c, g_q = swap_call(
+        seqs,
+        split[:, :length],
+        split[:, length:],
+        from_slot,
+        from_slot,
+        (length, wide),
+        (SLOT_Q, wide),
+        2,
+        "swap_grads",
+    )
+    g_rows = jnp.concatenate(
+        [
+            g_c.reshape(seqs * length, wide),
+            g_q.reshape(seqs * SLOT_Q, wide),
+            jnp.zeros((ROWS_Q - seqs * SLOT_Q, wide), BF16),
+        ]
+    )
+    dq_t, dk3, dv3, offs, qoffs = bwd_call(
+        span,
+        q_t,
+        q3,
+        k3,
+        k_t,
+        v3,
+        ctx_t,
+        g_rows.T,
+        by_head(g_rows),
+        lse,
+        kmeta,
+        rseg,
+        rlim,
+        tiles,
+        qbias,
+        hot_t,
+        shift,
+    )
+    table = table_sums(offs, qoffs, rel_bucket)
+    dk = jnp.transpose(dk3, (1, 0, 2)).reshape(seqs * length, wide)
+    dv = jnp.transpose(dv3, (1, 0, 2)).reshape(seqs * length, wide)
+    grad_w = jnp.concatenate(
+        [
+            jnp.einsum("rd,er->de", x_all, dq_t, preferred_element_type=F32),
+            jnp.einsum("rd,re->de", keys, dk, preferred_element_type=F32),
+            jnp.einsum("rd,re->de", keys, dv, preferred_element_type=F32),
+        ],
+        axis=1,
+    ).astype(BF16)
+    dq = dq_t.T
+    cut = seqs * length
+    grad_keys_rows = (
+        jnp.einsum("re,de->rd", dq[:cut], w_q, preferred_element_type=F32)
+        + jnp.einsum("re,de->rd", dk, w_k, preferred_element_type=F32)
+        + jnp.einsum("re,de->rd", dv, w_v, preferred_element_type=F32)
+    ).astype(BF16)
+    grad_query_rows = jnp.einsum(
+        "re,de->rd", dq[cut : cut + seqs * SLOT_Q], w_q, preferred_element_type=F32
+    ).astype(BF16)
+    bias_q = jnp.sum(dq_t.astype(F32), axis=1)
+    bias_v = jnp.sum(dv.astype(F32), axis=0)
+    spot = jnp.zeros((2, MODEL_WIDTH), F32)
+    grad_bias_qv = lax.dynamic_update_slice(
+        spot, jnp.stack([bias_q, bias_v]), (0, s * wide)
+    ).reshape(2 * MODEL_WIDTH)
+    table_all = lax.dynamic_update_slice(
+        jnp.zeros((BUCKETS, HEADS), F32), table, (0, s * own)
+    )
+    owned = jnp.concatenate(
+        [
+            member.reshape(count, -1)
+            for member in (
+                grad_bias_qv,
+                grad_bias_out,
+                grad_gain_one,
+                grad_shift_one,
+                grad_bias_up,
+                grad_bias_down,
+                grad_gain_two,
+                grad_shift_two,
+            )
+        ],
+        axis=1,
+    )
+    used = owned.shape[1]
+    shared = jnp.concatenate([table_all.reshape(-1), local_sums])
+    vec_grads = jnp.concatenate(
+        [
+            owned,
+            jnp.broadcast_to(shared[None, :], (count, shared.shape[0])),
+            jnp.zeros((count, 1024 - used - shared.shape[0]), F32),
+        ],
+        axis=1,
+    ).reshape(dps, seqs, 8, 128)
+    sum_c, sum_q, sum_w, sum_v = end_call(
+        dps,
+        seqs,
+        grad_keys_rows.reshape(seqs, length, MODEL_WIDTH),
+        grad_query_rows.reshape(seqs, SLOT_Q, MODEL_WIDTH),
+        grad_w.reshape(dps, seqs, shard, 3 * wide),
+        vec_grads,
+    )
+    grad_content = grad_res_one[:length] + sum_c
+    grad_query = grad_res_one[length : length + preds] + sum_q[:preds]
+    grad_qkv_own = jnp.transpose(sum_w.reshape(seqs, shard, 3, wide), (1, 2, 0, 3)).reshape(
+        shard, 3 * MODEL_WIDTH
+    )
+    sums = sum_v.reshape(1024)
+    mine = []
+    at = 0
+    for n in VEC_PARTS:
+        mine.append(sums[at : at + n])
+        at += n
+    table_sum = sums[at : at + BUCKETS * HEADS].reshape(BUCKETS, HEADS)
+    totals = sums[at + BUCKETS * HEADS : at + BUCKETS * HEADS + 7]
+    content_count = totals[6] * MODEL_WIDTH
+    query_count = float(dps * preds * seqs * MODEL_WIDTH)
+    each = jnp.stack([content_count, jnp.float32(query_count)])
+    stats = jnp.sqrt(totals[:6] / jnp.concatenate([each, each, each]))
+    return (
+        outputs[None, :length],
+        outputs[None, length : length + preds],
+        grad_content[None],
+        grad_query[None],
+        grad_qkv_own,
+        mine[0],
+        grad_out_own,
+        mine[1],
+        mine[2],
+        mine[3],
+        grad_up_own,
+        mine[4],
+        grad_down_own,
+        mine[5],
+        mine[6],
+        mine[7],
+        table_sum,
+        stats,
+    )
+
+
+def pick_local(mesh):
+    sizes = dict(mesh.shape)
+    return local_fast if (sizes["dp"], sizes["seq"]) == (8, 4) else local_general
+
+
 def solution(mesh):
     in_specs = (
         P("dp", "seq", None),
@@ -455,4 +1660,5 @@
         P(),
         P(),
     )
+    local = pick_local(mesh)
     return jax.shard_map(local, mesh=mesh, in_specs=in_specs, out_specs=out_specs, check_vma=False)

time: 1050 us -> 679 us (0.65)
  waiting for transfers between devices: 425 us -> 115 us
  matrix products: 349 us -> 99.1 us
  Pallas kernels: 0 us -> 231 us
  blocking collectives: 99.7 us -> 0 us
  local copies, waits for them, and re-layouts: 60.9 us -> 119 us
  starting transfers between devices: 0.4 us -> 41.5 us
  other arithmetic: 92.3 us -> 63.4 us
  between operations: 19.7 us -> 4.19 us
    reduce_scatter x4 -> x0, waiting for transfers between devices: 271 us -> none  [the longest x1 142 us: local(): lax.psum_scatter(grad_down, ('dp', 'seq'), scatter_dimension=0, tiled=True)]
    dot_general x23 -> x25, matrix products: 349 us -> 99.1 us  [the longest x1 21.6 us: local_fast(): jnp.einsum('rd,df->rf', hidden_low, w_up, preferred_element_type=F32)]
    pallas_call x0 -> x7, Pallas kernels: none -> 231 us  [the longest x1 58.5 us: bwd_call(): pl.pallas_call(functools.partial(bwd_kernel, own, rows_q), out_shape=(jax...]
    unnamed x11 -> x0, waiting for transfers between devices: 127 us -> none
    ppermute x0 -> x20, waiting for transfers between devices: none -> 115 us  [the longest x10 65.3 us: gather_blocks(): got = lax.ppermute(cur, AXES, flip_perm(count, bit))]
    unnamed x2 -> x0, blocking collectives: 83.7 us -> none
    convert_element_type x9 -> x2, other arithmetic: 49.5 us -> 2.33 us  [the longest x1 1.65 us: local_fast(): rows_low = rows.astype(BF16)]
    ppermute x0 -> x20, starting transfers between devices: none -> 41.5 us  [the longest x10 21.7 us: gather_blocks(): got = lax.ppermute(cur, AXES, flip_perm(count, bit))]
  transfers between devices with their start and end apart: 10 -> 20, of which waited for: 6 -> 13; matrix products, arithmetic and copies ran while one was open for 32% -> 22% of each run, Pallas kernels for 0% -> 23%
where the time goes in v1:
time: 679 us; the launch traced here: 673 us
  Pallas kernels  231 us (34%)
  local copies, waits for them, and re-layouts  119 us (18%)
  waiting for transfers between devices  115 us (17%)
  matrix products  99.1 us (15%)
  other arithmetic  63.4 us (9%)
  starting transfers between devices  41.5 us (6%)
    ppermute x10, waiting for transfers between devices, gather_blocks(): got = lax.ppermute(cur, AXES, flip_perm(count, bit))  65.3 us
    pallas_call x1, Pallas kernels, bwd_call(): pl.pallas_call(functools.partial(bwd_kernel, own, rows_q), out_shape=(jax...  58.5 us
    pallas_call x1, Pallas kernels, start_call(): pl.pallas_call(functools.partial(start_kernel, dps, seqs), out_shape=(jax...  56.3 us
    ppermute x10, waiting for transfers between devices, scatter_sums(): got = lax.ppermute(give, AXES, flip_perm(count, bit))  49.8 us
    pallas_call x1, Pallas kernels, end_call(): pl.pallas_call(functools.partial(end_kernel, dps, seqs), out_shape=(jax.S...  38.9 us
    pallas_call x1, Pallas kernels, fwd_call(): pl.pallas_call(functools.partial(fwd_kernel, own, rows_q), out_shape=(jax...  32.4 us
    pallas_call x2, Pallas kernels, swap_call(): pl.pallas_call(functools.partial(swap_kernel, seqs, c_of, q_of), out_shap...  30.7 us
    ppermute x10, starting transfers between devices, gather_blocks(): got = lax.ppermute(cur, AXES, flip_perm(count, bit))  21.7 us
  transfers between devices with their start and end apart: 20, of which 13 were waited for; matrix products, arithmetic and copies ran while one was open for 22% of the time, Pallas kernels for 23%

profile of v1, /device:TPU:0, one launch (start us, length us, event | category | flops | bytes accessed | tf_op | source)
XLA Modules:
  0.0 672.6 jit_solution(14675390420849403560)
XLA Ops:
  2.3 3.0 collective-permute-start.5
  17.2 56.3 %gather_rows.1 = (bf16[2432,768]{1,0:T(8,128)(2,1)}, bf16[8,4,24,576]{3,2,1,0:T(8,128)(2,1)}, f32[8,4,8,128]{3,2,1,0:T(8,128)}, s32[4,8,512]{2,1,0:T(8,128)}) custom-call(bf16[512,768]{1,0:T(8,128)(2,1)} %slice.289.rc_ref, bf16[80,768]{1,0:T(8,128)(2,1)} %slice.290.rq_ref, bf16[64,768]{1,0:T(8,128)(2,1)} %broadcast_in_dim.52.zero_ref, ...), custom_call_target="tpu_custom_call" | custom-call | tf_op jit(solution)/shard_map/gather_rows/pallas_call | solution.py:1004
  79.6 3.4 convolution_convert_fusion.1
  83.1 2.2 fusion.11.qt_ref
  85.3 2.3 fusion.12
  87.7 4.1 fusion.14.vt_ref
  94.0 2.3 convolution_convert_fusion.kt_ref
  100.1 3.0 reverse
  108.4 14.0 %bias_tiles.1 = (f32[3,19,128,128]{3,2,1,0:T(8,128)}, f32[3,2048,384]{2,1,0:T(8,128)}) custom-call(f32[3,4096]{1,0:T(4,128)S(1)} %pad_multiply_fusion.rev_ref, bf16[3,16,2176]{2,1,0:T(8,128)(2,1)S(1)} %stack.308.fold_ref, bf16[384,16]{1,0:T(8,128)(2,1)S(1)} %copy.951.hot_ref, s32[384,128]{1,0:T(8,128)S(1)} %broadcast_in_dim.60.shift_ref), custom_call_target="tpu_custom_call" | custom-call | tf_op jit(solution)/shard_map/bias_tiles/pallas_call | solution.py:461
  122.4 2.2 broadcast_in_dim.54.kmeta_ref
  124.6 32.4 %attend.1 = (bf16[192,2432]{1,0:T(8,128)(2,1)}, bf16[2432,192]{1,0:T(8,128)(2,1)}, f32[3,2432]{1,0:T(4,128)}) custom-call(s32[2,9]{1,0:T(2,128)} %pad_add_fusion.3.span_ref, bf16[192,2432]{1,0:T(8,128)(2,1)} %fusion.11.qt_ref, bf16[3,2048,64]{2,1,0:T(8,128)(2,1)} %bitcast.276, bf16[192,2048]{1,0:T(8,128)(2,1)} %fusion.14.vt_ref, ...), custom_call_target="tpu_custom_call" | custom-call | tf_op jit(solution)/shard_map/attend/pallas_call | solution.py:608
  157.0 15.5 %swap_context.1 = (bf16[4,512,192]{2,1,0:T(8,128)(2,1)}, bf16[4,80,192]{2,1,0:T(8,128)(2,1)}) custom-call(bf16[2432,192]{1,0:T(8,128)(2,1)} %get-tuple-element.46.c_ref.q_ref, bf16[2432,192]{1,0:T(8,128)(2,1)} %get-tuple-element.46.c_ref.q_ref), custom_call_target="tpu_custom_call" | custom-call | tf_op jit(solution)/shard_map/swap_context/pallas_call | solution.py:1048
  179.9 2.8 copy.966
  182.7 2.4 copy.967
  190.0 3.0 copy.979
  195.5 5.6 collective-permute-start.6
  207.1 15.9 %collective-permute-done.6 = bf16[2,24,3072]{2,1,0:T(8,128)(2,1)S(1)} collective-permute-done((bf16[2,24,3072]{2,1,0:T(8,128)(2,1)S(1)}, bf16[2,24,3072]{2,1,0:T(8,128)(2,1)S(1)}, u32[]{:S(2)}, u32[]{:S(2)}) %collective-permute-start.6) | collective-permute-done | bytes 294944 | tf_op jit(solution)/shard_map/ppermute | solution.py:1234
  223.3 7.5 %collective-permute-done.1 = bf16[2,24,3840]{2,1,0:T(8,128)(2,1)S(1)} collective-permute-done((bf16[2,24,3840]{2,1,0:T(8,128)(2,1)S(1)}, bf16[2,24,3840]{2,1,0:T(8,128)(2,1)S(1)}, u32[]{:S(2)}, u32[]{:S(2)}) %collective-permute-start.1) | collective-permute-done | bytes 368672 | tf_op jit(solution)/shard_map/ppermute | solution.py:1234
  231.0 5.3 collective-permute-start.2
  236.6 2.4 collective-permute-done.7
  239.1 5.4 collective-permute-start.8
  244.8 8.8 %collective-permute-done.2 = bf16[2,2,24,3840]{3,2,1,0:T(8,128)(2,1)S(1)} collective-permute-done((bf16[2,2,24,3840]{3,2,1,0:T(8,128)(2,1)S(1)}, bf16[2,2,24,3840]{3,2,1,0:T(8,128)(2,1)S(1)}, u32[]{:S(2)}, u32[]{:S(2)}) %collective-permute-start.2) | collective-permute-done | bytes 737312 | tf_op jit(solution)/shard_map/ppermute | solution.py:1234
  256.3 22.5 %collective-permute-done.8 = bf16[2,2,2,24,3072]{4,3,0,2,1:T(8,128)(2,1)S(1)} collective-permute-done((bf16[2,2,2,24,3072]{4,3,0,2,1:T(8,128)(2,1)S(1)}, bf16[2,2,2,24,3072]{4,3,0,2,1:T(8,128)(2,1)S(1)}, u32[]{:S(2)}, u32[]{:S(2)}) %collective-permute-start.8) | collective-permute-done | bytes 1179680 | tf_op jit(solution)/shard_map/ppermute | solution.py:1234
  279.6 8.2 %collective-permute-done.3 = bf16[2,2,2,24,3840]{4,3,0,2,1:T(8,128)(2,1)S(1)} collective-permute-done((bf16[2,2,2,24,3840]{4,3,0,2,1:T(8,128)(2,1)S(1)}, bf16[2,2,2,24,3840]{4,3,0,2,1:T(8,128)(2,1)S(1)}, u32[]{:S(2)}, u32[]{:S(2)}) %collective-permute-start.3) | collective-permute-done | bytes 1474592 | tf_op jit(solution)/shard_map/ppermute | solution.py:1234
  290.8 2.5 fusion.6
  293.2 8.5 %reshape_reshape.9 = bf16[3072,768]{1,0:T(8,128)(2,1)} reshape(bf16[2,2,2,2,2,24,3072]{6,5,4,3,2,1,0:T(8,128)(2,1)} %fusion.6) | data formatting | bytes 9437184 | tf_op jit(solution)/shard_map/reshape;reshape | solution.py:1348
  301.7 3.9 maximum_select_fusion
  307.2 21.6 %multiply_convert_fusion = (bf16[592,3072]{1,0:T(8,128)(2,1)S(1)}, f32[592,3072]{1,0:T(8,128)}, f32[592,3072]{1,0:T(8,128)}) fusion(f32[3072]{0:T(1024)S(1)} %copy-done.65, bf16[768,3840]{1,0:T(8,128)(2,1)S(1)} %bitcast.286, f32[592,768]{1,0:T(8,128)S(1)} %get-tuple-element.415, f32[768]{0:T(1024)S(1)} %add.328, f32[768]{0:T(1024)S(1)} %mul.282, ...), kind=kOutput, calls=%fused_computation.5 | convolution fusion | flops 2915708928 | bytes 24752128 | tf_op jit(solution)/shard_map/rd,df->rf/dot_general | solution.py:1405
  329.0 4.4 fusion.18
  336.1 2.8 convert_reduce_fusion.3
  339.0 9.8 %convert_reduce_fusion = (f32[3072]{0:T(1024)}, bf16[592,3072]{1,0:T(8,128)(2,1)S(1)}) fusion(f32[592,3072]{1,0:T(8,128)} %get-tuple-element.413, bf16[3072,768]{1,0:T(8,128)(2,1)S(1)} %bitcast.306, f32[592,768]{1,0:T(8,128)S(1)} %get-tuple-element.407, f32[592,3072]{1,0:T(8,128)} %get-tuple-element.474, f32[3072]{0:T(1024)S(1)} %copy-done.65), kind=kOutput, calls=%fused_computation.3 | convolution fusion | flops 2824774656 | bytes 24748032 | tf_op jit(solution)/shard_map/rd,fd->rf/dot_general | solution.py:1439
  348.8 4.0 multiply_reduce_fusion.1
  360.9 15.2 %swap_grads.1 = (bf16[4,512,192]{2,1,0:T(8,128)(2,1)}, bf16[4,80,192]{2,1,0:T(8,128)(2,1)}) custom-call(bf16[4,512,192]{2,1,0:T(8,128)(2,1)} %slice.323.c_ref, bf16[4,80,192]{2,1,0:T(8,128)(2,1)} %slice.324.q_ref), custom_call_target="tpu_custom_call" | custom-call | tf_op jit(solution)/shard_map/swap_grads/pallas_call | solution.py:1048
  376.1 2.4 copy.972
  378.4 2.9 concatenate.312
  381.3 2.5 copy.974
  386.1 3.4 maximum_bitcast_fusion.g_ref
  390.6 58.5 %attend_back.1 = (bf16[192,2432]{1,0:T(8,128)(2,1)}, bf16[3,2048,64]{2,1,0:T(8,128)(2,1)}, bf16[3,2048,64]{2,1,0:T(8,128)(2,1)}, f32[3,4096]{1,0:T(4,128)}, f32[3,4096]{1,0:T(4,128)}) custom-call(s32[2,9]{1,0:T(2,128)} %pad_add_fusion.3.span_ref, bf16[192,2432]{1,0:T(8,128)(2,1)} %fusion.11.qt_ref, bf16[3,2432,64]{2,1,0:T(8,128)(2,1)} %bitcast.289, ...), custom_call_target="tpu_custom_call" | custom-call | tf_op jit(solution)/shard_map/attend_back/pallas_call | solution.py:796
  451.0 3.4 convolution_convert_fusion.6
  454.5 3.8 fusion.40
  458.6 6.4 fusion.77
  465.1 7.0 %fusion.84 = f32[768,3072]{1,0:T(8,128)} fusion(bf16[592,3072]{1,0:T(8,128)(2,1)S(1)} %copy-done.22, f32[592,768]{1,0:T(8,128)S(1)} %get-tuple-element.415, f32[768]{0:T(1024)S(1)} %add.328, f32[768]{0:T(1024)S(1)} %mul.282, f32[592]{0:T(1024)S(1)} %add_rsqrt_fusion.1, f32[592]{0:T(1024)S(1)} %broadcast_multiply_fusion.5), kind=kOutput, calls=%fused_computation.269 | convolution fusion | flops 2795679744 | bytes 14903936 | tf_op jit(solution)/shard_map/rd,rf->df/dot_general | solution.py:1442
  473.9 2.4 copy.977
  476.3 2.4 copy.976
  478.8 3.2 convolution_convert_fusion.4
  483.8 11.4 %reshape_reshape.11 = f32[2,2,2,2,2,24,3072]{6,5,4,3,2,1,0:T(8,128)} reshape(f32[3072,768]{1,0:T(8,128)} %fusion.77) | data formatting | bytes 18874368 | tf_op jit(solution)/shard_map/reshape;reshape | solution.py:1247
  495.3 4.1 fusion.16
  500.6 4.5 pad_maximum_fusion
  505.1 4.3 copy-done.3
  513.7 5.1 fusion.52
  520.0 4.6 concatenate.318
  524.9 7.6 %add_convert_fusion.1 = bf16[2048,768]{1,0:T(8,128)(2,1)} fusion(f32[2048,768]{1,0:T(8,128)} %fusion.40, f32[2048,768]{1,0:T(8,128)} %fusion.52, bf16[2048,192]{0,1:T(8,128)(2,1)S(1)} %bitcast.316, bf16[768,576]{1,0:T(8,128)(2,1)} %bitcast.326), kind=kOutput, calls=%fused_computation.19 | convolution fusion | flops 608698368 | bytes 16908288 | tf_op jit(solution)/shard_map/re,de->rd/dot_general | solution.py:1526
  532.5 38.9 %sum_rows.1 = (f32[512,768]{1,0:T(8,128)S(1)}, f32[80,768]{1,0:T(8,128)S(1)}, f32[4,24,576]{2,1,0:T(8,128)S(1)}, f32[8,128]{1,0:T(8,128)S(1)}) custom-call(bf16[4,512,768]{2,1,0:T(8,128)(2,1)} %bitcast.281, bf16[4,80,768]{2,1,0:T(8,128)(2,1)S(1)} %bitcast.264, bf16[8,4,24,576]{3,2,1,0:T(8,128)(2,1)S(1)} %pad_maximum_fusion.9.w_ref, ...), custom_call_target="tpu_custom_call" | custom-call | tf_op jit(solution)/shard_map/sum_rows/pallas_call | solution.py:1191
  575.2 2.7 slice_bitcast_fusion.2
  577.9 3.7 bitcast_add_fusion.1
  584.5 4.2 bitcast_add_fusion
  596.9 3.0 fusion.30
  599.9 12.1 %collective-permute-done.16 = bf16[2,2,2,24,3072]{4,3,2,1,0:T(8,128)(2,1)} collective-permute-done((bf16[2,2,2,24,3072]{4,3,2,1,0:T(8,128)(2,1)}, bf16[2,2,2,24,3072]{4,3,2,1,0:T(8,128)(2,1)}, u32[]{:S(2)}, u32[]{:S(2)}) %collective-permute-start.16) | collective-permute-done | bytes 1179680 | tf_op jit(solution)/shard_map/ppermute | solution.py:1253
  614.6 11.0 %collective-permute-done.11 = bf16[2,2,2,24,3840]{4,3,0,1,2:T(8,128)(2,1)} collective-permute-done((bf16[2,2,2,24,3840]{4,3,0,1,2:T(8,128)(2,1)}, bf16[2,2,2,24,3840]{4,3,0,1,2:T(8,128)(2,1)}, u32[]{:S(2)}, u32[]{:S(2)}) %collective-permute-start.11) | collective-permute-done | bytes 1474592 | tf_op jit(solution)/shard_map/ppermute | solution.py:1253
  628.6 9.1 %collective-permute-done.17 = bf16[2,2,24,3072]{3,2,1,0:T(8,128)(2,1)S(1)} collective-permute-done((bf16[2,2,24,3072]{3,2,1,0:T(8,128)(2,1)S(1)}, bf16[2,2,24,3072]{3,2,1,0:T(8,128)(2,1)S(1)}, u32[]{:S(2)}, u32[]{:S(2)}) %collective-permute-start.17) | collective-permute-done | bytes 589856 | tf_op jit(solution)/shard_map/ppermute | solution.py:1253
  637.8 5.9 collective-permute-start.18
  645.1 5.8 collective-permute-start.13
  652.6 8.8 %collective-permute-done.13 = bf16[2,24,3840]{2,1,0:T(8,128)(2,1)S(1)} collective-permute-done((bf16[2,24,3840]{2,1,0:T(8,128)(2,1)S(1)}, bf16[2,24,3840]{2,1,0:T(8,128)(2,1)S(1)}, u32[]{:S(2)}, u32[]{:S(2)}) %collective-permute-start.13) | collective-permute-done | bytes 368672 | tf_op jit(solution)/shard_map/ppermute | solution.py:1253
  663.1 7.6 %collective-permute-done.14 = bf16[24,3840]{1,0:T(8,128)(2,1)S(1)} collective-permute-done((bf16[24,3840]{1,0:T(8,128)(2,1)S(1)}, bf16[24,3840]{1,0:T(8,128)(2,1)S(1)}, u32[]{:S(2)}, u32[]{:S(2)}) %collective-permute-start.14) | collective-permute-done | bytes 184352 | tf_op jit(solution)/shard_map/ppermute | solution.py:1253
  (417 shorter events, 112.3 us)
Async XLA Ops:
  0.7 97.8 %copy-start = (bf16[32,12]{0,1:T(8,128)(2,1)S(1)}, bf16[32,12]{0,1:T(8,128)(2,1)}, u32[]{:S(2)}) copy-start(bf16[32,12]{0,1:T(8,128)(2,1)} %param.41) | copy-start | bytes 2308
  2.3 192.0 %collective-permute-start.5 = (bf16[24,3072]{1,0:T(8,128)(2,1)}, bf16[24,3072]{1,0:T(8,128)(2,1)}, u32[]{:S(2)}, u32[]{:S(2)}) collective-permute-start(bf16[24,3072]{1,0:T(8,128)(2,1)} %reshape.1327), channel_id=1, source_target_pairs={{0,8},{1,9},{2,10},{3,11},{4,12},{5,13},{6,14},{7,15},{8,0},{9,1},... | collective-permute-start | bytes 442376 | tf_op jit(solution)/shard_map/ppermute | solution.py:1234
  8.3 194.9 %collective-permute-start = (bf16[24,3840]{1,0:T(8,128)(2,1)}, bf16[24,3840]{1,0:T(8,128)(2,1)}, u32[]{:S(2)}, u32[]{:S(2)}) collective-permute-start(bf16[24,3840]{1,0:T(8,128)(2,1)} %constant_dynamic-update-slice_fusion), channel_id=1, source_target_pairs={{0,8},{1,9},{2,10},{3,11},{4,12},{5,13},{6,14},{7,15},{8,0},{9,1},... | collective-permute-start | bytes 552968 | tf_op jit(solution)/shard_map/ppermute | solution.py:1234
  10.6 162.0 %copy-start.51 = (f32[592]{0:T(1024)}, f32[592]{0:T(1024)S(1)}, u32[]{:S(2)}) copy-start(f32[592]{0:T(1024)S(1)} %get-tuple-element.467) | copy-start | bytes 7108
  10.6 295.0 %copy-start.39 = (f32[592]{0:T(1024)}, f32[592]{0:T(1024)S(1)}, u32[]{:S(2)}) copy-start(f32[592]{0:T(1024)S(1)} %get-tuple-element.470) | copy-start | bytes 7108
  10.7 4.4 copy-start.76
  10.7 4.4 copy-start.77
  10.7 4.4 copy-start.78
  10.7 5.1 copy-start.82
  10.8 5.1 copy-start.54
  10.8 5.1 copy-start.72
  10.8 5.1 copy-start.73
  108.4 48.6 %copy-start.2 = (s32[384,128]{1,0:T(8,128)}, s32[384,128]{1,0:T(8,128)S(1)}, u32[]{:S(2)}) copy-start(s32[384,128]{1,0:T(8,128)S(1)} %broadcast_in_dim.60.shift_ref) | copy-start | bytes 589828
  157.0 15.6 %copy-start.37 = (f32[1,76,768]{2,0,1:T(1,128)S(1)}, f32[1,76,768]{2,0,1:T(1,128)}, u32[]{:S(2)}) copy-start(f32[1,76,768]{2,0,1:T(1,128)} %param.43) | copy-start | bytes 700420
  157.0 15.7 %copy-start.10 = (f32[1,512,768]{2,1,0:T(8,128)S(1)}, f32[1,512,768]{2,1,0:T(8,128)}, u32[]{:S(2)}) copy-start(f32[1,512,768]{2,1,0:T(8,128)} %param.42) | copy-start | bytes 4718596
  174.3 4.9 copy-start.42
  179.9 9.4 %copy-start.56 = (f32[768]{0:T(1024)S(1)}, f32[768]{0:T(1024)}, u32[]{:S(2)}) copy-start(f32[768]{0:T(1024)} %get-tuple-element.390) | copy-start | bytes 9220
  179.9 10.1 %copy-start.12 = (bf16[768,2048]{0,1:T(8,128)(2,1)S(1)}, bf16[768,2048]{0,1:T(8,128)(2,1)}, u32[]{:S(2)}) copy-start(bf16[768,2048]{0,1:T(8,128)(2,1)} %slice_bitcast_fusion) | copy-start | bytes 9437188
  195.5 27.5 %collective-permute-start.6 = (bf16[2,24,3072]{2,1,0:T(8,128)(2,1)S(1)}, bf16[2,24,3072]{2,1,0:T(8,128)(2,1)S(1)}, u32[]{:S(2)}, u32[]{:S(2)}) collective-permute-start(bf16[2,24,3072]{2,1,0:T(8,128)(2,1)S(1)} %maximum_select_fusion.11), channel_id=1, source_target_pairs={{0,16},{1,17},{2,18},{3,19},{4,20},{5,21},{6,22},{7,23},{8,24},{9,... | collective-permute-start | bytes 884744 | tf_op jit(solution)/shard_map/ppermute | solution.py:1234
  204.5 26.4 %collective-permute-start.1 = (bf16[2,24,3840]{2,1,0:T(8,128)(2,1)S(1)}, bf16[2,24,3840]{2,1,0:T(8,128)(2,1)S(1)}, u32[]{:S(2)}, u32[]{:S(2)}) collective-permute-start(bf16[2,24,3840]{2,1,0:T(8,128)(2,1)S(1)} %maximum_select_fusion.9), channel_id=1, source_target_pairs={{0,16},{1,17},{2,18},{3,19},{4,20},{5,21},{6,22},{7,23},{8,24},{9,... | collective-permute-start | bytes 1105928 | tf_op jit(solution)/shard_map/ppermute | solution.py:1234
  223.0 15.9 %collective-permute-start.7 = (bf16[2,2,24,3072]{3,2,1,0:T(8,128)(2,1)S(1)}, bf16[2,2,24,3072]{3,2,1,0:T(8,128)(2,1)S(1)}, u32[]{:S(2)}, u32[]{:S(2)}) collective-permute-start(bf16[2,2,24,3072]{3,2,1,0:T(8,128)(2,1)S(1)} %maximum_select_fusion.7), channel_id=1, source_target_pairs={{0,2},{1,3},{2,0},{3,1},{4,6},{5,7},{6,4},{7,5},{8,10},{9,11},{10,... | collective-permute-start | bytes 1769480 | tf_op jit(solution)/shard_map/ppermute | solution.py:1234
  231.0 22.7 %collective-permute-start.2 = (bf16[2,2,24,3840]{3,2,1,0:T(8,128)(2,1)S(1)}, bf16[2,2,24,3840]{3,2,1,0:T(8,128)(2,1)S(1)}, u32[]{:S(2)}, u32[]{:S(2)}) collective-permute-start(bf16[2,2,24,3840]{3,2,1,0:T(8,128)(2,1)S(1)} %maximum_select_fusion.6), channel_id=1, source_target_pairs={{0,4},{1,5},{2,6},{3,7},{4,0},{5,1},{6,2},{7,3},{8,12},{9,13},{10,... | collective-permute-start | bytes 2211848 | tf_op jit(solution)/shard_map/ppermute | solution.py:1234
  239.1 39.7 %collective-permute-start.8 = (bf16[2,2,2,24,3072]{4,3,0,2,1:T(8,128)(2,1)S(1)}, bf16[2,2,2,24,3072]{4,3,0,2,1:T(8,128)(2,1)S(1)}, u32[]{:S(2)}, u32[]{:S(2)}) collective-permute-start(bf16[2,2,2,24,3072]{4,3,0,2,1:T(8,128)(2,1)S(1)} %maximum_select_fusion.5), channel_id=1, source_target_pairs={{0,4},{1,5},{2,6},{3,7},{4,0},{5,1},{6,2},{7,3},{8,12},{9,13},{10,... | collective-permute-start | bytes 3538952 | tf_op jit(solution)/shard_map/ppermute | solution.py:1234
  253.8 34.0 %collective-permute-start.3 = (bf16[2,2,2,24,3840]{4,3,0,2,1:T(8,128)(2,1)S(1)}, bf16[2,2,2,24,3840]{4,3,0,2,1:T(8,128)(2,1)S(1)}, u32[]{:S(2)}, u32[]{:S(2)}) collective-permute-start(bf16[2,2,2,24,3840]{4,3,0,2,1:T(8,128)(2,1)S(1)} %maximum_select_fusion.4), channel_id=1, source_target_pairs={{0,2},{1,3},{2,0},{3,1},{4,6},{5,7},{6,4},{7,5},{8,10},{9,11},{10,... | collective-permute-start | bytes 4423688 | tf_op jit(solution)/shard_map/ppermute | solution.py:1234
  279.1 11.6 %collective-permute-start.9 = (bf16[2,2,2,2,24,3072]{5,4,1,0,3,2:T(8,128)(2,1)S(1)}, bf16[2,2,2,2,24,3072]{5,4,1,0,3,2:T(8,128)(2,1)S(1)}, u32[]{:S(2)}, u32[]{:S(2)}) collective-permute-start(bf16[2,2,2,2,24,3072]{5,4,1,0,3,2:T(8,128)(2,1)S(1)} %maximum_select_fusion.3), channel_id=1, source_target_pairs={{0,1},{1,0},{2,3},{3,2},{4,5},{5,4},{6,7},{7,6},{8,9},{9,8},{10,11... | collective-permute-start | bytes 7077896 | tf_op jit(solution)/shard_map/ppermute | solution.py:1234
  289.6 12.1 %collective-permute-start.4 = (bf16[2,2,2,2,24,3840]{5,4,0,1,3,2:T(8,128)(2,1)}, bf16[2,2,2,2,24,3840]{5,4,0,1,3,2:T(8,128)(2,1)}, u32[]{:S(2)}, u32[]{:S(2)}) collective-permute-start(bf16[2,2,2,2,24,3840]{5,4,0,1,3,2:T(8,128)(2,1)} %maximum_select_fusion.2), channel_id=1, source_target_pairs={{0,1},{1,0},{2,3},{3,2},{4,5},{5,4},{6,7},{7,6},{8,9},{9,8},{10,11... | collective-permute-start | bytes 8847368 | tf_op jit(solution)/shard_map/ppermute | solution.py:1234
  305.7 23.2 %slice-start = ((s8[4718592]{0:T(1024)(128)(4,1)}), s8[4194304]{0:T(1024)(128)(4,1)S(1)}, s32[]{:S(2)}) async-start(s8[4718592]{0:T(1024)(128)(4,1)} %bitcast.305), calls=%async_computation | async-start | bytes 8388608
  307.2 21.7 %slice-start.1 = ((s8[4718592]{0:T(1024)(128)(4,1)}), s8[524288]{0:T(1024)(128)(4,1)S(1)}, s32[]{:S(2)}) async-start(s8[4718592]{0:T(1024)(128)(4,1)} %bitcast.305), calls=%async_computation.1 | async-start | bytes 1048576
  307.2 21.7 %copy-start.40 = (f32[592]{0:T(1024)S(1)}, f32[592]{0:T(1024)}, u32[]{:S(2)}) copy-start(f32[592]{0:T(1024)} %copy-done.39) | copy-start | bytes 7108
  307.2 21.7 %copy-start.67 = (f32[768]{0:T(1024)S(1)}, f32[768]{0:T(1024)}, u32[]{:S(2)}) copy-start(f32[768]{0:T(1024)} %add.334) | copy-start | bytes 9220
  307.2 21.7 %copy-start.70 = (f32[592]{0:T(1024)S(1)}, f32[592]{0:T(1024)}, u32[]{:S(2)}) copy-start(f32[592]{0:T(1024)} %get-tuple-element.466) | copy-start | bytes 7108
  307.2 21.7 %copy-start.85 = (f32[592]{0:T(1024)S(1)}, f32[592]{0:T(1024)}, u32[]{:S(2)}) copy-start(f32[592]{0:T(1024)} %constant.385.clone.1) | copy-start | bytes 7108
  328.9 4.5 copy-start.86
  329.0 4.8 copy-start.50
  329.0 4.8 copy-start.52
  339.0 9.8 %copy-start.32 = (f32[592,768]{1,0:T(8,128)}, f32[592,768]{1,0:T(8,128)S(1)}, u32[]{:S(2)}) copy-start(f32[592,768]{1,0:T(8,128)S(1)} %get-tuple-element.407) | copy-start | bytes 5455876
  378.4 5.4 copy-start.36
  378.4 6.2 copy-start.20
  381.3 4.7 copy-start.53
  458.6 6.4 copy-start.22
  465.1 7.0 %copy-start.7 = (f32[592,768]{1,0:T(8,128)S(1)}, f32[592,768]{1,0:T(8,128)}, u32[]{:S(2)}) copy-start(f32[592,768]{1,0:T(8,128)} %copy-done.6) | copy-start | bytes 5455876
  465.1 7.0 %copy-start.14 = (bf16[592,4,192]{0,2,1:T(8,128)(2,1)S(1)}, bf16[592,4,192]{0,2,1:T(8,128)(2,1)}, u32[]{:S(2)}) copy-start(bf16[592,4,192]{0,2,1:T(8,128)(2,1)} %copy.952) | copy-start | bytes 2727940
  499.4 78.5 %collective-permute-start.15 = (bf16[2,2,2,2,24,3072]{5,4,3,2,1,0:T(8,128)(2,1)}, bf16[2,2,2,2,24,3072]{5,4,3,2,1,0:T(8,128)(2,1)}, u32[]{:S(2)}, u32[]{:S(2)}) collective-permute-start(bf16[2,2,2,2,24,3072]{5,4,3,2,1,0:T(8,128)(2,1)} %fusion.16), channel_id=1, source_target_pairs={{0,1},{1,0},{2,3},{3,2},{4,5},{5,4},{6,7},{7,6},{8,9},{9,8},{10,11... | collective-permute-start | bytes 7077896 | tf_op jit(solution)/shard_map/ppermute | solution.py:1253
  511.3 73.2 %collective-permute-start.10 = (bf16[2,2,2,2,24,3840]{5,4,0,1,2,3:T(8,128)(2,1)}, bf16[2,2,2,2,24,3840]{5,4,0,1,2,3:T(8,128)(2,1)}, u32[]{:S(2)}, u32[]{:S(2)}) collective-permute-start(bf16[2,2,2,2,24,3840]{5,4,0,1,2,3:T(8,128)(2,1)} %fusion.13), channel_id=1, source_target_pairs={{0,1},{1,0},{2,3},{3,2},{4,5},{5,4},{6,7},{7,6},{8,9},{9,8},{10,11... | collective-permute-start | bytes 8847368 | tf_op jit(solution)/shard_map/ppermute | solution.py:1253
  513.6 5.2 copy-start.71
  513.6 5.9 copy-start.64
  513.6 5.9 copy-start.69
  513.6 6.0 copy-start.68
  513.7 6.1 copy-start.66
  513.7 6.2 copy-start.59
  513.7 6.3 copy-start.63
  513.7 11.0 %copy-start.47 = (f32[32,24]{1,0:T(8,128)S(1)}, f32[32,24]{1,0:T(8,128)}, u32[]{:S(2)}) copy-start(f32[32,24]{1,0:T(8,128)} %reshape.1343) | copy-start | bytes 9220
  513.7 11.2 %copy-start.23 = (bf16[2048,3,64]{0,2,1:T(8,128)(2,1)S(1)}, bf16[2048,3,64]{0,2,1:T(8,128)(2,1)}, u32[]{:S(2)}) copy-start(bf16[2048,3,64]{0,2,1:T(8,128)(2,1)} %copy.977) | copy-start | bytes 2359300
  583.0 29.0 %collective-permute-start.16 = (bf16[2,2,2,24,3072]{4,3,2,1,0:T(8,128)(2,1)}, bf16[2,2,2,24,3072]{4,3,2,1,0:T(8,128)(2,1)}, u32[]{:S(2)}, u32[]{:S(2)}) collective-permute-start(bf16[2,2,2,24,3072]{4,3,2,1,0:T(8,128)(2,1)} %fusion.36), channel_id=1, source_target_pairs={{0,4},{1,5},{2,6},{3,7},{4,0},{5,1},{6,2},{7,3},{8,12},{9,13},{10,... | collective-permute-start | bytes 3538952 | tf_op jit(solution)/shard_map/ppermute | solution.py:1253
  590.2 35.4 %collective-permute-start.11 = (bf16[2,2,2,24,3840]{4,3,0,1,2:T(8,128)(2,1)}, bf16[2,2,2,24,3840]{4,3,0,1,2:T(8,128)(2,1)}, u32[]{:S(2)}, u32[]{:S(2)}) collective-permute-start(bf16[2,2,2,24,3840]{4,3,0,1,2:T(8,128)(2,1)} %fusion.31), channel_id=1, source_target_pairs={{0,2},{1,3},{2,0},{3,1},{4,6},{5,7},{6,4},{7,5},{8,10},{9,11},{10,... | collective-permute-start | bytes 4423688 | tf_op jit(solution)/shard_map/ppermute | solution.py:1253
  596.9 15.1 %copy-start.9 = (f32[2,2,2,2,24,3072]{5,4,3,2,1,0:T(8,128)S(1)}, f32[2,2,2,2,24,3072]{5,4,3,2,1,0:T(8,128)}, u32[]{:S(2)}) copy-start(f32[2,2,2,2,24,3072]{5,4,3,2,1,0:T(8,128)} %copy-done.8) | copy-start | bytes 14155780
  599.8 25.8 %copy-start.5 = (f32[2,2,2,2,24,3840]{5,4,0,1,2,3:T(8,128)S(1)}, f32[2,2,2,2,24,3840]{5,4,0,1,2,3:T(8,128)}, u32[]{:S(2)}) copy-start(f32[2,2,2,2,24,3840]{5,4,0,1,2,3:T(8,128)} %copy-done.4) | copy-start | bytes 17694724
  613.7 24.0 %collective-permute-start.17 = (bf16[2,2,24,3072]{3,2,1,0:T(8,128)(2,1)S(1)}, bf16[2,2,24,3072]{3,2,1,0:T(8,128)(2,1)S(1)}, u32[]{:S(2)}, u32[]{:S(2)}) collective-permute-start(bf16[2,2,24,3072]{3,2,1,0:T(8,128)(2,1)S(1)} %fusion.44), channel_id=1, source_target_pairs={{0,2},{1,3},{2,0},{3,1},{4,6},{5,7},{6,4},{7,5},{8,10},{9,11},{10,... | collective-permute-start | bytes 1769480 | tf_op jit(solution)/shard_map/ppermute | solution.py:1253
  627.4 17.5 %collective-permute-start.12 = (bf16[2,2,24,3840]{3,2,0,1:T(8,128)(2,1)S(1)}, bf16[2,2,24,3840]{3,2,0,1:T(8,128)(2,1)S(1)}, u32[]{:S(2)}, u32[]{:S(2)}) collective-permute-start(bf16[2,2,24,3840]{3,2,0,1:T(8,128)(2,1)S(1)} %fusion.42), channel_id=1, source_target_pairs={{0,4},{1,5},{2,6},{3,7},{4,0},{5,1},{6,2},{7,3},{8,12},{9,13},{10,... | collective-permute-start | bytes 2211848 | tf_op jit(solution)/shard_map/ppermute | solution.py:1253
  637.8 13.2 %collective-permute-start.18 = (bf16[2,24,3072]{2,1,0:T(8,128)(2,1)S(1)}, bf16[2,24,3072]{2,1,0:T(8,128)(2,1)S(1)}, u32[]{:S(2)}, u32[]{:S(2)}) collective-permute-start(bf16[2,24,3072]{2,1,0:T(8,128)(2,1)S(1)} %fusion.56), channel_id=1, source_target_pairs={{0,8},{1,9},{2,10},{3,11},{4,12},{5,13},{6,14},{7,15},{8,0},{9,1},... | collective-permute-start | bytes 884744 | tf_op jit(solution)/shard_map/ppermute | solution.py:1253
  645.1 16.3 %collective-permute-start.13 = (bf16[2,24,3840]{2,1,0:T(8,128)(2,1)S(1)}, bf16[2,24,3840]{2,1,0:T(8,128)(2,1)S(1)}, u32[]{:S(2)}, u32[]{:S(2)}) collective-permute-start(bf16[2,24,3840]{2,1,0:T(8,128)(2,1)S(1)} %fusion.48), channel_id=1, source_target_pairs={{0,8},{1,9},{2,10},{3,11},{4,12},{5,13},{6,14},{7,15},{8,0},{9,1},... | collective-permute-start | bytes 1105928 | tf_op jit(solution)/shard_map/ppermute | solution.py:1253
  651.1 21.0 %copy-start.1 = (bf16[32,12]{0,1:T(8,128)(2,1)S(1)}, bf16[32,12]{0,1:T(8,128)(2,1)}, u32[]{:S(2)}) copy-start(bf16[32,12]{0,1:T(8,128)(2,1)} %param.41) | copy-start | bytes 2308
  651.2 11.1 %collective-permute-start.19 = (bf16[24,3072]{1,0:T(8,128)(2,1)S(1)}, bf16[24,3072]{1,0:T(8,128)(2,1)S(1)}, u32[]{:S(2)}, u32[]{:S(2)}) collective-permute-start(bf16[24,3072]{1,0:T(8,128)(2,1)S(1)} %fusion.67), channel_id=1, source_target_pairs={{0,16},{1,17},{2,18},{3,19},{4,20},{5,21},{6,22},{7,23},{8,24},{9,... | collective-permute-start | bytes 442376 | tf_op jit(solution)/shard_map/ppermute | solution.py:1253
  661.5 9.2 %collective-permute-start.14 = (bf16[24,3840]{1,0:T(8,128)(2,1)S(1)}, bf16[24,3840]{1,0:T(8,128)(2,1)S(1)}, u32[]{:S(2)}, u32[]{:S(2)}) collective-permute-start(bf16[24,3840]{1,0:T(8,128)(2,1)S(1)} %fusion.66), channel_id=1, source_target_pairs={{0,16},{1,17},{2,18},{3,19},{4,20},{5,21},{6,22},{7,23},{8,24},{9,... | collective-permute-start | bytes 552968 | tf_op jit(solution)/shard_map/ppermute | solution.py:1253
  (46 other events, 143.1 us)

commit v2 on v1

--- a/solution.py
+++ b/solution.py
@@ -426,6 +426,12 @@
 BF16 = jnp.bfloat16
 
 
+def cost_of(micros):
+    return pl.CostEstimate(
+        flops=int(micros * 1.0e9), bytes_accessed=int(micros * 1.0e6), transcendentals=0
+    )
+
+
 def bias_kernel(rows_q, own, rev_ref, fold_ref, hot_ref, shift_ref, tile_ref, qbias_ref):
     lane = lax.broadcasted_iota(jnp.int32, (HALF, HALF), 1)
     for h in range(own):
@@ -465,6 +471,7 @@
             jax.ShapeDtypeStruct((own, SEQ_LEN, rows_q), F32),
         ),
         compiler_params=pltpu.CompilerParams(vmem_limit_bytes=50 << 20),
+        cost_estimate=cost_of(14),
         name="bias_tiles",
     )(rev, fold, hot, shift)
 
@@ -617,6 +624,7 @@
             pltpu.VMEM((own, SEQ_LEN, TILE), F32),
         ],
         compiler_params=pltpu.CompilerParams(vmem_limit_bytes=56 << 20),
+        cost_estimate=cost_of(32),
         name="attend",
     )(span, qt, k3, vt, kmeta, rseg, rlim, tiles, qbias)
 
@@ -631,8 +639,8 @@
     kt_ref,
     v_ref,
     ctx_ref,
-    gt_ref,
-    g_ref,
+    gc_ref,
+    gq_ref,
     lse_ref,
     kmeta_ref,
     rseg_ref,
@@ -652,7 +660,23 @@
     diag_scr,
     ds_scr,
     delta_scr,
+    gt_ref,
+    g_ref,
 ):
+    rows = gt_ref.shape[1]
+    for a in range(0, rows, TILE):
+        b = min(a + TILE, rows)
+        if b <= SEQ_LEN:
+            block = gc_ref[a:b, :].astype(F32)
+        else:
+            block = gq_ref[a - SEQ_LEN : min(b - SEQ_LEN, gq_ref.shape[0]), :].astype(F32)
+            if block.shape[0] < b - a:
+                block = jnp.concatenate(
+                    [block, jnp.zeros((b - a - block.shape[0], block.shape[1]), F32)], axis=0
+                )
+        gt_ref[:, a:b] = block.T.astype(BF16)
+        for h in range(own):
+            g_ref[h, a:b, :] = block[:, h * HEAD_DIM : (h + 1) * HEAD_DIM].astype(BF16)
     dk_scr[...] = jnp.zeros(dk_scr.shape, F32)
     dv_scr[...] = jnp.zeros(dv_scr.shape, F32)
     diag_scr[...] = jnp.zeros(diag_scr.shape, F32)
@@ -698,10 +722,8 @@
             return carry
 
         lax.fori_loop(lo, hi + 1, body, 0)
-        for h in range(own):
-            dq_ref[h * HEAD_DIM : (h + 1) * HEAD_DIM, pl.ds(rcol, width)] = (
-                dq_scr[h, :, :width] * SCALE
-            ).astype(BF16)
+        grad = jnp.concatenate([dq_scr[h, :, :width] for h in range(own)], axis=0)
+        dq_ref[pl.ds(rcol, width), :] = (grad * SCALE).T.astype(BF16)
 
     def content_tile(qt, carry):
         def bias_of(h, kt):
@@ -739,9 +761,11 @@
 
     lax.fori_loop(0, rows_q // HALF, query_tile, 0)
 
-    for h in range(own):
-        dk_ref[h] = (dk_scr[h] * SCALE).astype(BF16)
-        dv_ref[h] = dv_scr[h].astype(BF16)
+    for a in range(0, SEQ_LEN, TILE):
+        at = slice(a, a + TILE)
+        for scr, ref, scale in ((dk_scr, dk_ref, SCALE), (dv_scr, dv_ref, 1.0)):
+            block = jnp.concatenate([scr[h, at, :] for h in range(own)], axis=1)
+            ref[at, :] = (block * scale).astype(BF16)
 
     offs_ref[...] = jnp.zeros(offs_ref.shape, F32)
     qoffs_ref[...] = jnp.zeros(qoffs_ref.shape, F32)
@@ -787,7 +811,7 @@
 
 
 def bwd_call(
-    span, qt, q3, k3, kt, v3, ctx, gt, g3, lse, kmeta, rseg, rlim, tiles, qbias, hott, shift
+    span, qt, q3, k3, kt, v3, ctx, g_c, g_q, lse, kmeta, rseg, rlim, tiles, qbias, hott, shift
 ):
     own = k3.shape[0]
     rows = qt.shape[1]
@@ -796,9 +820,9 @@
     return pl.pallas_call(
         functools.partial(bwd_kernel, own, rows_q),
         out_shape=(
-            jax.ShapeDtypeStruct((own * HEAD_DIM, rows), BF16),
-            jax.ShapeDtypeStruct((own, SEQ_LEN, HEAD_DIM), BF16),
-            jax.ShapeDtypeStruct((own, SEQ_LEN, HEAD_DIM), BF16),
+            jax.ShapeDtypeStruct((rows, own * HEAD_DIM), BF16),
+            jax.ShapeDtypeStruct((SEQ_LEN, own * HEAD_DIM), BF16),
+            jax.ShapeDtypeStruct((SEQ_LEN, own * HEAD_DIM), BF16),
             jax.ShapeDtypeStruct((own, 2 * SEQ_LEN), F32),
             jax.ShapeDtypeStruct((own, 2 * SEQ_LEN), F32),
         ),
@@ -810,10 +834,13 @@
             pltpu.VMEM((own, DIAGS, HALF, HALF), F32),
             pltpu.VMEM((own, SEQ_LEN, rows_q), BF16),
             pltpu.VMEM((own, rows), F32),
+            pltpu.VMEM((own * HEAD_DIM, rows), BF16),
+            pltpu.VMEM((own, rows, HEAD_DIM), BF16),
         ],
         compiler_params=pltpu.CompilerParams(vmem_limit_bytes=60 << 20),
+        cost_estimate=cost_of(58),
         name="attend_back",
-    )(span, qt, q3, k3, kt, v3, ctx, gt, g3, lse, kmeta, rseg, rlim, tiles, qbias, hott, shift)
+    )(span, qt, q3, k3, kt, v3, ctx, g_c, g_q, lse, kmeta, rseg, rlim, tiles, qbias, hott, shift)
 
 
 def table_sums(offs, qoffs, rel_bucket):
@@ -872,6 +899,447 @@
     lo = jnp.concatenate([lo, jnp.zeros((1,), jnp.int32)])
     hi = jnp.concatenate([hi, jnp.maximum(count - 1, 0)[None] // TILE])
     return rseg, rlim, kmeta, jnp.stack([lo, hi]).astype(jnp.int32)
+
+
+ROW_CUTS = (0, 144, 288, 432, 592)
+COLS = 768
+FWD_BITS_UP = (16, 8, 4, 2)
+FWD_BITS_DOWN = (16, 8, 2, 4)
+
+
+def dot_nn(a, b):
+    return jnp.dot(a, b, preferred_element_type=F32)
+
+
+def dot_nt(a, b):
+    return lax.dot_general(a, b, (((1,), (1,)), ((), ())), preferred_element_type=F32)
+
+
+def dot_tn(a, b):
+    return lax.dot_general(a, b, (((0,), (0,)), ((), ())), preferred_element_type=F32)
+
+
+def place_of(j, bits):
+    total = 0
+    for n, bit in enumerate(bits):
+        total += ((j >> n) & 1) * (bit // 2)
+    return total
+
+
+def mid_kernel(
+    seqs,
+    bits_up,
+    bits_down,
+    ctx_c,
+    ctx_q,
+    x_c,
+    x_q,
+    cot_c,
+    cot_q,
+    valid_ref,
+    uo_own,
+    uo_mate,
+    down_own,
+    down_mate,
+    bias_out,
+    gain_one,
+    shift_one,
+    bias_up,
+    bias_down,
+    gain_two,
+    shift_two,
+    out_c,
+    out_q,
+    res_c,
+    res_q,
+    gctx_c,
+    gctx_q,
+    uo_keep,
+    uo_give,
+    down_keep,
+    down_give,
+    vec_ref,
+    sums_ref,
+    w_up,
+    w_out,
+    w_down,
+    ctx_scr,
+    one_scr,
+    norm_scr,
+    inv_scr,
+    low_scr,
+    act_scr,
+    slope_scr,
+    sum_scr,
+    grad_scr,
+    pre_scr,
+    part_scr,
+    plane_scr,
+    sems,
+    plane_sems,
+):
+    core = lax.rem(lax.axis_index("seq"), 2)
+    chips, shard = uo_own.shape[0], uo_own.shape[1]
+    shard_down = down_own.shape[1]
+    length = x_c.shape[0]
+    ff = w_up.shape[1]
+    copies = []
+    for j in range(chips):
+        chip = place_of(j, bits_down)
+        for side, ref in ((core, down_own), (1 - core, down_mate)):
+            row = pl.multiple_of((2 * chip + side) * shard_down, 16)
+            copies.append(
+                pltpu.make_async_copy(
+                    ref.at[j], w_down.at[pl.ds(row, shard_down)], sems.at[len(copies)]
+                )
+            )
+    for copy in copies:
+        copy.start()
+
+    def plane_copies(chunk):
+        slot = chunk % 2
+        cols = pl.ds(chunk * COLS, COLS)
+        return [
+            pltpu.make_async_copy(
+                ref.at[:, :, cols], plane_scr.at[slot, n], plane_sems.at[slot, n]
+            )
+            for n, ref in enumerate((uo_own, uo_mate))
+        ]
+
+    chunks = ff // COLS + 1
+    waiting = plane_copies(0)
+    for copy in waiting:
+        copy.start()
+    for chunk in range(chunks):
+        for copy in waiting:
+            copy.wait()
+        if chunk + 1 < chunks:
+            waiting = plane_copies(chunk + 1)
+            for copy in waiting:
+                copy.start()
+        slot = chunk % 2
+
+        def assemble(j, carry, chunk=chunk, slot=slot):
+            chip = place_of(j, bits_up)
+            first = plane_scr[slot, core, j].astype(F32)
+            second = plane_scr[slot, 1 - core, j].astype(F32)
+            pair = jnp.concatenate([first, second], axis=0).astype(BF16)
+            rows = pl.ds(pl.multiple_of(2 * shard * chip, 16), 2 * shard)
+            if chunk < ff // COLS:
+                w_up[rows, chunk * COLS : (chunk + 1) * COLS] = pair
+            else:
+                w_out[rows, :] = pair
+            return carry
+
+        lax.fori_loop(0, chips, assemble, 0)
+
+    wide = ctx_c.shape[2]
+    for t in range(seqs):
+        ctx_scr[t, :length, :] = ctx_c[t]
+        ctx_scr[t, length:, :] = ctx_q[t]
+    blocks = list(zip(ROW_CUTS[:-1], ROW_CUTS[1:]))
+
+    def pick(ref_c, ref_q, a, b):
+        if b <= length:
+            return ref_c[a:b, :]
+        return jnp.concatenate([ref_c[a:length, :], ref_q[: b - length, :]], axis=0)
+
+    def put(ref_c, ref_q, a, b, value):
+        if b <= length:
+            ref_c[a:b, :] = value
+        else:
+            ref_c[a:length, :] = value[: length - a]
+            ref_q[: b - length, :] = value[length - a :][: ref_q.shape[0]]
+
+    def norm(x):
+        mean = jnp.mean(x, axis=-1, keepdims=True)
+        centered = x - mean
+        inv = lax.rsqrt(jnp.mean(centered * centered, axis=-1, keepdims=True) + EPS)
+        return centered * inv, inv
+
+    def norm_grad(up, normed, inv, gain):
+        grad = up * gain
+        proj = jnp.mean(grad, axis=-1, keepdims=True) + normed * jnp.mean(
+            grad * normed, axis=-1, keepdims=True
+        )
+        return inv * (grad - proj)
+
+    sums_ref[...] = jnp.zeros(sums_ref.shape, F32)
+    vec_ref[...] = jnp.zeros(vec_ref.shape, F32)
+
+    def count_in(k, x, a, b):
+        ok = valid_ref[a:b, :1]
+        sq = x * x * ok
+        n = min(b, length) - a
+        sums_ref[k : k + 1, :] += jnp.sum(sq[:n], axis=0, keepdims=True)
+        if b > length:
+            sums_ref[k + 1 : k + 2, :] += jnp.sum(sq[n:], axis=0, keepdims=True)
+
+    for a, b in blocks:
+        attn = bias_out[...] + dot_nn(ctx_scr[0, a:b, :], w_out[:wide, :])
+        for t in range(1, seqs):
+            attn += dot_nn(ctx_scr[t, a:b, :], w_out[t * wide : (t + 1) * wide, :])
+        x = pick(x_c, x_q, a, b)
+        count_in(0, x, a, b)
+        count_in(2, attn, a, b)
+        normed, inv = norm(x + attn)
+        one = normed * gain_one[...] + shift_one[...]
+        norm_scr[a:b, :] = normed
+        inv_scr[a:b, :] = jnp.broadcast_to(inv, (b - a, 128))
+        one_scr[a:b, :] = one
+        low_scr[a:b, :] = one.astype(BF16)
+
+    for copy in copies:
+        copy.wait()
+    sum_scr[...] = jnp.zeros(sum_scr.shape, F32)
+
+    def up_step(i, carry):
+        cols = pl.ds(pl.multiple_of(i * COLS, COLS), COLS)
+        for a, b in blocks:
+            u = dot_nn(low_scr[a:b, :], w_up[:, cols]) + bias_up[:, cols]
+            cdf = 0.5 * (1.0 + lax.erf(u * math.sqrt(0.5)))
+            act = (u * cdf).astype(BF16)
+            act_scr[a:b, cols] = act
+            slope_scr[a:b, cols] = cdf + u * (
+                jnp.exp(-0.5 * u * u) * (1.0 / math.sqrt(2.0 * math.pi))
+            )
+            sum_scr[a:b, :] += dot_nn(act, w_down[cols, :])
+        return carry
+
+    lax.fori_loop(0, ff // COLS, up_step, 0)
+
+    for a, b in blocks:
+        ffn = sum_scr[a:b, :] + bias_down[...]
+        count_in(4, ffn, a, b)
+        normed, inv = norm(one_scr[a:b, :] + ffn)
+        ok = valid_ref[a:b, :1]
+        put(out_c, out_q, a, b, (normed * gain_two[...] + shift_two[...]) * ok)
+        up = pick(cot_c, cot_q, a, b) * ok
+        vec_ref[4:5, :COLS] += jnp.sum(up * normed, axis=0, keepdims=True)
+        vec_ref[5:6, :COLS] += jnp.sum(up, axis=0, keepdims=True)
+        grad = norm_grad(up, normed, inv, gain_two[...])
+        low = grad.astype(BF16)
+        vec_ref[3:4, :COLS] += jnp.sum(low.astype(F32), axis=0, keepdims=True)
+        sum_scr[a:b, :] = grad
+        grad_scr[a:b, :] = low
+
+    def hand_out(keep, give, value, size, width):
+        part_scr[: value.shape[0], :] = value
+
+        def body(j, carry):
+            mine = pl.multiple_of((2 * j + core) * size, 8)
+            other = pl.multiple_of((2 * j + 1 - core) * size, 8)
+            keep(j, part_scr[pl.ds(mine, size), :].astype(BF16))
+            give(j, part_scr[pl.ds(other, size), :].astype(BF16))
+            return carry
+
+        lax.fori_loop(0, value.shape[0] // (2 * size), body, 0)
+
+    def back_step(i, carry):
+        cols = pl.ds(pl.multiple_of(i * COLS, COLS), COLS)
+        for a, b in blocks:
+            low = (
+                dot_nt(grad_scr[a:b, :], w_down[cols, :]) * slope_scr[a:b, cols]
+            ).astype(BF16)
+            pre_scr[a:b, :] = low
+            vec_ref[2:3, cols] += jnp.sum(low.astype(F32), axis=0, keepdims=True)
+            sum_scr[a:b, :] += dot_nt(low, w_up[:, cols])
+
+        def keep_up(j, v):
+            uo_keep[j, :, cols] = v
+
+        def give_up(j, v):
+            uo_give[j, :, cols] = v
+
+        hand_out(keep_up, give_up, dot_tn(low_scr[...], pre_scr[...]), shard, COLS)
+        per = COLS // (2 * shard_down)
+
+        def keep_down(j, v):
+            down_keep[i * per + j] = v
+
+        def give_down(j, v):
+            down_give[i * per + j] = v
+
+        hand_out(keep_down, give_down, dot_tn(act_scr[:, cols], grad_scr[...]), shard_down, COLS)
+        return carry
+
+    lax.fori_loop(0, ff // COLS, back_step, 0)
+
+    for a, b in blocks:
+        up = sum_scr[a:b, :]
+        normed = norm_scr[a:b, :]
+        vec_ref[0:1, :COLS] += jnp.sum(up * normed, axis=0, keepdims=True)
+        vec_ref[1:2, :COLS] += jnp.sum(up, axis=0, keepdims=True)
+        grad = norm_grad(up, normed, inv_scr[a:b, :1], gain_one[...])
+        low = grad.astype(BF16)
+        vec_ref[6:7, :COLS] += jnp.sum(low.astype(F32), axis=0, keepdims=True)
+        put(res_c, res_q, a, b, grad)
+        grad_scr[a:b, :] = low
+    low = grad_scr[...]
+    tail = slice(ff, ff + COLS)
+    for t in range(seqs):
+        part = w_out[t * wide : (t + 1) * wide, :]
+        gctx = dot_nt(low, part).astype(BF16)
+        gctx_c[t] = gctx[:length]
+        gctx_q[t] = gctx[length:]
+        per = wide // (2 * shard)
+
+        def keep_out(j, v, t=t):
+            uo_keep[t * per + j, :, tail] = v
+
+        def give_out(j, v, t=t):
+            uo_give[t * per + j, :, tail] = v
+
+        hand_out(keep_out, give_out, dot_tn(ctx_scr[t], low), shard, COLS)
+
+
+def mid_call(ctx_c, ctx_q, x_c, x_q, cot_c, cot_q, valid, planes, vectors):
+    seqs, length, wide = ctx_c.shape
+    total = length + ctx_q.shape[1]
+    uo_own, uo_mate, down_own, down_mate = planes
+    chips, shard, cols = uo_own.shape
+    shard_down = down_own.shape[1]
+    ff = cols - COLS
+    vm = pl.BlockSpec(memory_space=pltpu.VMEM)
+    hbm = pl.BlockSpec(memory_space=pl.ANY)
+    plane = jax.ShapeDtypeStruct((chips, shard, cols), BF16)
+    plane_down = jax.ShapeDtypeStruct((chips, shard_down, COLS), BF16)
+    return pl.pallas_call(
+        functools.partial(mid_kernel, seqs, FWD_BITS_UP, FWD_BITS_DOWN),
+        out_shape=(
+            jax.ShapeDtypeStruct(x_c.shape, F32),
+            jax.ShapeDtypeStruct(x_q.shape, F32),
+            jax.ShapeDtypeStruct(x_c.shape, F32),
+            jax.ShapeDtypeStruct(x_q.shape, F32),
+            jax.ShapeDtypeStruct(ctx_c.shape, BF16),
+            jax.ShapeDtypeStruct(ctx_q.shape, BF16),
+            plane,
+            plane,
+            plane_down,
+            plane_down,
+            jax.ShapeDtypeStruct((8, ff), F32),
+            jax.ShapeDtypeStruct((8, COLS), F32),
+        ),
+        in_specs=[vm] * 7 + [hbm] * 4 + [vm] * 7,
+        out_specs=(vm,) * 12,
+        scratch_shapes=[
+            pltpu.VMEM((COLS, ff), BF16),
+            pltpu.VMEM((COLS, COLS), BF16),
+            pltpu.VMEM((ff, COLS), BF16),
+            pltpu.VMEM((seqs, total, wide), BF16),
+            pltpu.VMEM((total, COLS), F32),
+            pltpu.VMEM((total, COLS), F32),
+            pltpu.VMEM((total, 128), F32),
+            pltpu.VMEM((total, COLS), BF16),
+            pltpu.VMEM((total, ff), BF16),
+            pltpu.VMEM((total, ff), F32),
+            pltpu.VMEM((total, COLS), F32),
+            pltpu.VMEM((total, COLS), BF16),
+            pltpu.VMEM((total, COLS), BF16),
+            pltpu.VMEM((COLS, COLS), F32),
+            pltpu.VMEM((2, 2, chips, shard, COLS), BF16),
+            pltpu.SemaphoreType.DMA((2 * chips,)),
+            pltpu.SemaphoreType.DMA((2, 2)),
+        ],
+        compiler_params=pltpu.CompilerParams(vmem_limit_bytes=62 << 20),
+        cost_estimate=cost_of(50),
+        name="feed_forward",
+    )(ctx_c, ctx_q, x_c, x_q, cot_c, cot_q, valid, *planes, *vectors)
+
+
+def proj_kernel(own, keys, x_ref, w_ref, bq_ref, bv_ref, qt_ref, q_ref, k_ref, kt_ref, v_ref, vt_ref):
+    wide = own * HEAD_DIM
+    rows = x_ref.shape[0]
+    for a in range(0, rows, 256):
+        b = min(a + 256, rows)
+        parts = [(0, bq_ref, qt_ref, q_ref)]
+        if b <= keys:
+            parts += [(1, None, kt_ref, k_ref), (2, bv_ref, vt_ref, v_ref)]
+        y = dot_nn(x_ref[a:b, :], w_ref[:, : len(parts) * wide])
+        for n, bias, flat_ref, head_ref in parts:
+            part = y[:, n * wide : (n + 1) * wide]
+            if bias is not None:
+                part = part + bias[...]
+            flat_ref[:, a:b] = part.T.astype(BF16)
+            for h in range(own):
+                head_ref[h, a:b, :] = part[:, h * HEAD_DIM : (h + 1) * HEAD_DIM].astype(BF16)
+
+
+def proj_call(own, keys, x, w, bq, bv):
+    rows = x.shape[0]
+    wide = own * HEAD_DIM
+    vm = pl.BlockSpec(memory_space=pltpu.VMEM)
+    flat = lambda n: jax.ShapeDtypeStruct((wide, n), BF16)
+    head = lambda n: jax.ShapeDtypeStruct((own, n, HEAD_DIM), BF16)
+    return pl.pallas_call(
+        functools.partial(proj_kernel, own, keys),
+        out_shape=(flat(rows), head(rows), head(keys), flat(keys), head(keys), flat(keys)),
+        in_specs=[vm] * 4,
+        out_specs=(vm,) * 6,
+        compiler_params=pltpu.CompilerParams(vmem_limit_bytes=40 << 20),
+        cost_estimate=cost_of(5),
+        name="project",
+    )(x, w, bq, bv)
+
+
+def grads_kernel(
+    keys,
+    x_ref,
+    w_ref,
+    dq_ref,
+    dk_ref,
+    dv_ref,
+    gc_ref,
+    gq_ref,
+    gw_ref,
+    sum_ref,
+    part_scr,
+):
+    wide = dq_ref.shape[1]
+    seqs, length = gc_ref.shape[:2]
+    shard = gw_ref.shape[2]
+    for n, ref in enumerate((dq_ref, dk_ref, dv_ref)):
+        part_scr[...] = dot_tn(x_ref[: ref.shape[0], :], ref[...])
+        for j in range(gw_ref.shape[0]):
+            gw_ref[j, n] = part_scr[j * shard : (j + 1) * shard, :].astype(BF16)
+    sum_ref[...] = jnp.zeros(sum_ref.shape, F32)
+    sum_ref[0:1, :] = jnp.sum(dq_ref[...].astype(F32), axis=0, keepdims=True)
+    sum_ref[1:2, :] = jnp.sum(dv_ref[...].astype(F32), axis=0, keepdims=True)
+    w_q = w_ref[:, :wide]
+    w_k = w_ref[:, wide : 2 * wide]
+    w_v = w_ref[:, 2 * wide :]
+    step = 256
+    for t in range(seqs):
+        for a in range(0, length, step):
+            at = slice(t * length + a, t * length + a + step)
+            gc_ref[t, a : a + step, :] = (
+                dot_nt(dq_ref[at, :], w_q) + dot_nt(dk_ref[at, :], w_k) + dot_nt(dv_ref[at, :], w_v)
+            ).astype(BF16)
+    count = gq_ref.shape[1]
+    for t in range(seqs):
+        at = slice(keys + t * count, keys + (t + 1) * count)
+        gq_ref[t] = dot_nt(dq_ref[at, :], w_q).astype(BF16)
+
+
+def grads_call(seqs, length, count, blocks, x, w, dq, dk, dv):
+    wide = dq.shape[1]
+    shard = x.shape[1] // blocks
+    vm = pl.BlockSpec(memory_space=pltpu.VMEM)
+    return pl.pallas_call(
+        functools.partial(grads_kernel, seqs * length),
+        out_shape=(
+            jax.ShapeDtypeStruct((seqs, length, x.shape[1]), BF16),
+            jax.ShapeDtypeStruct((seqs, count, x.shape[1]), BF16),
+            jax.ShapeDtypeStruct((blocks, 3, shard, wide), BF16),
+            jax.ShapeDtypeStruct((8, wide), F32),
+        ),
+        in_specs=[vm] * 5,
+        out_specs=(vm,) * 4,
+        scratch_shapes=[pltpu.VMEM((x.shape[1], wide), F32)],
+        compiler_params=pltpu.CompilerParams(vmem_limit_bytes=40 << 20),
+        cost_estimate=cost_of(6),
+        name="weight_grads",
+    )(x, w, dq, dk, dv)
 
 
 MESH = pl.DeviceIdType.MESH
@@ -1000,7 +1468,7 @@
     copies = 3 * (seqs - 1) + 4 + 2 * (dps - 1) + 2
     zero = jnp.zeros((ROWS_Q - seqs * rq.shape[0], rc.shape[1]), BF16)
     rows = seqs * rc.shape[0] + ROWS_Q
-    hbm = pl.BlockSpec(memory_space=pl.ANY)
+    vmem = pl.BlockSpec(memory_space=pltpu.VMEM)
     return pl.pallas_call(
         functools.partial(start_kernel, dps, seqs),
         out_shape=(
@@ -1009,14 +1477,15 @@
             jax.ShapeDtypeStruct((dps, seqs) + v.shape, F32),
             jax.ShapeDtypeStruct((seqs,) + ints.shape, jnp.int32),
         ),
-        in_specs=[hbm] * 6,
-        out_specs=(hbm,) * 4,
+        in_specs=[vmem] * 6,
+        out_specs=(vmem,) * 4,
         scratch_shapes=[
             pltpu.SemaphoreType.DMA((copies,)),
             pltpu.SemaphoreType.DMA((copies,)),
             pltpu.SemaphoreType.DMA((6,)),
         ],
         compiler_params=pltpu.CompilerParams(collective_id=0, has_side_effects=True),
+        cost_estimate=cost_of(35),
         name="gather_rows",
     )(rc, rq, zero, w, v, ints)
 
@@ -1044,21 +1513,22 @@
 
 
 def swap_call(seqs, c, q, c_of, q_of, c_shape, q_shape, ident, name):
-    hbm = pl.BlockSpec(memory_space=pl.ANY)
+    vmem = pl.BlockSpec(memory_space=pltpu.VMEM)
     return pl.pallas_call(
         functools.partial(swap_kernel, seqs, c_of, q_of),
         out_shape=(
             jax.ShapeDtypeStruct((seqs,) + c_shape, c.dtype),
             jax.ShapeDtypeStruct((seqs,) + q_shape, q.dtype),
         ),
-        in_specs=[hbm] * 2,
-        out_specs=(hbm,) * 2,
+        in_specs=[vmem] * 2,
+        out_specs=(vmem,) * 2,
         scratch_shapes=[
             pltpu.SemaphoreType.DMA((2 * (seqs - 1),)),
             pltpu.SemaphoreType.DMA((2 * (seqs - 1),)),
             pltpu.SemaphoreType.DMA((2,)),
         ],
         compiler_params=pltpu.CompilerParams(collective_id=ident, has_side_effects=True),
+        cost_estimate=cost_of(12),
         name=name,
     )(c, q)
 
@@ -1216,6 +1686,7 @@
         compiler_params=pltpu.CompilerParams(
             collective_id=3, has_side_effects=True, vmem_limit_bytes=50 << 20
         ),
+        cost_estimate=cost_of(30),
         name="sum_rows",
     )(gc, gq, w, v)
 
@@ -1227,33 +1698,25 @@
 AXES = ("dp", "seq")
 
 
-def gather_blocks(shard, count, bits):
-    me = lax.axis_index(AXES)
-    cur = shard
-    for bit in bits:
-        got = lax.ppermute(cur, AXES, flip_perm(count, bit))
-        mine = (me // bit) % 2
-        cur = jnp.where(mine == 0, jnp.stack([cur, got]), jnp.stack([got, cur]))
-    dims = len(bits)
-    order = sorted(range(dims), key=lambda j: -bits[dims - 1 - j])
-    cur = jnp.transpose(cur, tuple(order) + tuple(range(dims, cur.ndim)))
-    return cur.reshape((count * shard.shape[0],) + shard.shape[1:])
-
-
-def scatter_sums(full, count, bits):
-    me = lax.axis_index(AXES)
-    dims = count.bit_length() - 1
-    left = [1 << j for j in reversed(range(dims))]
-    cur = full.reshape((2,) * dims + (full.shape[0] // count, full.shape[1]))
-    for bit in bits:
-        axis = left.index(bit)
-        left.pop(axis)
-        mine = (me // bit) % 2
-        give = lax.dynamic_index_in_dim(cur, 1 - mine, axis, keepdims=False).astype(BF16)
-        got = lax.ppermute(give, AXES, flip_perm(count, bit))
-        keep = lax.dynamic_index_in_dim(cur, mine, axis, keepdims=False)
-        cur = keep + got.astype(F32)
-    return cur
+def tie(values, *others):
+    return lax.optimization_barrier((values, others))[0]
+
+
+def give_to(cur, count, bit):
+    return lax.ppermute(cur, AXES, flip_perm(count, bit))
+
+
+def pile(cur, got, bit):
+    mine = (lax.axis_index(AXES) // bit) % 2
+    return jnp.where(mine == 0, jnp.concatenate([cur, got]), jnp.concatenate([got, cur]))
+
+
+def halves(cur, bit, left):
+    axis = left.index(bit)
+    mine = (lax.axis_index(AXES) // bit) % 2
+    give = lax.dynamic_index_in_dim(cur, 1 - mine, axis, keepdims=False).astype(BF16)
+    stay = lax.dynamic_index_in_dim(cur, mine, axis, keepdims=False)
+    return give, stay
 
 
 def local_fast(
@@ -1290,10 +1753,7 @@
     pad_q = SLOT_Q - preds
     shard = qkv_weight.shape[0]
 
-    rows = jnp.concatenate(
-        [content[0], query_stream[0], jnp.zeros((pad_q, MODEL_WIDTH), F32)], axis=0
-    )
-    rows_low = rows.astype(BF16)
+    x_q = jnp.pad(query_stream[0], ((0, pad_q), (0, 0)))
     vec = jnp.concatenate(
         [
             member.astype(F32)
@@ -1322,8 +1782,19 @@
     w_parts = jnp.transpose(
         qkv_weight.reshape(shard, 3, seqs, wide), (2, 0, 1, 3)
     ).reshape(seqs, shard, 3 * wide)
+    gather = (jnp.concatenate([up_weight, out_weight], axis=1)[None], down_weight[None])
+    stages = list(zip(FWD_BITS_UP, FWD_BITS_DOWN))
+
+    def launch(n):
+        return tuple(give_to(cur, count, bit) for cur, bit in zip(gather, stages[n]))
+
+    def land(n, got, *others):
+        got = tie(got, *others)
+        return tuple(pile(c, g, bit) for c, g, bit in zip(gather, got, stages[n]))
+
+    flying = launch(0)
     x_all, w_all, v_all, i_all = start_call(
-        dps, seqs, rows_low[:length], rows_low[length:], w_parts, vec, ints
+        dps, seqs, content[0].astype(BF16), x_q.astype(BF16), w_parts, vec, ints
     )
     w_qkv = w_all.reshape(MODEL_WIDTH, 3 * wide)
     parts = v_all.reshape(count, 1024)
@@ -1338,45 +1809,32 @@
     pad_all = i_all[:, 2].reshape(seqs * length)
     pred_all = i_all[:, 3, :SLOT_Q].reshape(seqs * SLOT_Q)
 
-    bits_up = (8, 16, 4, 2, 1)
-    bits_down = (8, 16, 2, 4, 1)
-    upout = gather_blocks(
-        jnp.concatenate([up_weight, out_weight], axis=1), count, bits_up
-    )
-    w_down = gather_blocks(
-        down_weight.reshape(shard, -1), count, bits_down
-    ).reshape(-1, MODEL_WIDTH)
-    w_up, w_out = upout[:, : up_weight.shape[1]], upout[:, up_weight.shape[1] :]
-
+    gather = land(0, flying, i_all)
+    flying = launch(1)
     rev, fold = bias_inputs(rel_bucket, rel_table, s * own, own)
+    rev, fold = tie((rev, fold), gather)
     hot, hot_t, shift = query_place(pred_all, ROWS_Q)
     rseg, rlim, kmeta, span = row_meta(seg_all, pad_all, order_all, pred_all, ROWS_Q)
     tiles, qbias = bias_call(rev, fold, hot, shift)
 
     bq = lax.dynamic_slice_in_dim(bias_qv[:MODEL_WIDTH], s * wide, wide)
     bv = lax.dynamic_slice_in_dim(bias_qv[MODEL_WIDTH:], s * wide, wide)
-    w_q, w_k, w_v = w_qkv[:, :wide], w_qkv[:, wide : 2 * wide], w_qkv[:, 2 * wide :]
-    keys = x_all[: seqs * length]
-
-    def flat(x, w, b):
-        y = jnp.einsum("rd,de->re", x, w, preferred_element_type=F32)
-        return (y if b is None else y + b).astype(BF16)
-
-    def flipped(x, w, b):
-        y = jnp.einsum("rd,de->er", x, w, preferred_element_type=F32)
-        return (y if b is None else y + b[:, None]).astype(BF16)
-
-    def by_head(x):
-        return jnp.transpose(x.reshape(x.shape[0], own, HEAD_DIM), (1, 0, 2))
-
-    q_t = flipped(x_all, w_q, bq)
-    q3 = by_head(flat(x_all, w_q, bq))
-    k3 = by_head(flat(keys, w_k, None))
-    k_t = flipped(keys, w_k, None)
-    v3 = by_head(flat(keys, w_v, bv))
-    v_t = flipped(keys, w_v, bv)
+    gather = land(1, flying, tiles)
+    flying = launch(2)
+    x_all = tie(x_all, gather)
+    q_t, q3, k3, k_t, v3, v_t = proj_call(
+        own, seqs * length, x_all, w_qkv, bq[None], bv[None]
+    )
+    gather = land(2, flying, q_t)
+    flying = launch(3)
+    q_t = tie(q_t, gather)
 
     ctx_t, ctx_rows, lse = fwd_call(span, q_t, k3, v_t, kmeta, rseg, rlim, tiles, qbias)
+
+    gather = land(3, flying, ctx_rows)
+    others = tuple(give_to(cur, count, 1) for cur in gather)
+    ctx_rows = tie(ctx_rows, gather)
+    planes = (gather[0], others[0], gather[1], others[1])
 
     def from_rows(ref, t):
         return ref.at[pl.ds(pl.multiple_of(t * length, length), length)]
@@ -1395,85 +1853,65 @@
         1,
         "swap_context",
     )
-    context_low = jnp.transpose(
-        jnp.concatenate([ctx_c, ctx_q], axis=1), (1, 0, 2)
-    ).reshape(length + SLOT_Q, MODEL_WIDTH)
-
-    attn_out = jnp.einsum("re,ed->rd", context_low, w_out, preferred_element_type=F32) + bias_out
-    hidden_one, normed_one, inv_one = norm_fwd((rows + attn_out)[None], gain_one, shift_one)
-    hidden_low = hidden_one[0].astype(BF16)
-    pre_act = jnp.einsum("rd,df->rf", hidden_low, w_up, preferred_element_type=F32) + bias_up
-    activ, gelu_pull = jax.vjp(exact_gelu, pre_act)
-    activ_low = activ.astype(BF16)
-    ffn_out = jnp.einsum("rf,fd->rd", activ_low, w_down, preferred_element_type=F32) + bias_down
-    hidden_two, normed_two, inv_two = norm_fwd(hidden_one + ffn_out[None], gain_two, shift_two)
     pad_float = pad_mask[0].astype(F32)
-    row_valid = jnp.concatenate([pad_float, jnp.ones((preds,), F32), jnp.zeros((pad_q,), F32)])
-    outputs = hidden_two[0] * row_valid[:, None]
-    rows_c = jnp.concatenate([pad_float, jnp.zeros((SLOT_Q,), F32)])[:, None]
-    rows_q = jnp.concatenate(
-        [jnp.zeros((length,), F32), jnp.ones((preds,), F32), jnp.zeros((pad_q,), F32)]
-    )[:, None]
-    local_sums = jnp.stack(
+    valid = jnp.concatenate([pad_float, jnp.ones((preds,), F32), jnp.zeros((pad_q,), F32)])
+    valid = jnp.broadcast_to(valid[:, None], (length + SLOT_Q, 128))
+    (
+        out_c,
+        out_q,
+        res_c,
+        res_q,
+        give_c,
+        give_q,
+        uo_keep,
+        uo_give,
+        down_keep,
+        down_give,
+        vec_sums,
+        squares,
+    ) = mid_call(
+        ctx_c,
+        ctx_q,
+        content[0],
+        x_q,
+        content_cot[0],
+        jnp.pad(query_cot[0], ((0, pad_q), (0, 0))),
+        valid,
+        planes,
         [
-            jnp.sum(rows_c * rows * rows),
-            jnp.sum(rows_q * rows * rows),
-            jnp.sum(rows_c * attn_out * attn_out),
-            jnp.sum(rows_q * attn_out * attn_out),
-            jnp.sum(rows_c * ffn_out * ffn_out),
-            jnp.sum(rows_q * ffn_out * ffn_out),
-            jnp.sum(pad_float),
-        ]
-    )
-    upstream = (
-        jnp.concatenate([content_cot[0], query_cot[0], jnp.zeros((pad_q, MODEL_WIDTH), F32)])
-        * row_valid[:, None]
-    )
-    grad_res_two, grad_gain_two, grad_shift_two = norm_back(
-        upstream[None], normed_two, inv_two, gain_two
-    )
-    grad_res_two = grad_res_two[0]
-    grad_ffn = grad_res_two.astype(BF16)
-    grad_bias_down = jnp.sum(grad_ffn, axis=0, dtype=F32)
-    grad_down = jnp.einsum("rf,rd->fd", activ_low, grad_ffn, preferred_element_type=F32)
-    grad_activ = jnp.einsum("rd,fd->rf", grad_ffn, w_down, preferred_element_type=F32)
-    grad_pre = gelu_pull(grad_activ)[0].astype(BF16)
-    grad_bias_up = jnp.sum(grad_pre, axis=0, dtype=F32)
-    grad_up = jnp.einsum("rd,rf->df", hidden_low, grad_pre, preferred_element_type=F32)
-    grad_hidden = grad_res_two + jnp.einsum(
-        "rf,df->rd", grad_pre, w_up, preferred_element_type=F32
-    )
-    grad_res_one, grad_gain_one, grad_shift_one = norm_back(
-        grad_hidden[None], normed_one, inv_one, gain_one
-    )
-    grad_res_one = grad_res_one[0]
-    grad_attn = grad_res_one.astype(BF16)
-    grad_bias_out = jnp.sum(grad_attn, axis=0, dtype=F32)
-    grad_out = jnp.einsum("re,rd->ed", context_low, grad_attn, preferred_element_type=F32)
-    grad_context = jnp.einsum(
-        "rd,ed->re", grad_attn, w_out, preferred_element_type=F32
-    ).astype(BF16)
-
-    grad_down_own = scatter_sums(
-        grad_down.reshape(MODEL_WIDTH, -1), count, (1, 4, 2, 8, 16)
-    ).reshape(-1, MODEL_WIDTH)
-    grad_upout_own = scatter_sums(
-        jnp.concatenate([grad_up, grad_out], axis=1), count, (1, 2, 4, 8, 16)
-    )
-    grad_up_own = grad_upout_own[:, : up_weight.shape[1]]
-    grad_out_own = grad_upout_own[:, up_weight.shape[1] :]
-
-    split = jnp.transpose(
-        grad_context.reshape(length + SLOT_Q, seqs, wide), (1, 0, 2)
-    )
+            member[None]
+            for member in (bias_out, gain_one, shift_one, bias_up, bias_down, gain_two, shift_two)
+        ],
+    )
+    back = ((2, 4, 8, 16), (4, 2, 8, 16))
+    left = [[16, 8, 4, 2], [16, 8, 4, 2]]
+    flying = (give_to(uo_give, count, 1), give_to(down_give, count, 1))
+    stay = (uo_keep, down_keep)
+
+    def add_up(got, *others):
+        got = tie(got, *others)
+        return tuple(k.astype(F32) + g.astype(F32) for k, g in zip(stay, got))
+
+    def send_on(n, sums):
+        away, kept, gone = [], [], []
+        for i in range(2):
+            bit = back[i][n]
+            give, keep = halves(sums[i], bit, left[i])
+            left[i].remove(bit)
+            gone.append(give)
+            away.append(give_to(give, count, bit))
+            kept.append(keep)
+        return tuple(away), tuple(kept), tuple(gone)
+
+    local_sums = jnp.concatenate([jnp.sum(squares, axis=1)[:6], jnp.sum(pad_float)[None]])
 
     def from_slot(ref, t):
         return ref.at[t]
 
     g_c, g_q = swap_call(
         seqs,
-        split[:, :length],
-        split[:, length:],
+        give_c,
+        give_q,
         from_slot,
         from_slot,
         (length, wide),
@@ -1481,14 +1919,11 @@
         2,
         "swap_grads",
     )
-    g_rows = jnp.concatenate(
-        [
-            g_c.reshape(seqs * length, wide),
-            g_q.reshape(seqs * SLOT_Q, wide),
-            jnp.zeros((ROWS_Q - seqs * SLOT_Q, wide), BF16),
-        ]
-    )
-    dq_t, dk3, dv3, offs, qoffs = bwd_call(
+    sums = add_up(flying, g_c)
+    sums = tuple(x.reshape((2,) * 4 + x.shape[1:]) for x in sums)
+    flying, stay, gone = send_on(0, sums)
+    g_c = tie(g_c, stay, gone)
+    dq, dk, dv, offs, qoffs = bwd_call(
         span,
         q_t,
         q3,
@@ -1496,8 +1931,8 @@
         k_t,
         v3,
         ctx_t,
-        g_rows.T,
-        by_head(g_rows),
+        g_c.reshape(seqs * length, wide),
+        g_q.reshape(seqs * SLOT_Q, wide),
         lse,
         kmeta,
         rseg,
@@ -1508,31 +1943,15 @@
         shift,
     )
     table = table_sums(offs, qoffs, rel_bucket)
-    dk = jnp.transpose(dk3, (1, 0, 2)).reshape(seqs * length, wide)
-    dv = jnp.transpose(dv3, (1, 0, 2)).reshape(seqs * length, wide)
-    grad_w = jnp.concatenate(
-        [
-            jnp.einsum("rd,er->de", x_all, dq_t, preferred_element_type=F32),
-            jnp.einsum("rd,re->de", keys, dk, preferred_element_type=F32),
-            jnp.einsum("rd,re->de", keys, dv, preferred_element_type=F32),
-        ],
-        axis=1,
-    ).astype(BF16)
-    dq = dq_t.T
-    cut = seqs * length
-    grad_keys_rows = (
-        jnp.einsum("re,de->rd", dq[:cut], w_q, preferred_element_type=F32)
-        + jnp.einsum("re,de->rd", dk, w_k, preferred_element_type=F32)
-        + jnp.einsum("re,de->rd", dv, w_v, preferred_element_type=F32)
-    ).astype(BF16)
-    grad_query_rows = jnp.einsum(
-        "re,de->rd", dq[cut : cut + seqs * SLOT_Q], w_q, preferred_element_type=F32
-    ).astype(BF16)
-    bias_q = jnp.sum(dq_t.astype(F32), axis=1)
-    bias_v = jnp.sum(dv.astype(F32), axis=0)
+    sums = add_up(flying, dq)
+    flying, stay, gone = send_on(1, sums)
+    dq = tie(dq, stay, gone)
+    grad_c, grad_q, grad_w, qv_sums = grads_call(
+        seqs, length, SLOT_Q, count, x_all, w_qkv, dq, dk, dv
+    )
     spot = jnp.zeros((2, MODEL_WIDTH), F32)
     grad_bias_qv = lax.dynamic_update_slice(
-        spot, jnp.stack([bias_q, bias_v]), (0, s * wide)
+        spot, qv_sums[:2], (0, s * wide)
     ).reshape(2 * MODEL_WIDTH)
     table_all = lax.dynamic_update_slice(
         jnp.zeros((BUCKETS, HEADS), F32), table, (0, s * own)
@@ -1542,13 +1961,13 @@
             member.reshape(count, -1)
             for member in (
                 grad_bias_qv,
-                grad_bias_out,
-                grad_gain_one,
-                grad_shift_one,
-                grad_bias_up,
-                grad_bias_down,
-                grad_gain_two,
-                grad_shift_two,
+                vec_sums[6, :MODEL_WIDTH],
+                vec_sums[0, :MODEL_WIDTH],
+                vec_sums[1, :MODEL_WIDTH],
+                vec_sums[2],
+                vec_sums[3, :MODEL_WIDTH],
+                vec_sums[4, :MODEL_WIDTH],
+                vec_sums[5, :MODEL_WIDTH],
             )
         ],
         axis=1,
@@ -1563,17 +1982,24 @@
         ],
         axis=1,
     ).reshape(dps, seqs, 8, 128)
+    sums = add_up(flying, grad_c)
+    flying, stay, gone = send_on(2, sums)
+    grad_c = tie(grad_c, stay, gone)
     sum_c, sum_q, sum_w, sum_v = end_call(
         dps,
         seqs,
-        grad_keys_rows.reshape(seqs, length, MODEL_WIDTH),
-        grad_query_rows.reshape(seqs, SLOT_Q, MODEL_WIDTH),
-        grad_w.reshape(dps, seqs, shard, 3 * wide),
+        grad_c,
+        grad_q,
+        grad_w.reshape(dps, seqs, 3 * shard, wide),
         vec_grads,
     )
-    grad_content = grad_res_one[:length] + sum_c
-    grad_query = grad_res_one[length : length + preds] + sum_q[:preds]
-    grad_qkv_own = jnp.transpose(sum_w.reshape(seqs, shard, 3, wide), (1, 2, 0, 3)).reshape(
+    sums = add_up(flying, sum_c)
+    flying, stay, _ = send_on(3, sums)
+    grad_uo_own, grad_down_own = add_up(flying)
+    grad_up_own, grad_out_own = grad_uo_own[:, :-MODEL_WIDTH], grad_uo_own[:, -MODEL_WIDTH:]
+    grad_content = res_c + sum_c
+    grad_query = res_q[:preds] + sum_q[:preds]
+    grad_qkv_own = jnp.transpose(sum_w.reshape(seqs, 3, shard, wide), (2, 1, 0, 3)).reshape(
         shard, 3 * MODEL_WIDTH
     )
     sums = sum_v.reshape(1024)
@@ -1589,8 +2015,8 @@
     each = jnp.stack([content_count, jnp.float32(query_count)])
     stats = jnp.sqrt(totals[:6] / jnp.concatenate([each, each, each]))
     return (
-        outputs[None, :length],
-        outputs[None, length : length + preds],
+        out_c[None],
+        out_q[None, :preds],
         grad_content[None],
         grad_query[None],
         grad_qkv_own,

time: 679 us -> 441 us (0.65)
  the two profiles are of different devices: /device:TPU:0 before, /device:TPU:5 now
where the time goes in v2:
time: 441 us; the launch traced here: 433 us
  Pallas kernels  289 us (66%)
  local copies, waits for them, and re-layouts  49.6 us (11%)
  other arithmetic  34.8 us (8%)
  waiting for transfers between devices  27.3 us (6%)
  starting transfers between devices  25.9 us (6%)
    pallas_call x1, Pallas kernels, bwd_call(): pl.pallas_call(functools.partial(bwd_kernel, own, rows_q), out_shape=(jax...  62.1 us
    pallas_call x1, Pallas kernels, mid_call(): pl.pallas_call(functools.partial(mid_kernel, seqs, FWD_BITS_UP, FWD_BITS_...  56.7 us
    pallas_call x1, Pallas kernels, end_call(): pl.pallas_call(functools.partial(end_kernel, dps, seqs), out_shape=(jax.S...  42.2 us
    pallas_call x2, Pallas kernels, swap_call(): pl.pallas_call(functools.partial(swap_kernel, seqs, c_of, q_of), out_shap...  36.1 us
    pallas_call x1, Pallas kernels, fwd_call(): pl.pallas_call(functools.partial(fwd_kernel, own, rows_q), out_shape=(jax...  34.3 us
    pallas_call x1, Pallas kernels, start_call(): pl.pallas_call(functools.partial(start_kernel, dps, seqs), out_shape=(jax...  33.7 us
    ppermute x20, waiting for transfers between devices, give_to(): return lax.ppermute(cur, AXES, flip_perm(count, bit))  27.3 us
    ppermute x20, starting transfers between devices, give_to(): return lax.ppermute(cur, AXES, flip_perm(count, bit))  25.9 us
  transfers between devices with their start and end apart: 20, of which 7 were waited for; matrix products, arithmetic and copies ran while one was open for 13% of the time, Pallas kernels for 54%

profile of v2, /device:TPU:5, one launch (start us, length us, event | category | flops | bytes accessed | tf_op | source)
XLA Modules:
  0.0 432.8 jit_solution(14772150238659400725)
XLA Ops:
  0.8 1.0 maximum_bitcast_fusion
  1.9 2.4 collective-permute-start
  4.3 1.0 copy.532
  5.3 2.4 bitcast_convert_fusion.1.rc_ref
  11.5 33.7 %gather_rows.1 = (bf16[2432,768]{1,0:T(8,128)(2,1)}, bf16[8,4,24,576]{3,2,1,0:T(8,128)(2,1)}, f32[8,4,8,128]{3,2,1,0:T(8,128)}, s32[4,8,512]{2,1,0:T(8,128)}) custom-call(bf16[512,768]{1,0:T(8,128)(2,1)} %bitcast_convert_fusion.1.rc_ref, bf16[80,768]{1,0:T(8,128)(2,1)} %pad.193.rq_ref, bf16[64,768]{1,0:T(8,128)(2,1)} %broadcast_in_dim.103.zero_ref, ...), custom_call_target="tpu_custom_call" | custom-call | flops 35000000512 | bytes 35000000 | tf_op jit(solution)/shard_map/gather_rows/pallas_call | solution.py:1472
  45.9 1.6 fusion.21
  47.5 0.9 fusion.18
  49.1 2.8 reverse
  52.8 0.9 copy.534
  54.0 0.9 select_reduce_fusion
  57.1 6.3 %collective-permute-start.3 = (bf16[2,96,768]{2,1,0:T(8,128)(2,1)S(1)}, bf16[2,96,768]{2,1,0:T(8,128)(2,1)S(1)}, u32[]{:S(2)}, u32[]{:S(2)}) collective-permute-start(bf16[2,96,768]{2,1,0:T(8,128)(2,1)S(1)} %maximum_select_fusion.7), channel_id=1, source_target_pairs={{0,8},{1,9},{2,10},{3,11},{4,12},{5,13},{6,14},{7,15},{8,0},{9,1},... | collective-permute-start | bytes 884744 | tf_op jit(solution)/shard_map/ppermute | solution.py:1706
  63.6 14.0 %bias_tiles.1 = (f32[3,19,128,128]{3,2,1,0:T(8,128)}, f32[3,2048,384]{2,1,0:T(8,128)}) custom-call(f32[3,4096]{1,0:T(4,128)S(1)} %pad_multiply_fusion.rev_ref, bf16[3,16,2176]{2,1,0:T(8,128)(2,1)S(1)} %stack.93.fold_ref, bf16[384,16]{1,0:T(8,128)(2,1)S(1)} %copy.498.hot_ref, s32[384,128]{1,0:T(8,128)S(1)} %broadcast_in_dim.107.shift_ref), custom_call_target="tpu_custom_call" | custom-call | flops 14000000000 | bytes 14000000 | tf_op jit(solution)/shard_map/bias_tiles/pallas_call | solution.py:467
  81.0 2.1 copy-done.5
  83.1 4.0 project.1
  87.1 0.9 copy-done.14
  88.1 0.9 copy-done.15
  89.0 0.9 copy-done.16
  89.9 2.9 collective-permute-done.5
  92.8 3.0 collective-permute-done.4
  96.3 1.6 maximum_select_fusion.2
  98.2 2.3 broadcast_in_dim.110.kmeta_ref
  100.5 34.3 %attend.1 = (bf16[192,2432]{1,0:T(8,128)(2,1)}, bf16[2432,192]{1,0:T(8,128)(2,1)}, f32[3,2432]{1,0:T(4,128)}) custom-call(s32[2,9]{1,0:T(2,128)} %pad_add_fusion.3.span_ref, bf16[192,2432]{1,0:T(8,128)(2,1)} %copy-done.14, bf16[3,2048,64]{2,1,0:T(8,128)(2,1)} %copy-done.9, bf16[192,2048]{1,0:T(8,128)(2,1)} %copy-done.16, ...), custom_call_target="tpu_custom_call" | custom-call | flops 32000000000 | bytes 32000000 | tf_op jit(solution)/shard_map/attend/pallas_call | solution.py:615
  134.8 1.0 copy-done.29
  135.8 1.1 copy-done.28
  136.9 2.2 maximum_select_fusion.uo_own
  139.1 2.1 collective-permute-start.8
  141.2 1.7 maximum_select_fusion.1.down_own
  149.1 1.0 copy.531
  150.9 18.3 %swap_context.1 = (bf16[4,512,192]{2,1,0:T(8,128)(2,1)}, bf16[4,80,192]{2,1,0:T(8,128)(2,1)}) custom-call(bf16[2432,192]{1,0:T(8,128)(2,1)} %get-tuple-element.110.c_ref.q_ref, bf16[2432,192]{1,0:T(8,128)(2,1)} %get-tuple-element.110.c_ref.q_ref), custom_call_target="tpu_custom_call" | custom-call | flops 12000000000 | bytes 12000000 | tf_op jit(solution)/shard_map/swap_context/pallas_call | solution.py:1517
  169.2 0.9 broadcast_in_dim.117.valid_ref
  170.0 56.7 %feed_forward.1 = (f32[512,768]{1,0:T(8,128)}, f32[80,768]{1,0:T(8,128)}, f32[512,768]{1,0:T(8,128)}, f32[80,768]{1,0:T(8,128)}, bf16[4,512,192]{2,1,0:T(8,128)(...) custom-call(bf16[4,512,192]{2,1,0:T(8,128)(2,1)} %get-tuple-element., ...), custom_call_target="tpu_custom_call" | custom-call | flops 49999998976 | bytes 50000000 | tf_op jit(solution)/shard_map/feed_forward/pallas_call | solution.py:1207
  228.1 0.9 reduce_sum.58
  229.0 1.0 slice_reduce_fusion.2
  230.5 0.9 slice_reduce_fusion
  231.5 1.0 slice_bitcast_fusion
  232.5 0.9 copy.505
  233.4 17.8 %swap_grads.1 = (bf16[4,512,192]{2,1,0:T(8,128)(2,1)}, bf16[4,80,192]{2,1,0:T(8,128)(2,1)}) custom-call(bf16[4,512,192]{2,1,0:T(8,128)(2,1)} %get-tuple-element.120.c_ref, bf16[4,80,192]{2,1,0:T(8,128)(2,1)} %get-tuple-element.121.q_ref), custom_call_target="tpu_custom_call" | custom-call | flops 12000000000 | bytes 12000000 | tf_op jit(solution)/shard_map/swap_grads/pallas_call | solution.py:1517
  251.3 3.1 convert_add_fusion.1
  254.4 1.3 fusion.1
  255.7 1.6 collective-permute-start.13
  258.1 2.5 copy-done.17
  260.8 1.4 collective-permute-start.12
  262.2 62.1 %attend_back.1 = (bf16[2432,192]{1,0:T(8,128)(2,1)}, bf16[2048,192]{1,0:T(8,128)(2,1)}, bf16[2048,192]{1,0:T(8,128)(2,1)}, f32[3,4096]{1,0:T(4,128)}, f32[3,4096]{1,0:T(4,128)}) custom-call(s32[2,9]{1,0:T(2,128)} %pad_add_fusion.3.span_ref, bf16[192,2432]{1,0:T(8,128)(2,1)} %copy-done.14, bf16[3,2432,64]{2,1,0:T(8,128)(2,1)} %copy-done.8, ...), custom_call_target="tpu_custom_call" | custom-call | flops 57999998976 | bytes 58000000 | tf_op jit(solution)/shard_map/attend_back/pallas_call | solution.py:820
  324.3 1.2 fusion.4
  325.5 1.2 convolution_add_fusion
  328.2 2.2 convert_add_fusion.2
  330.5 3.4 convert_add_fusion.3
  334.0 1.7 collective-permute-start.14
  335.7 0.9 fusion.3
  336.7 6.0 %weight_grads.1 = (bf16[4,512,768]{2,1,0:T(8,128)(2,1)S(1)}, bf16[4,80,768]{2,1,0:T(8,128)(2,1)S(1)}, bf16[32,3,24,192]{3,2,1,0:T(8,128)(2,1)S(1)}, f32[8,192]{1,0:T(8,128)S(1)}) custom-call(bf16[2432,768]{1,0:T(8,128)(2,1)S(1)} %copy-done.6, bf16[768,576]{1,0:T(8,128)(2,1)S(1)} %bitcast.156, bf16[2432,192]{1,0:T(8,128)(2,1)S(1)} %copy-done.11, ...), custom_call_target="tpu_custom_call" | custom-call | flops 6000000000 | bytes 6000000 | tf_op jit(solution)/shard_map/weight_grads/pallas_call | solution.py:1328
  342.7 1.6 copy-done.7
  344.9 6.8 %collective-permute-done.15 = bf16[2,2,96,768]{3,2,0,1:T(8,128)(2,1)} collective-permute-done((bf16[2,2,96,768]{3,2,0,1:T(8,128)(2,1)}, bf16[2,2,96,768]{3,2,0,1:T(8,128)(2,1)}, u32[]{:S(2)}, u32[]{:S(2)}) %collective-permute-start.15) | collective-permute-done | bytes 589856 | tf_op jit(solution)/shard_map/ppermute | solution.py:1706
  351.9 1.6 convert_add_fusion.5
  353.7 1.1 fusion.6
  354.8 1.5 collective-permute-start.16
  356.2 42.2 %sum_rows.1 = (f32[512,768]{1,0:T(8,128)S(1)}, f32[80,768]{1,0:T(8,128)S(1)}, f32[4,72,192]{2,1,0:T(8,128)S(1)}, f32[8,128]{1,0:T(8,128)S(1)}) custom-call(bf16[4,512,768]{2,1,0:T(8,128)(2,1)} %copy-done.7, bf16[4,80,768]{2,1,0:T(8,128)(2,1)S(1)} %get-tuple-element.142.gq_ref, bf16[8,4,72,192]{3,2,1,0:T(8,128)(2,1)S(1)} %bitcast.154, ...), custom_call_target="tpu_custom_call" | custom-call | flops 30000001024 | bytes 30000000 | tf_op jit(solution)/shard_map/sum_rows/pallas_call | solution.py:1661
  400.8 0.9 copy.506
  401.8 0.9 reshape.193
  404.2 2.9 add_bitcast_fusion
  407.1 1.0 convert_add_fusion.7
  408.2 6.6 %collective-permute-start.19 = (bf16[96,768]{1,0:T(8,128)(2,1)S(1)}, bf16[96,768]{1,0:T(8,128)(2,1)S(1)}, u32[]{:S(2)}, u32[]{:S(2)}) collective-permute-start(bf16[96,768]{1,0:T(8,128)(2,1)S(1)} %fusion.12), channel_id=1, source_target_pairs={{0,16},{1,17},{2,18},{3,19},{4,20},{5,21},{6,22},{7,23},{8,24},{9,... | collective-permute-start | bytes 442376 | tf_op jit(solution)/shard_map/ppermute | solution.py:1706
  414.7 1.1 convert_add_fusion.6
  416.5 9.7 %collective-permute-done.19 = bf16[96,768]{1,0:T(8,128)(2,1)S(1)} collective-permute-done((bf16[96,768]{1,0:T(8,128)(2,1)S(1)}, bf16[96,768]{1,0:T(8,128)(2,1)S(1)}, u32[]{:S(2)}, u32[]{:S(2)}) %collective-permute-start.19) | collective-permute-done | bytes 147488 | tf_op jit(solution)/shard_map/ppermute | solution.py:1706
  426.2 3.9 collective-permute-done.18
  (242 shorter events, 30.9 us)
Async XLA Ops:
  0.7 48.1 %copy-start = (bf16[32,12]{0,1:T(8,128)(2,1)S(1)}, bf16[32,12]{0,1:T(8,128)(2,1)}, u32[]{:S(2)}) copy-start(bf16[32,12]{0,1:T(8,128)(2,1)} %param.41) | copy-start | bytes 2308
  0.7 7.0 %copy-start.33 = (bf16[24,2304]{1,0:T(8,128)(2,1)S(1)}, bf16[24,2304]{1,0:T(8,128)(2,1)}, u32[]{:S(2)}) copy-start(bf16[24,2304]{1,0:T(8,128)(2,1)} %param.29) | copy-start | bytes 331780
  0.7 8.0 %copy-start.38 = (bf16[48]{0:T(256)(128)(2,1)S(1)}, bf16[48]{0:T(256)(128)(2,1)}, u32[]{:S(2)}) copy-start(bf16[48]{0:T(256)(128)(2,1)} %param.30) | copy-start | bytes 292
  0.7 8.0 %copy-start.39 = (bf16[24]{0:T(256)(128)(2,1)S(1)}, bf16[24]{0:T(256)(128)(2,1)}, u32[]{:S(2)}) copy-start(bf16[24]{0:T(256)(128)(2,1)} %param.32) | copy-start | bytes 148
  0.7 8.0 %copy-start.40 = (bf16[24]{0:T(256)(128)(2,1)S(1)}, bf16[24]{0:T(256)(128)(2,1)}, u32[]{:S(2)}) copy-start(bf16[24]{0:T(256)(128)(2,1)} %param.33) | copy-start | bytes 148
  0.7 8.0 %copy-start.41 = (bf16[24]{0:T(256)(128)(2,1)S(1)}, bf16[24]{0:T(256)(128)(2,1)}, u32[]{:S(2)}) copy-start(bf16[24]{0:T(256)(128)(2,1)} %param.34) | copy-start | bytes 148
  0.7 8.0 %copy-start.42 = (bf16[96]{0:T(256)(128)(2,1)S(1)}, bf16[96]{0:T(256)(128)(2,1)}, u32[]{:S(2)}) copy-start(bf16[96]{0:T(256)(128)(2,1)} %param.36) | copy-start | bytes 580
  0.7 8.0 %copy-start.43 = (bf16[24]{0:T(256)(128)(2,1)S(1)}, bf16[24]{0:T(256)(128)(2,1)}, u32[]{:S(2)}) copy-start(bf16[24]{0:T(256)(128)(2,1)} %param.38) | copy-start | bytes 148
  0.8 8.0 %copy-start.44 = (bf16[24]{0:T(256)(128)(2,1)S(1)}, bf16[24]{0:T(256)(128)(2,1)}, u32[]{:S(2)}) copy-start(bf16[24]{0:T(256)(128)(2,1)} %param.39) | copy-start | bytes 148
  0.8 8.0 %copy-start.45 = (bf16[24]{0:T(256)(128)(2,1)S(1)}, bf16[24]{0:T(256)(128)(2,1)}, u32[]{:S(2)}) copy-start(bf16[24]{0:T(256)(128)(2,1)} %param.40) | copy-start | bytes 148
  0.8 9.4 %copy-start.46 = (s32[1,76]{1,0:T(1,128)S(1)}, s32[1,76]{1,0:T(1,128)}, u32[]{:S(2)}) copy-start(s32[1,76]{1,0:T(1,128)} %param.26) | copy-start | bytes 916
  0.8 9.4 %copy-start.37 = (s32[1,512]{1,0:T(1,128)S(1)}, s32[1,512]{1,0:T(1,128)}, u32[]{:S(2)}) copy-start(s32[1,512]{1,0:T(1,128)} %param.24) | copy-start | bytes 6148
  0.8 9.4 %copy-start.35 = (s32[1,512]{1,0:T(1,128)S(1)}, s32[1,512]{1,0:T(1,128)}, u32[]{:S(2)}) copy-start(s32[1,512]{1,0:T(1,128)} %param.25) | copy-start | bytes 6148
  0.8 9.4 %copy-start.36 = (s32[1,512]{1,0:T(1,128)S(1)}, s32[1,512]{1,0:T(1,128)}, u32[]{:S(2)}) copy-start(s32[1,512]{1,0:T(1,128)} %param.27) | copy-start | bytes 6148
  1.9 55.1 %collective-permute-start = (bf16[1,24,3840]{2,1,0:T(8,128)(2,1)S(1)}, bf16[1,24,3840]{2,1,0:T(8,128)(2,1)S(1)}, u32[]{:S(2)}, u32[]{:S(2)}) collective-permute-start(bf16[1,24,3840]{2,1,0:T(8,128)(2,1)S(1)} %maximum_bitcast_fusion), channel_id=1, source_target_pairs={{0,16},{1,17},{2,18},{3,19},{4,20},{5,21},{6,22},{7,23},{8,24},{9,... | collective-permute-start | bytes 552968 | tf_op jit(solution)/shard_map/ppermute | solution.py:1706
  4.2 52.8 %collective-permute-start.1 = (bf16[1,96,768]{2,1,0:T(8,128)(2,1)}, bf16[1,96,768]{2,1,0:T(8,128)(2,1)S(1)}, u32[]{:S(2)}, u32[]{:S(2)}) collective-permute-start(bf16[1,96,768]{2,1,0:T(8,128)(2,1)} %bitcast.170), channel_id=1, source_target_pairs={{0,16},{1,17},{2,18},{3,19},{4,20},{5,21},{6,22},{7,23},{8,24},{9,... | collective-permute-start | bytes 442376 | tf_op jit(solution)/shard_map/ppermute | solution.py:1706
  11.5 37.4 %copy-start.34 = (s32[4095]{0:T(1024)S(1)}, s32[4095]{0:T(1024)}, u32[]{:S(2)}) copy-start(s32[4095]{0:T(1024)} %param.28) | copy-start | bytes 49144
  45.1 11.9 %copy-start.32 = (bf16[96,768]{1,0:T(8,128)(2,1)S(1)}, bf16[96,768]{1,0:T(8,128)(2,1)}, u32[]{:S(2)}) copy-start(bf16[96,768]{1,0:T(8,128)(2,1)} %param.37) | copy-start | bytes 442372
  57.1 20.5 %collective-permute-start.3 = (bf16[2,96,768]{2,1,0:T(8,128)(2,1)S(1)}, bf16[2,96,768]{2,1,0:T(8,128)(2,1)S(1)}, u32[]{:S(2)}, u32[]{:S(2)}) collective-permute-start(bf16[2,96,768]{2,1,0:T(8,128)(2,1)S(1)} %maximum_select_fusion.7), channel_id=1, source_target_pairs={{0,8},{1,9},{2,10},{3,11},{4,12},{5,13},{6,14},{7,15},{8,0},{9,1},... | collective-permute-start | bytes 884744 | tf_op jit(solution)/shard_map/ppermute | solution.py:1706
  63.4 15.0 %collective-permute-start.2 = (bf16[2,24,3840]{2,1,0:T(8,128)(2,1)S(1)}, bf16[2,24,3840]{2,1,0:T(8,128)(2,1)S(1)}, u32[]{:S(2)}, u32[]{:S(2)}) collective-permute-start(bf16[2,24,3840]{2,1,0:T(8,128)(2,1)S(1)} %maximum_select_fusion.6), channel_id=1, source_target_pairs={{0,8},{1,9},{2,10},{3,11},{4,12},{5,13},{6,14},{7,15},{8,0},{9,1},... | collective-permute-start | bytes 1105928 | tf_op jit(solution)/shard_map/ppermute | solution.py:1706
  63.6 14.0 %copy-start.2 = (s32[384,128]{1,0:T(8,128)}, s32[384,128]{1,0:T(8,128)S(1)}, u32[]{:S(2)}) copy-start(s32[384,128]{1,0:T(8,128)S(1)} %broadcast_in_dim.107.shift_ref) | copy-start | bytes 589828
  77.6 3.4 copy-start.3
  78.5 17.3 %collective-permute-start.4 = (bf16[4,24,3840]{2,1,0:T(8,128)(2,1)S(1)}, bf16[4,24,3840]{2,1,0:T(8,128)(2,1)}, u32[]{:S(2)}, u32[]{:S(2)}) collective-permute-start(bf16[4,24,3840]{2,1,0:T(8,128)(2,1)S(1)} %maximum_select_fusion.4), channel_id=1, source_target_pairs={{0,4},{1,5},{2,6},{3,7},{4,0},{5,1},{6,2},{7,3},{8,12},{9,13},{10,... | collective-permute-start | bytes 2211848 | tf_op jit(solution)/shard_map/ppermute | solution.py:1706
  78.7 14.1 %collective-permute-start.5 = (bf16[4,96,768]{2,1,0:T(8,128)(2,1)S(1)}, bf16[4,96,768]{2,1,0:T(8,128)(2,1)S(1)}, u32[]{:S(2)}, u32[]{:S(2)}) collective-permute-start(bf16[4,96,768]{2,1,0:T(8,128)(2,1)S(1)} %maximum_select_fusion.5), channel_id=1, source_target_pairs={{0,2},{1,3},{2,0},{3,1},{4,6},{5,7},{6,4},{7,5},{8,10},{9,11},{10,... | collective-permute-start | bytes 1769480 | tf_op jit(solution)/shard_map/ppermute | solution.py:1706
  81.0 2.1 copy-start.5
  89.9 8.1 %copy-start.8 = (bf16[3,2432,64]{2,1,0:T(8,128)(2,1)}, bf16[3,2432,64]{2,1,0:T(8,128)(2,1)S(1)}, u32[]{:S(2)}) copy-start(bf16[3,2432,64]{2,1,0:T(8,128)(2,1)S(1)} %get-tuple-element.116.q_ref) | copy-start | bytes 2801668
  89.9 8.1 %copy-start.9 = (bf16[3,2048,64]{2,1,0:T(8,128)(2,1)}, bf16[3,2048,64]{2,1,0:T(8,128)(2,1)S(1)}, u32[]{:S(2)}) copy-start(bf16[3,2048,64]{2,1,0:T(8,128)(2,1)S(1)} %get-tuple-element.104.k_ref) | copy-start | bytes 2359300
  89.9 8.1 %copy-start.10 = (bf16[3,2048,64]{2,1,0:T(8,128)(2,1)}, bf16[3,2048,64]{2,1,0:T(8,128)(2,1)S(1)}, u32[]{:S(2)}) copy-start(bf16[3,2048,64]{2,1,0:T(8,128)(2,1)S(1)} %get-tuple-element.118.v_ref) | copy-start | bytes 2359300
  95.9 38.8 %collective-permute-start.7 = (bf16[8,96,768]{2,1,0:T(8,128)(2,1)S(1)}, bf16[8,96,768]{2,1,0:T(8,128)(2,1)S(1)}, u32[]{:S(2)}, u32[]{:S(2)}) collective-permute-start(bf16[8,96,768]{2,1,0:T(8,128)(2,1)S(1)} %maximum_select_fusion.3), channel_id=1, source_target_pairs={{0,4},{1,5},{2,6},{3,7},{4,0},{5,1},{6,2},{7,3},{8,12},{9,13},{10,... | collective-permute-start | bytes 3538952 | tf_op jit(solution)/shard_map/ppermute | solution.py:1706
  98.0 36.8 %collective-permute-start.6 = (bf16[8,24,3840]{2,1,0:T(8,128)(2,1)S(1)}, bf16[8,24,3840]{2,1,0:T(8,128)(2,1)S(1)}, u32[]{:S(2)}, u32[]{:S(2)}) collective-permute-start(bf16[8,24,3840]{2,1,0:T(8,128)(2,1)S(1)} %maximum_select_fusion.2), channel_id=1, source_target_pairs={{0,2},{1,3},{2,0},{3,1},{4,6},{5,7},{6,4},{7,5},{8,10},{9,11},{10,... | collective-permute-start | bytes 4423688 | tf_op jit(solution)/shard_map/ppermute | solution.py:1706
  134.8 1.0 copy-start.29
  135.8 1.1 copy-start.28
  136.9 4.3 copy-start.30
  139.1 3.8 copy-start.27
  139.1 30.1 %collective-permute-start.8 = (bf16[16,24,3840]{2,1,0:T(8,128)(2,1)S(1)}, bf16[16,24,3840]{2,1,0:T(8,128)(2,1)}, u32[]{:S(2)}, u32[]{:S(2)}) collective-permute-start(bf16[16,24,3840]{2,1,0:T(8,128)(2,1)S(1)} %maximum_select_fusion.uo_own), channel_id=1, source_target_pairs={{0,1},{1,0},{2,3},{3,2},{4,5},{5,4},{6,7},{7,6},{8,9},{9,8},{10,11... | collective-permute-start | bytes 8847368 | tf_op jit(solution)/shard_map/ppermute | solution.py:1706
  142.9 26.2 %collective-permute-start.9 = (bf16[16,96,768]{2,1,0:T(8,128)(2,1)}, bf16[16,96,768]{2,1,0:T(8,128)(2,1)}, u32[]{:S(2)}, u32[]{:S(2)}) collective-permute-start(bf16[16,96,768]{2,1,0:T(8,128)(2,1)} %maximum_select_fusion.1.down_own), channel_id=1, source_target_pairs={{0,1},{1,0},{2,3},{3,2},{4,5},{5,4},{6,7},{7,6},{8,9},{9,8},{10,11... | collective-permute-start | bytes 7077896 | tf_op jit(solution)/shard_map/ppermute | solution.py:1706
  226.7 24.6 %collective-permute-start.10 = (bf16[16,24,3840]{2,1,0:T(8,128)(2,1)}, bf16[16,24,3840]{2,1,0:T(8,128)(2,1)S(1)}, u32[]{:S(2)}, u32[]{:S(2)}) collective-permute-start(bf16[16,24,3840]{2,1,0:T(8,128)(2,1)} %get-tuple-element.124), channel_id=1, source_target_pairs={{0,1},{1,0},{2,3},{3,2},{4,5},{5,4},{6,7},{7,6},{8,9},{9,8},{10,11... | collective-permute-start | bytes 8847368 | tf_op jit(solution)/shard_map/ppermute | solution.py:1706
  226.8 24.5 %collective-permute-start.11 = (bf16[16,96,768]{2,1,0:T(8,128)(2,1)}, bf16[16,96,768]{2,1,0:T(8,128)(2,1)}, u32[]{:S(2)}, u32[]{:S(2)}) collective-permute-start(bf16[16,96,768]{2,1,0:T(8,128)(2,1)} %get-tuple-element.125), channel_id=1, source_target_pairs={{0,1},{1,0},{2,3},{3,2},{4,5},{5,4},{6,7},{7,6},{8,9},{9,8},{10,11... | collective-permute-start | bytes 7077896 | tf_op jit(solution)/shard_map/ppermute | solution.py:1706
  251.3 6.1 %copy-start.26 = (bf16[16,24,3840]{2,1,0:T(8,128)(2,1)S(1)}, bf16[16,24,3840]{2,1,0:T(8,128)(2,1)}, u32[]{:S(2)}) copy-start(bf16[16,24,3840]{2,1,0:T(8,128)(2,1)} %get-tuple-element.123) | copy-start | bytes 8847364
  254.4 3.0 copy-start.18
  255.7 72.5 %collective-permute-start.13 = (bf16[2,2,2,96,768]{4,3,0,1,2:T(8,128)(2,1)}, bf16[2,2,2,96,768]{4,3,0,1,2:T(8,128)(2,1)}, u32[]{:S(2)}, u32[]{:S(2)}) collective-permute-start(bf16[2,2,2,96,768]{4,3,0,1,2:T(8,128)(2,1)} %fusion.1), channel_id=1, source_target_pairs={{0,4},{1,5},{2,6},{3,7},{4,0},{5,1},{6,2},{7,3},{8,12},{9,13},{10,... | collective-permute-start | bytes 3538952 | tf_op jit(solution)/shard_map/ppermute | solution.py:1706
  258.1 2.6 copy-start.17
  260.8 67.4 %collective-permute-start.12 = (bf16[2,2,2,24,3840]{4,3,0,1,2:T(8,128)(2,1)S(1)}, bf16[2,2,2,24,3840]{4,3,0,1,2:T(8,128)(2,1)S(1)}, u32[]{:S(2)}, u32[]{:S(2)}) collective-permute-start(bf16[2,2,2,24,3840]{4,3,0,1,2:T(8,128)(2,1)S(1)} %fusion), channel_id=1, source_target_pairs={{0,2},{1,3},{2,0},{3,1},{4,6},{5,7},{6,4},{7,5},{8,10},{9,11},{10,... | collective-permute-start | bytes 4423688 | tf_op jit(solution)/shard_map/ppermute | solution.py:1706
  330.4 3.6 copy-start.19
  330.4 6.3 %copy-start.13 = (bf16[2048,192]{1,0:T(8,128)(2,1)S(1)}, bf16[2048,192]{1,0:T(8,128)(2,1)}, u32[]{:S(2)}) copy-start(bf16[2048,192]{1,0:T(8,128)(2,1)} %get-tuple-element.137.dv_ref) | copy-start | bytes 2359300
  330.5 6.2 %copy-start.4 = (bf16[8,4,24,576]{3,2,1,0:T(8,128)(2,1)S(1)}, bf16[8,4,24,576]{3,2,1,0:T(8,128)(2,1)}, u32[]{:S(2)}) copy-start(bf16[8,4,24,576]{3,2,1,0:T(8,128)(2,1)} %get-tuple-element.98) | copy-start | bytes 2654212
  330.5 6.2 %copy-start.6 = (bf16[2432,768]{1,0:T(8,128)(2,1)S(1)}, bf16[2432,768]{1,0:T(8,128)(2,1)}, u32[]{:S(2)}) copy-start(bf16[2432,768]{1,0:T(8,128)(2,1)} %get-tuple-element.97.x_ref) | copy-start | bytes 11206660
  330.5 6.2 %copy-start.11 = (bf16[2432,192]{1,0:T(8,128)(2,1)S(1)}, bf16[2432,192]{1,0:T(8,128)(2,1)}, u32[]{:S(2)}) copy-start(bf16[2432,192]{1,0:T(8,128)(2,1)} %get-tuple-element.135.dq_ref) | copy-start | bytes 2801668
  330.5 6.2 %copy-start.12 = (bf16[2048,192]{1,0:T(8,128)(2,1)S(1)}, bf16[2048,192]{1,0:T(8,128)(2,1)}, u32[]{:S(2)}) copy-start(bf16[2048,192]{1,0:T(8,128)(2,1)} %get-tuple-element.136.dk_ref) | copy-start | bytes 2359300
  334.0 2.7 copy-start.21
  334.0 17.8 %collective-permute-start.14 = (bf16[2,2,24,3840]{3,2,0,1:T(8,128)(2,1)S(1)}, bf16[2,2,24,3840]{3,2,0,1:T(8,128)(2,1)S(1)}, u32[]{:S(2)}, u32[]{:S(2)}) collective-permute-start(bf16[2,2,24,3840]{3,2,0,1:T(8,128)(2,1)S(1)} %fusion.2), channel_id=1, source_target_pairs={{0,4},{1,5},{2,6},{3,7},{4,0},{5,1},{6,2},{7,3},{8,12},{9,13},{10,... | collective-permute-start | bytes 2211848 | tf_op jit(solution)/shard_map/ppermute | solution.py:1706
  336.6 15.1 %collective-permute-start.15 = (bf16[2,2,96,768]{3,2,0,1:T(8,128)(2,1)}, bf16[2,2,96,768]{3,2,0,1:T(8,128)(2,1)}, u32[]{:S(2)}, u32[]{:S(2)}) collective-permute-start(bf16[2,2,96,768]{3,2,0,1:T(8,128)(2,1)} %fusion.3), channel_id=1, source_target_pairs={{0,2},{1,3},{2,0},{3,1},{4,6},{5,7},{6,4},{7,5},{8,10},{9,11},{10,... | collective-permute-start | bytes 1769480 | tf_op jit(solution)/shard_map/ppermute | solution.py:1706
  342.7 1.6 copy-start.7
  344.8 8.6 %copy-start.20 = (f32[2,2,2,24,3840]{4,3,0,1,2:T(8,128)S(1)}, f32[2,2,2,24,3840]{4,3,0,1,2:T(8,128)}, u32[]{:S(2)}) copy-start(f32[2,2,2,24,3840]{4,3,0,1,2:T(8,128)} %copy-done.19) | copy-start | bytes 8847364
  353.4 1.3 copy-start.24
  353.6 44.8 %copy-start.22 = (f32[2,2,24,3840]{3,2,0,1:T(8,128)}, f32[2,2,24,3840]{3,2,0,1:T(8,128)S(1)}, u32[]{:S(2)}) copy-start(f32[2,2,24,3840]{3,2,0,1:T(8,128)S(1)} %convert_add_fusion.4) | copy-start | bytes 4423684
  354.8 52.3 %collective-permute-start.17 = (bf16[2,96,768]{2,1,0:T(8,128)(2,1)S(1)}, bf16[2,96,768]{2,1,0:T(8,128)(2,1)}, u32[]{:S(2)}, u32[]{:S(2)}) collective-permute-start(bf16[2,96,768]{2,1,0:T(8,128)(2,1)S(1)} %fusion.7), channel_id=1, source_target_pairs={{0,8},{1,9},{2,10},{3,11},{4,12},{5,13},{6,14},{7,15},{8,0},{9,1},... | collective-permute-start | bytes 884744 | tf_op jit(solution)/shard_map/ppermute | solution.py:1706
  354.8 52.3 %collective-permute-start.16 = (bf16[2,24,3840]{2,1,0:T(8,128)(2,1)}, bf16[2,24,3840]{2,1,0:T(8,128)(2,1)}, u32[]{:S(2)}, u32[]{:S(2)}) collective-permute-start(bf16[2,24,3840]{2,1,0:T(8,128)(2,1)} %fusion.6), channel_id=1, source_target_pairs={{0,8},{1,9},{2,10},{3,11},{4,12},{5,13},{6,14},{7,15},{8,0},{9,1},... | collective-permute-start | bytes 1105928 | tf_op jit(solution)/shard_map/ppermute | solution.py:1706
  356.2 42.2 %copy-start.31 = (f32[80,768]{1,0:T(8,128)S(1)}, f32[80,768]{1,0:T(8,128)}, u32[]{:S(2)}) copy-start(f32[80,768]{1,0:T(8,128)} %get-tuple-element.150) | copy-start | bytes 737284
  404.2 2.9 copy-start.25
  404.2 10.5 %copy-start.23 = (f32[2,2,24,3840]{3,2,0,1:T(8,128)S(1)}, f32[2,2,24,3840]{3,2,0,1:T(8,128)}, u32[]{:S(2)}) copy-start(f32[2,2,24,3840]{3,2,0,1:T(8,128)} %copy-done.22) | copy-start | bytes 4423684
  408.1 24.2 %copy-start.1 = (bf16[32,12]{0,1:T(8,128)(2,1)S(1)}, bf16[32,12]{0,1:T(8,128)(2,1)}, u32[]{:S(2)}) copy-start(bf16[32,12]{0,1:T(8,128)(2,1)} %param.41) | copy-start | bytes 2308
  408.2 18.0 %collective-permute-start.19 = (bf16[96,768]{1,0:T(8,128)(2,1)S(1)}, bf16[96,768]{1,0:T(8,128)(2,1)S(1)}, u32[]{:S(2)}, u32[]{:S(2)}) collective-permute-start(bf16[96,768]{1,0:T(8,128)(2,1)S(1)} %fusion.12), channel_id=1, source_target_pairs={{0,16},{1,17},{2,18},{3,19},{4,20},{5,21},{6,22},{7,23},{8,24},{9,... | collective-permute-start | bytes 442376 | tf_op jit(solution)/shard_map/ppermute | solution.py:1706
  415.8 14.3 %collective-permute-start.18 = (bf16[24,3840]{1,0:T(8,128)(2,1)S(1)}, bf16[24,3840]{1,0:T(8,128)(2,1)S(1)}, u32[]{:S(2)}, u32[]{:S(2)}) collective-permute-start(bf16[24,3840]{1,0:T(8,128)(2,1)S(1)} %fusion.11), channel_id=1, source_target_pairs={{0,16},{1,17},{2,18},{3,19},{4,20},{5,21},{6,22},{7,23},{8,24},{9,... | collective-permute-start | bytes 552968 | tf_op jit(solution)/shard_map/ppermute | solution.py:1706
  (3 other events, 2.7 us)
